TPU v7x, 512 devices: a whole 4x8x8 slice. The times are simulated.
512 devices in a mesh: uly: 8 (over x, z_lo), blk: 64 (over y, z_hi, core).
Axes of the slice: x: 4, y: 8, z: 8 (z_hi: 4, z_lo: 2; z = z_hi * 2 + z_lo), core: 2. Of those that a mesh axis runs over, the one named last changes fastest.
Arguments:
- prompt: bfloat16 [64, 128, 3072], P('blk')
- image_rows: bfloat16 [8, 64, 8, 3072], P('uly', 'blk'), may hold values from -6 to 6
- image_slots: int32 [8, 64, 8], P('uly', 'blk'), may hold values from -1 to 127, as said below
- norm_gain: float32 [3072], replicated, may hold values from 0.1 to 1.9
- w_query: bfloat16 [3072, 3072], P(None, 'uly')
- key_matrix: bfloat16 [3072, 1024], P(None, 'uly'), may hold values from -0.109375 to 0.109375
- value_matrix: bfloat16 [3072, 1024], P(None, 'uly'), may hold values from -0.109375 to 0.109375
- w_out: bfloat16 [3072, 3072], P('uly', 'blk'), may hold values from -0.109375 to 0.109375
Outputs:
- hidden_out: bfloat16 [64, 128, 3072], P('blk', 'uly')
Inputs may be any that keep to these rules, and one draw needn't show every extreme that they name: `image_slots`: entry (u, b, s) is -1 for an empty slot or a position inside block b. The live entries of one block are distinct and form one run of consecutive positions, of 8 up to three times 8 image rows, held by one to three devices of that block; in every block one device holds exactly 8 live rows.
All inputs are finite; a program needn't handle non-finite values.
Results may differ from a plain program's by a relative error of at most 0.0075.
The roundings to bfloat16 on the way count: a program that leaves them out, or rounds other values in their place, can miss the bound.
Values may be sent and summed in bfloat16 or wider, within the bound.
No kernel may reach another device: no remote copies, remote signals or barrier semaphores. Data moves between devices by JAX's collectives and lax.ppermute only.
A program may use at most 64 MiB of HBM per device.

v0:
```python
from functools import partial
import math

import jax
import jax.numpy as jnp
from jax import lax
from jax.sharding import Mesh
from jax.sharding import PartitionSpec as P

HEAD_SIZE = 128
BLK = ("blk_0", "blk_1", "blk_2")


def joined_along(tiles, dim):
    tiles = jnp.moveaxis(tiles, 0, dim)
    shape = tiles.shape
    return tiles.reshape(*shape[:dim], shape[dim] * shape[dim + 1], *shape[dim + 2 :])


def from_everyone(array, axis):
    devices = lax.axis_size(axis)
    return lax.all_to_all(
        jnp.broadcast_to(array[None], (devices, *array.shape)), axis, 0, 0, tiled=True
    )


def gathered_copies(array, axis, dim):
    return joined_along(from_everyone(array, axis), dim)


def gathered_by_axis(array, axes, dim):
    far, near = axes
    leading = from_everyone(array, far)
    tiles = jnp.swapaxes(from_everyone(leading, near), 0, 1)
    return joined_along(tiles.reshape(-1, *array.shape), dim)


def in_blocks(array, dim, devices):
    before, after = (array.shape[:dim], array.shape[dim + 1 :])
    return jnp.moveaxis(array.reshape(*before, devices, -1, *after), dim, 0)


def summed_on_arrival(array, axis, dim):
    tiles = in_blocks(array, dim, lax.axis_size(axis))
    arrived = lax.all_to_all(tiles, axis, split_axis=0, concat_axis=0, tiled=True)
    return arrived.astype(jnp.float32).sum(axis=0)


def rope_tables(positions, head_width):
    fraction = jnp.arange(0, head_width, 2).astype(jnp.float32) / head_width
    inverse = jnp.exp(-math.log(500000.0) * fraction)
    angles = positions.astype(jnp.float32)[:, None] * inverse[None, :]
    angles = jnp.concatenate([angles, angles], axis=1)
    return (jnp.cos(angles), jnp.sin(angles))


def rotate_halves(values, cosine_table, sine_table):
    half_width = values.shape[-1] // 2
    turned = jnp.concatenate([-values[..., half_width:], values[..., :half_width]], axis=-1)
    return values * cosine_table + turned * sine_table


def body(prompt, image_rows, image_slots, norm_gain, w_query, key_matrix, value_matrix, w_out):
    block_images, block_slots = (
        gathered_copies(image_rows, "uly", 0),
        gathered_copies(image_slots, "uly", 0),
    )
    model_width = prompt.shape[2]
    block_len = prompt.shape[1]
    tok_dev = block_len // lax.axis_size("uly")
    head_dim = HEAD_SIZE
    local_heads = w_query.shape[1] // head_dim
    local_kv = key_matrix.shape[1] // head_dim
    group_count = local_heads // local_kv
    blk_index = lax.axis_index(BLK)
    uly_index = lax.axis_index("uly")
    picture_rows = block_images.reshape(-1, model_width)
    placeholder_labels = block_slots.reshape(-1)
    equality_flags = placeholder_labels[None, :] == jnp.arange(block_len, dtype=jnp.int32)[:, None]
    chosen_entries = jnp.dot(
        equality_flags.astype(jnp.bfloat16), picture_rows, preferred_element_type=jnp.float32
    )
    placed = jnp.where(
        jnp.any(equality_flags, axis=1)[:, None], chosen_entries, prompt[0].astype(jnp.float32)
    )
    mean_square = jnp.mean(placed * placed, axis=1, keepdims=True)
    normed_input = (placed * lax.rsqrt(mean_square + 1e-05) * norm_gain[None, :]).astype(
        jnp.bfloat16
    )
    positions = blk_index * block_len + jnp.arange(block_len, dtype=jnp.int32)
    cosine_table, sine_table = rope_tables(positions, head_dim)
    cosine_table = cosine_table[:, None, :]
    sine_table = sine_table[:, None, :]
    queries = jnp.dot(normed_input, w_query, preferred_element_type=jnp.float32).reshape(
        block_len, local_heads, head_dim
    )
    queries = (
        rotate_halves(queries, cosine_table, sine_table)
        .astype(jnp.bfloat16)
        .reshape(block_len, local_kv, group_count, head_dim)
    )
    keys = jnp.dot(normed_input, key_matrix, preferred_element_type=jnp.float32).reshape(
        block_len, local_kv, head_dim
    )
    keys = (
        rotate_halves(keys, cosine_table, sine_table)
        .astype(jnp.bfloat16)
        .reshape(block_len, local_kv * head_dim)
    )
    values = jnp.dot(normed_input, value_matrix, preferred_element_type=jnp.float32).astype(
        jnp.bfloat16
    )
    key_value = jnp.concatenate([keys, values], axis=1)[None]
    asker_collections = [(queries, blk_index * block_len)]
    scale = 1.0 / math.sqrt(head_dim)
    kv_width = local_kv * head_dim

    def empty_state(length):
        return (
            jnp.full((local_kv, group_count, length), -1e30, jnp.float32),
            jnp.zeros((local_kv, group_count, length), jnp.float32),
            jnp.zeros((local_kv, group_count, length, head_dim), jnp.float32),
        )

    initial = tuple([empty_state(entry[0].shape[0]) for entry in asker_collections])

    def own_positions(collection_ordinal, length):
        return asker_collections[collection_ordinal][1] + jnp.arange(length, dtype=jnp.int32)

    def attend_positions(state, key_block, key_first, query_block, query_pos):
        best, denominator, accumulated = state
        key_part = key_block[:, :kv_width].reshape(-1, local_kv, head_dim)
        value_part = key_block[:, kv_width:].reshape(-1, local_kv, head_dim)
        scores = (
            jnp.einsum("qkrd,skd->krqs", query_block, key_part, preferred_element_type=jnp.float32)
            * scale
        )
        key_pos = key_first + jnp.arange(key_block.shape[0], dtype=jnp.int32)
        allowed = key_pos[None, :] <= query_pos[:, None]
        scores = jnp.where(allowed[None, None], scores, -jnp.inf)
        updated = jnp.maximum(best, jnp.max(scores, axis=3))
        weights = jnp.exp(scores - updated[..., None])
        factor = jnp.exp(best - updated)
        denominator = denominator * factor + jnp.sum(weights, axis=3)
        accumulated = accumulated * factor[..., None] + jnp.einsum(
            "krqs,skd->krqd",
            weights.astype(jnp.bfloat16),
            value_part,
            preferred_element_type=jnp.float32,
        )
        return (updated, denominator, accumulated)

    piece_blocks = gathered_by_axis(key_value, (("blk_0", "blk_1"), "blk_2"), 0)
    block_total = piece_blocks.shape[0]
    each_iteration_share = math.gcd(block_total, max(1, 1024 // block_len))
    steps_count = block_total // each_iteration_share
    stacked = piece_blocks.reshape(
        steps_count, each_iteration_share * block_len, piece_blocks.shape[2]
    )

    def step_fn(carry, inputs):
        key_block, step_index = inputs
        key_first = step_index * each_iteration_share * block_len
        query_block, query_first = asker_collections[0]
        query_pos = own_positions(0, query_block.shape[0])
        last_pos = jnp.max(query_pos)
        update = partial(
            attend_positions,
            key_block=key_block,
            key_first=key_first,
            query_block=query_block,
            query_pos=query_pos,
        )
        results = [lax.cond(key_first <= last_pos, update, lambda kept: kept, carry[0])]
        return (tuple(results), None)

    folded, leftover = lax.scan(
        step_fn, initial, (stacked, jnp.arange(steps_count, dtype=jnp.int32))
    )
    best, denominator, accumulated = folded[0]
    mixed = accumulated / denominator[..., None]
    attended = (
        jnp.transpose(mixed, (2, 0, 1, 3))
        .reshape(mixed.shape[2], local_heads * head_dim)
        .astype(jnp.bfloat16)
    )
    projected = jnp.dot(
        attended, lax.all_gather(w_out, BLK, axis=1, tiled=True), preferred_element_type=jnp.float32
    )
    summed = summed_on_arrival(projected.astype(jnp.bfloat16), "uly", 0)
    own_rows = lax.dynamic_slice_in_dim(placed, uly_index * tok_dev, tok_dev, 0)
    return (own_rows + summed).astype(jnp.bfloat16)[None]


def solution(mesh):
    split = Mesh(
        mesh.devices.reshape(mesh.shape["uly"], 8, 4, 2), ("uly", "blk_0", "blk_1", "blk_2")
    )
    placed = (
        P(BLK, None, None),
        P("uly", BLK, None, None),
        P("uly", BLK, None),
        P(),
        P(None, "uly"),
        P(None, "uly"),
        P(None, "uly"),
        P("uly", BLK),
    )
    return jax.shard_map(
        body, mesh=split, in_specs=placed, out_specs=P(BLK, "uly", None), check_vma=False
    )
```

profile of v0, /device:TPU:1, one launch (start us, length us, event | category | flops | bytes accessed | tf_op | source)
XLA Modules:
  0.0 194.2 jit_solution(17779617066381102296)
XLA Ops:
  6.5 0.8 broadcast_in_dim.50
  7.4 11.6 %all_to_all.25 = s32[8,1,1,8]{3,2,1,0:T(1,128)S(1)} all-to-all(s32[8,1,1,8]{3,2,1,0:T(1,128)S(1)} %broadcast_in_dim.50), channel_id=1, replica_groups=mesh['uly'=8,'blk_0'=8,'blk_1'=4,'blk_2'=2] {'uly'}, dimensions={0} | all-to-all | bytes 512 | tf_op jit(solution)/shard_map/all_to_all | solution.py:22
  18.9 1.6 broadcast_in_dim.81
  20.5 3.5 %all-to-all-start.1 = ((bf16[8,1,1,8,3072]{4,3,2,1,0:T(8,128)(2,1)}), bf16[8,1,1,8,3072]{4,3,2,1,0:T(8,128)(2,1)S(1)}, u32[]{:S(2)}, u32[]{:S(2)}) async-start(bf16[8,1,1,8,3072]{4,3,2,1,0:T(8,128)(2,1)} %broadcast_in_dim.81), calls=%async_computation.1 | async-start | bytes 786432 | tf_op jit(solution)/shard_map/all_to_all | solution.py:22
  24.0 0.7 broadcast_multiply_fusion
  26.6 4.1 %all-to-all-done.1 = bf16[8,1,1,8,3072]{4,3,2,1,0:T(8,128)(2,1)S(1)} async-done(((bf16[8,1,1,8,3072]{4,3,2,1,0:T(8,128)(2,1)}), bf16[8,1,1,8,3072]{4,3,2,1,0:T(8,128)(2,1)S(1)}, u32[]{:S(2)}, u32[]{:S(2)}) %all-to-all-start.1) | async-done | bytes 393248 | tf_op jit(solution)/shard_map/all_to_all | solution.py:22
  30.7 1.2 multiply_reduce_fusion
  32.2 1.4 copy-done.2
  35.0 1.6 broadcast_in_dim.85
  36.5 14.9 %all-to-all-start.2 = ((bf16[32,1,128,256]{3,2,1,0:T(8,128)(2,1)}), bf16[32,1,128,256]{3,2,1,0:T(8,128)(2,1)}, u32[]{:S(2)}, u32[]{:S(2)}) async-start(bf16[32,1,128,256]{3,2,1,0:T(8,128)(2,1)} %broadcast_in_dim.85), calls=%async_computation.2 | async-start | bytes 4194304 | tf_op jit(solution)/shard_map/all_to_all | solution.py:22
  51.5 0.7 all-gather.2.cloned.1.call-update
  52.2 1.0 fusion.23
  53.5 45.2 %all-to-all-done.2 = bf16[32,1,128,256]{3,2,1,0:T(8,128)(2,1)} async-done(((bf16[32,1,128,256]{3,2,1,0:T(8,128)(2,1)}), bf16[32,1,128,256]{3,2,1,0:T(8,128)(2,1)}, u32[]{:S(2)}, u32[]{:S(2)}) %all-to-all-start.2) | async-done | bytes 2097184 | tf_op jit(solution)/shard_map/all_to_all | solution.py:22
  98.7 2.1 %broadcast_in_dim.87 = bf16[2,32,1,128,256]{4,3,1,2,0:T(8,128)(2,1)S(1)} broadcast(bf16[32,128,256]{2,1,0:T(8,128)(2,1)} %bitcast.20), dimensions={1,3,4} | broadcast | bytes 6291456 | tf_op jit(solution)/shard_map/broadcast_in_dim | solution.py:23
  100.8 13.0 %all_to_all.26 = bf16[2,32,1,128,256]{4,3,1,2,0:T(8,128)(2,1)S(1)} all-to-all(bf16[2,32,1,128,256]{4,3,1,2,0:T(8,128)(2,1)S(1)} %broadcast_in_dim.87), channel_id=1, replica_groups=mesh['uly'=8,'blk_0'=8,'blk_1'=4,'blk_2'=2] {'blk_2'}, dimensions={0} | all-to-all | bytes 8388608 | tf_op jit(solution)/shard_map/all_to_all | solution.py:22
  113.8 2.2 %copy.37 = bf16[2,32,1,128,256]{4,3,0,1,2:T(8,128)(2,1)} copy(bf16[2,32,1,128,256]{4,3,1,2,0:T(8,128)(2,1)S(1)} %all_to_all.26) | data formatting | bytes 8388608 | tf_op jit(solution)/shard_map/all_to_all | solution.py:22
  116.0 23.2 %while.16 = (s32[]{:T(128)}, f32[1,3,128]{2,1,0:T(4,128)S(1)}, f32[1,3,128]{2,1,0:T(4,128)S(1)}, f32[1,3,128,128]{3,2,1,0:T(8,128)S(1)}, s32[8]{0:T(128)S(1)}, /...) while((s32[]{:T(128)}, f32[1,3,128]{2,1,0:T(4,128)S(1)}, ...), condition=%wide.region_8.9_spmd, body=%wide.region_2.8_spmd.sunk | while | flops 204310912 | bytes 7080211 | solution.py:177
  118.6 2.5 %conditional.2 = ((f32[1,3,128]{2,1,0:T(4,128)S(1)}, f32[1,3,128]{2,1,0:T(4,128)S(1)}, f32[1,3,128,128]{3,2,1,0:T(8,128)S(1)})) conditional(s32[]{:T(128)} %convert_element_type.101, (f32[1,3,128]{2,1,0:T(4,128)S(1)}, f32[1,3,128]{2,1,0:T(4,128)S(1)}, f32[1,3,128,128]{3,2,1,0:T(8,128)S(1)}) %tuple.54, (s32[]{:T(128)}, s32[128]{0:T(128)S(1)}, ...), branch_computations={%region_4.4_spmd, %region_5.7_spmd} | conditional | flops 204310656 | bytes 7079464 | solution.py:174
  118.6 1.1 dynamic-slice_bitcast_fusion
  139.4 26.0 %all-gather.2.cloned.1.call-done = bf16[384,3072]{0,1:T(8,128)(2,1)} async-done(((bf16[384,48]{0,1:T(8,128)(2,1)}), bf16[384,3072]{0,1:T(8,128)(2,1)}) %all-gather.2.cloned.1.call-update) | async-done | bytes 2359312 | tf_op jit(solution)/shard_map/all_gather | solution.py:188
  165.4 3.4 %convolution_convert_fusion = bf16[128,3072]{1,0:T(8,128)(2,1)} fusion(bf16[128,384]{0,1:T(8,128)(2,1)S(1)} %bitcast.84, bf16[384,3072]{0,1:T(8,128)(2,1)} %all-gather.2.cloned.1.call-done), kind=kOutput, calls=%fused_computation.21 | convolution fusion | flops 302383104 | bytes 3244032 | tf_op jit(solution)/shard_map/dot_general | solution.py:187
  168.9 4.2 %all-to-all-start.4 = ((bf16[8,16,3072]{2,1,0:T(8,128)(2,1)}), bf16[8,16,3072]{2,1,0:T(8,128)(2,1)S(1)}, u32[]{:S(2)}, u32[]{:S(2)}) async-start(bf16[8,16,3072]{2,1,0:T(8,128)(2,1)} %bitcast.78), calls=%async_computation.4 | async-start | bytes 1572864 | tf_op jit(solution)/shard_map/all_to_all | solution.py:45
  173.1 12.5 %all-to-all-done.4 = bf16[8,16,3072]{2,1,0:T(8,128)(2,1)S(1)} async-done(((bf16[8,16,3072]{2,1,0:T(8,128)(2,1)}), bf16[8,16,3072]{2,1,0:T(8,128)(2,1)S(1)}, u32[]{:S(2)}, u32[]{:S(2)}) %all-to-all-start.4) | async-done | bytes 786464 | tf_op jit(solution)/shard_map/all_to_all | solution.py:45
  185.8 1.6 fusion.12
  (69 shorter events, 15.7 us)
Async XLA Ops:
  6.5 45.7 %copy-start = (bf16[3072,384]{1,0:T(8,128)(2,1)S(1)}, bf16[3072,384]{1,0:T(8,128)(2,1)}, u32[]{:S(2)}) copy-start(bf16[3072,384]{1,0:T(8,128)(2,1)} %param.16) | copy-start | bytes 7077892
  6.5 24.2 %copy-start.4 = (bf16[1,128,3072]{2,1,0:T(8,128)(2,1)S(1)}, bf16[1,128,3072]{2,1,0:T(8,128)(2,1)}, u32[]{:S(2)}) copy-start(bf16[1,128,3072]{2,1,0:T(8,128)(2,1)} %param.12) | copy-start | bytes 2359300
  20.5 10.2 %all-to-all-start.1 = ((bf16[8,1,1,8,3072]{4,3,2,1,0:T(8,128)(2,1)}), bf16[8,1,1,8,3072]{4,3,2,1,0:T(8,128)(2,1)S(1)}, u32[]{:S(2)}, u32[]{:S(2)}) async-start(bf16[8,1,1,8,3072]{4,3,2,1,0:T(8,128)(2,1)} %broadcast_in_dim.81), calls=%async_computation.1 | async-start | bytes 786432 | tf_op jit(solution)/shard_map/all_to_all | solution.py:22
  26.0 6.0 %copy-start.6 = (f32[3072]{0:T(1024)S(1)}, f32[3072]{0:T(1024)}, u32[]{:S(2)}) copy-start(f32[3072]{0:T(1024)} %param.15) | copy-start | bytes 36868
  31.9 2.2 %copy-start.1 = (f32[128,3072]{1,0:T(8,128)}, f32[128,3072]{1,0:T(8,128)S(1)}, u32[]{:S(2)}) copy-start(f32[128,3072]{1,0:T(8,128)S(1)} %get-tuple-element.229) | copy-start | bytes 4718596
  32.0 1.7 copy-start.2
  32.0 2.1 %copy-start.3 = (bf16[3072,128]{1,0:T(8,128)(2,1)S(1)}, bf16[3072,128]{1,0:T(8,128)(2,1)}, u32[]{:S(2)}) copy-start(bf16[3072,128]{1,0:T(8,128)(2,1)} %param.18) | copy-start | bytes 2359300
  33.7 0.9 copy-start.5
  36.5 62.1 %all-to-all-start.2 = ((bf16[32,1,128,256]{3,2,1,0:T(8,128)(2,1)}), bf16[32,1,128,256]{3,2,1,0:T(8,128)(2,1)}, u32[]{:S(2)}, u32[]{:S(2)}) async-start(bf16[32,1,128,256]{3,2,1,0:T(8,128)(2,1)} %broadcast_in_dim.85), calls=%async_computation.2 | async-start | bytes 4194304 | tf_op jit(solution)/shard_map/all_to_all | solution.py:22
  51.5 114.0 %all-gather.2.cloned.1.call-start = ((), (), s32[]{:S(2)}) async-start(), calls=%async_computation.5 | async-start | bytes 2396160 | tf_op jit(solution)/shard_map/all_gather | solution.py:188
  168.9 16.8 %all-to-all-start.4 = ((bf16[8,16,3072]{2,1,0:T(8,128)(2,1)}), bf16[8,16,3072]{2,1,0:T(8,128)(2,1)S(1)}, u32[]{:S(2)}, u32[]{:S(2)}) async-start(bf16[8,16,3072]{2,1,0:T(8,128)(2,1)} %bitcast.78), calls=%async_computation.4 | async-start | bytes 1572864 | tf_op jit(solution)/shard_map/all_to_all | solution.py:45
Sparse Core Ops, SparseCore 0:
  55.6 109.7 all-gather.1
where the time goes:
time: 195 us; the launch traced here: 194 us
  waiting for transfers between devices  88.6 us (45%)
  blocking collectives  24.6 us (13%)
  starting transfers between devices  22.7 us (12%)
  local copies, waits for them, and re-layouts  17.1 us (9%)
  between operations  13.6 us (7%)
  loops' own time  10.5 us (5%)
  other arithmetic  9.73 us (5%)
  matrix products  7.38 us (4%)
    all_to_all x2, waiting for transfers between devices, from_everyone(): lax.all_to_all(jnp.broadcast_to(array[None], (devices, *array.shape)), ax...  49.4 us
    all_gather x1, waiting for transfers between devices, body(): lax.all_gather(w_out, BLK, axis=1, tiled=True)  26 us
    all_to_all x2, blocking collectives, from_everyone(): lax.all_to_all(jnp.broadcast_to(array[None], (devices, *array.shape)), ax...  24.6 us
    all_to_all x2, starting transfers between devices, from_everyone(): lax.all_to_all(jnp.broadcast_to(array[None], (devices, *array.shape)), ax...  18.4 us
    all_to_all x1, waiting for transfers between devices, summed_on_arrival(): lax.all_to_all(tiles, axis, split_axis=0, concat_axis=0, tiled=True)  12.5 us
    another operation x1, loops' own time, body(): lax.scan(step_fn, initial, (stacked, jnp.arange(steps_count, dtype=jnp.in...  10.4 us
    broadcast_in_dim x4, local copies, waits for them, and re-layouts, from_everyone(): jnp.broadcast_to(array[None], (devices, *array.shape))  6.03 us
    dynamic_slice x8, local copies, waits for them, and re-layouts, body(): lax.scan(step_fn, initial, (stacked, jnp.arange(steps_count, dtype=jnp.in...  5.31 us
  transfers between devices with their start and end apart: 4, of which 4 were waited for; matrix products, arithmetic and copies ran while one was open for 11% of the time, Pallas kernels for 0%

commit v1 on v0

v1 whole, which is shorter than its diff:
```python
import functools
import math

import jax
import jax.numpy as jnp
from jax import lax
from jax.experimental import pallas as pl
from jax.experimental.pallas import tpu as pltpu
from jax.sharding import Mesh
from jax.sharding import PartitionSpec as P

HEAD = 128
BLK = ("blk_y", "blk_z", "blk_c")
NEG = -2.0e38
STAT_ROWS = 16
F32 = jnp.float32
BF16 = jnp.bfloat16


def nt_dot(a, b):
    return lax.dot_general(a, b, (((1,), (1,)), ((), ())), preferred_element_type=F32)


def tn_dot(a, b):
    return lax.dot_general(a, b, (((0,), (0,)), ((), ())), preferred_element_type=F32)


def rope_tables(positions):
    fraction = jnp.arange(0, HEAD, 2).astype(F32) / HEAD
    inverse = jnp.exp(-math.log(500000.0) * fraction)
    angles = positions.astype(F32)[:, None] * inverse[None, :]
    cosine, sine = jnp.cos(angles), jnp.sin(angles)
    return jnp.concatenate([cosine, cosine], axis=1), jnp.concatenate([-sine, sine], axis=1)


def qkv_kernel(where_ref, img_ref, prompt_ref, gain_ref, wq_ref, wk_ref, wv_ref, cos_ref, sin_ref,
               q_ref, kv_ref, own_ref, placed_ref):
    width = prompt_ref.shape[1]
    length = prompt_ref.shape[0]
    own_len = own_ref.shape[0]
    rows = img_ref.shape[0]
    slots = img_ref[:, width : width + 1].astype(F32)
    lanes = lax.broadcasted_iota(jnp.int32, (rows, length), 1).astype(F32)
    flags = jnp.where(slots == lanes, 1.0, 0.0).astype(BF16)
    present = tn_dot(flags, img_ref[:, width:])[:, 1:2] > 0.5
    chosen = tn_dot(flags, img_ref[:, :width])
    placed = jnp.where(present, chosen, prompt_ref[...].astype(F32))
    placed_ref[...] = placed
    mean_square = jnp.mean(placed * placed, axis=1, keepdims=True)
    normed = (placed * lax.rsqrt(mean_square + 1e-05) * gain_ref[...]).astype(BF16)
    first = pl.multiple_of(where_ref[0] * own_len, own_len)
    own_ref[...] = placed_ref[pl.ds(first, own_len), :]
    cosine, sine = cos_ref[...], sin_ref[...]

    def rope(v):
        return (v * cosine + pltpu.roll(v, HEAD // 2, 1) * sine).astype(BF16)

    keys = rope(jnp.dot(normed, wk_ref[...], preferred_element_type=F32))
    values = jnp.dot(normed, wv_ref[...], preferred_element_type=F32).astype(BF16)
    for i in range(kv_ref.shape[0]):
        kv_ref[i, :, :HEAD] = keys
        kv_ref[i, :, HEAD:] = values
    queries = jnp.dot(normed, wq_ref[...], preferred_element_type=F32)
    for h in range(wq_ref.shape[1] // HEAD):
        turned = rope(queries[:, h * HEAD : (h + 1) * HEAD])
        for i in range(q_ref.shape[0]):
            q_ref[i, h * HEAD : (h + 1) * HEAD, :] = turned


def attend_kernel(where_ref, q_ref, near_ref, far_ref, o_ref, s_ref):
    y, z, c = where_ref[1], where_ref[2], where_ref[3]
    zq = pl.program_id(0)
    rows = q_ref.shape[1]
    length = near_ref.shape[1]
    heads = rows // length
    queries = q_ref[0]
    scale = 1.0 / math.sqrt(HEAD)

    def raw(i):
        keys = jnp.concatenate([near_ref[i, :, :HEAD], far_ref[i, :, :HEAD]], axis=0)
        return nt_dot(queries, keys) * scale

    def folded(s, op):
        return op(s[:, :HEAD], s[:, HEAD:])

    def first_pass(i, best):
        s = raw(i)
        s_ref[i] = s
        return jnp.maximum(best, folded(s, jnp.maximum))

    best = lax.fori_loop(0, y, first_pass, jnp.full((rows, HEAD), NEG, F32))
    s = raw(y)
    q_pos = (2 * zq + c) * length + lax.rem(
        lax.broadcasted_iota(jnp.int32, s.shape, 0), length
    )
    lane = lax.broadcasted_iota(jnp.int32, s.shape, 1)
    k_core = jnp.where(lane < length, c, 1 - c)
    k_pos = (2 * z + k_core) * length + jnp.where(lane < length, lane, lane - length)
    s = jnp.where(k_pos <= q_pos, s, NEG)
    s_ref[y] = s
    best = jnp.maximum(best, folded(s, jnp.maximum))
    top = jnp.max(best, axis=1, keepdims=True).astype(BF16).astype(F32)

    def second_pass(i, carry):
        total, mixed = carry
        weights = jnp.exp(s_ref[i] - top)
        total = total + folded(weights, jnp.add)
        values = jnp.concatenate([near_ref[i, :, HEAD:], far_ref[i, :, HEAD:]], axis=0)
        mixed = mixed + jnp.dot(weights.astype(BF16), values, preferred_element_type=F32)
        return total, mixed

    zeros = jnp.zeros((rows, HEAD), F32)
    total, mixed = lax.fori_loop(0, y + 1, second_pass, (zeros, zeros))
    total = jnp.sum(total, axis=1, keepdims=True)
    o_ref[0, :rows, :] = mixed.astype(BF16)
    column = lax.broadcasted_iota(jnp.int32, (length, HEAD), 1)
    tile = jnp.zeros((length, HEAD), F32)
    for h in range(heads):
        part = slice(h * length, (h + 1) * length)
        tile = jnp.where(column == h, top[part], tile)
        tile = jnp.where(column == heads + h, total[part], tile)
    stats = tile.T[: 2 * heads]
    tops, totals = stats[:heads], stats[heads:]
    high = totals.astype(BF16)
    rest = totals - high.astype(F32)
    middle = rest.astype(BF16)
    low = (rest - middle.astype(F32)).astype(BF16)
    packed = jnp.concatenate(
        [tops, high.astype(F32), middle.astype(F32), low.astype(F32),
         jnp.zeros((STAT_ROWS - 4 * heads, length), F32)], axis=0
    )
    o_ref[0, rows:, :] = packed.astype(BF16)


def project_kernel(o_ref, w_ref, out_ref, attended_ref):
    parts = o_ref.shape[0]
    rows = o_ref.shape[1] - STAT_ROWS
    length = o_ref.shape[2]
    heads = rows // length

    @pl.when(pl.program_id(0) == 0)
    def _():
        tops, totals = [], []
        for i in range(parts):
            stats = o_ref[i, rows:, :].astype(F32)
            tops.append(stats[:heads])
            totals.append(stats[heads : 2 * heads] + stats[2 * heads : 3 * heads] + stats[3 * heads : 4 * heads])
        best = functools.reduce(jnp.maximum, tops)
        grown = [jnp.exp(t - best) for t in tops]
        whole = sum(g * t for g, t in zip(grown, totals))
        share = [g / whole for g in grown]
        tile = jnp.concatenate(share + [jnp.zeros((HEAD - parts * heads, length), F32)], axis=0).T
        for h in range(heads):
            part = slice(h * length, (h + 1) * length)
            mixed = sum(
                o_ref[i, part, :].astype(F32) * tile[:, i * heads + h : i * heads + h + 1]
                for i in range(parts)
            )
            attended_ref[:, h * HEAD : (h + 1) * HEAD] = mixed.astype(BF16)

    out_ref[...] = nt_dot(attended_ref[...], w_ref[...]).astype(BF16)


def whole_block(shape):
    return pl.BlockSpec(shape, lambda *_: (0,) * len(shape))


def body(prompt, image_rows, image_slots, norm_gain, w_query, key_matrix, value_matrix, w_out):
    block_len, width = prompt.shape[1:]
    n_uly = lax.axis_size("uly")
    n_y, n_z, n_c = (lax.axis_size(a) for a in BLK)
    own_len = block_len // n_uly
    q_width = w_query.shape[1]
    heads = q_width // HEAD
    y, z, c = (lax.axis_index(a) for a in BLK)
    uly = lax.axis_index("uly")
    where = jnp.stack([uly, y, z, c]).astype(jnp.int32)

    slot_column = image_slots.reshape(-1, 1).astype(BF16)
    ones = jnp.ones_like(slot_column)
    pad = jnp.zeros((slot_column.shape[0], HEAD - 2), BF16)
    tagged = jnp.concatenate([image_rows[0, 0], slot_column, ones, pad], axis=1)
    images = lax.all_to_all(
        jnp.broadcast_to(tagged[None], (n_uly, *tagged.shape)), "uly", 0, 0, tiled=True
    ).reshape(-1, width + HEAD)

    w_turned = w_out.T
    w_near = lax.all_to_all(
        jnp.broadcast_to(w_turned[None], (n_z * n_c, *w_turned.shape)), BLK[1:], 0, 0, tiled=True
    ).reshape(-1, q_width)
    w_all = lax.all_gather(w_near, BLK[0], axis=0, tiled=True)

    block = (y * n_z + z) * n_c + c
    cosine, sine = rope_tables(block * block_len + jnp.arange(block_len, dtype=jnp.int32))

    smem = pl.BlockSpec(memory_space=pltpu.SMEM)
    vmem = pl.BlockSpec(memory_space=pltpu.VMEM)
    queries, key_value, own = pl.pallas_call(
        qkv_kernel,
        out_shape=(
            jax.ShapeDtypeStruct((n_z, heads * block_len, HEAD), BF16),
            jax.ShapeDtypeStruct((n_y, block_len, 2 * HEAD), BF16),
            jax.ShapeDtypeStruct((own_len, width), F32),
        ),
        in_specs=[smem] + [vmem] * 8,
        out_specs=[vmem] * 3,
        scratch_shapes=[pltpu.VMEM((block_len, width), F32)],
        compiler_params=pltpu.CompilerParams(vmem_limit_bytes=24 << 20),
        name="qkv",
    )(where, images, prompt[0], norm_gain[None], w_query, key_matrix, value_matrix, cosine, sine)

    near = lax.all_to_all(key_value, BLK[0], 0, 0, tiled=True)
    asked = lax.all_to_all(queries, BLK[1], 0, 0, tiled=True)
    far = lax.ppermute(near, BLK[2], [(i, (i + 1) % n_c) for i in range(n_c)])

    rows = heads * block_len
    partial = pl.pallas_call(
        attend_kernel,
        out_shape=jax.ShapeDtypeStruct((n_z, rows + STAT_ROWS, HEAD), BF16),
        grid=(n_z,),
        in_specs=[
            smem,
            pl.BlockSpec((1, rows, HEAD), lambda i: (i, 0, 0)),
            whole_block(near.shape),
            whole_block(far.shape),
        ],
        out_specs=pl.BlockSpec((1, rows + STAT_ROWS, HEAD), lambda i: (i, 0, 0)),
        scratch_shapes=[pltpu.VMEM((n_y, rows, 2 * block_len), F32)],
        compiler_params=pltpu.CompilerParams(vmem_limit_bytes=24 << 20),
        name="attend",
    )(where, asked, near, far)

    parts = lax.all_to_all(partial, BLK[1], 0, 0, tiled=True)
    chunk = width // 4
    projected = pl.pallas_call(
        project_kernel,
        out_shape=jax.ShapeDtypeStruct((block_len, width), BF16),
        grid=(width // chunk,),
        in_specs=[whole_block(parts.shape), pl.BlockSpec((chunk, q_width), lambda i: (i, 0))],
        out_specs=pl.BlockSpec((block_len, chunk), lambda i: (0, i)),
        scratch_shapes=[pltpu.VMEM((block_len, q_width), BF16)],
        compiler_params=pltpu.CompilerParams(vmem_limit_bytes=24 << 20),
        name="project",
    )(parts, w_all)

    shares = lax.all_to_all(
        projected.reshape(n_uly, own_len, width), "uly", 0, 0, tiled=True
    )
    return (own + shares.astype(F32).sum(axis=0)).astype(BF16)[None]


def solution(mesh):
    split = Mesh(mesh.devices.reshape(mesh.shape["uly"], 8, 4, 2), ("uly", *BLK))
    placed = (
        P(BLK, None, None),
        P("uly", BLK, None, None),
        P("uly", BLK, None),
        P(),
        P(None, "uly"),
        P(None, "uly"),
        P(None, "uly"),
        P("uly", BLK),
    )
    return jax.shard_map(
        body, mesh=split, in_specs=placed, out_specs=P(BLK, "uly", None), check_vma=False
    )
```

time: 195 us -> 151 us (0.77)
  the two profiles are of different devices: /device:TPU:1 before, /device:TPU:48 now
where the time goes in v1:
time: 151 us
  blocking collectives  77.8 us (52%)
  Pallas kernels  18.6 us (12%)
  waiting for transfers between devices  17.4 us (12%)
  between operations  13.5 us (9%)
  local copies, waits for them, and re-layouts  10.4 us (7%)
  starting transfers between devices  9.79 us (6%)
  other arithmetic  3.17 us (2%)
    all_to_all x1, blocking collectives, body(): near = lax.all_to_all(key_value, BLK[0], 0, 0, tiled=True)  24.6 us
    all_to_all x1, blocking collectives, body(): lax.all_to_all(jnp.broadcast_to(w_turned[None], (n_z * n_c, *w_turned.sha...  23.7 us
    all_to_all x1, blocking collectives, body(): parts = lax.all_to_all(partial, BLK[1], 0, 0, tiled=True)  14.9 us
    all_to_all x1, blocking collectives, body(): lax.all_to_all(projected.reshape(n_uly, own_len, width), 'uly', 0, 0, til...  14.7 us
    pallas_call x1, Pallas kernels, body(): pl.pallas_call(attend_kernel, out_shape=jax.ShapeDtypeStruct((n_z, rows +...  14.6 us
    all_to_all x1, waiting for transfers between devices, body(): asked = lax.all_to_all(queries, BLK[1], 0, 0, tiled=True)  10.3 us
    unnamed x26, local copies, waits for them, and re-layouts  7.66 us
    all_to_all x1, waiting for transfers between devices, body(): lax.all_to_all(jnp.broadcast_to(tagged[None], (n_uly, *tagged.shape)), 'u...  7.11 us
  transfers between devices with their start and end apart: 4, of which 2 were waited for; matrix products, arithmetic and copies ran while one was open for 3% of the time, Pallas kernels for 11%

profile of v1, /device:TPU:48, one launch (start us, length us, event | category | flops | bytes accessed | tf_op | source)
XLA Modules:
  0.0 150.7 jit_solution(13333464033341977570)
XLA Ops:
  6.5 0.9 broadcast_in_dim.26
  7.5 23.7 %all_to_all.30 = bf16[8,48,384]{2,1,0:T(8,128)(2,1)} all-to-all(bf16[8,48,384]{2,1,0:T(8,128)(2,1)S(1)} %broadcast_in_dim.26), channel_id=1, replica_groups=mesh['uly'=8,'blk_y'=8,'blk_z'=4,'blk_c'=2] {'blk_z','blk_c'}, dimensions={0} | all-to-all | bytes 589824 | tf_op jit(solution)/shard_map/all_to_all | solution.py:188
  31.2 0.7 convert_bitcast_fusion
  31.9 0.9 concatenate.9
  32.8 0.8 broadcast_in_dim.11
  33.6 4.4 %all-to-all-start = ((bf16[8,8,3200]{2,1,0:T(8,128)(2,1)}), bf16[8,8,3200]{2,1,0:T(8,128)(2,1)S(1)}, u32[]{:S(2)}, u32[]{:S(2)}) async-start(bf16[8,8,3200]{2,1,0:T(8,128)(2,1)} %broadcast_in_dim.11), calls=%async_computation | async-start | bytes 819200 | tf_op jit(solution)/shard_map/all_to_all | solution.py:183
  39.0 0.8 pad_maximum_fusion
  39.8 7.1 %all-to-all-done = bf16[8,8,3200]{2,1,0:T(8,128)(2,1)S(1)} async-done(((bf16[8,8,3200]{2,1,0:T(8,128)(2,1)}), bf16[8,8,3200]{2,1,0:T(8,128)(2,1)S(1)}, u32[]{:S(2)}, u32[]{:S(2)}) %all-to-all-start) | async-done | bytes 409632 | tf_op jit(solution)/shard_map/all_to_all | solution.py:183
  46.9 1.1 copy-done.3
  48.0 1.1 copy-done.4
  49.2 0.8 copy-done.6
  50.0 0.8 copy-done.7
  50.8 0.7 copy-done.10
  52.2 2.2 %qkv.1 = (bf16[4,384,128]{2,1,0:T(8,128)(2,1)S(1)}, bf16[8,128,256]{2,1,0:T(8,128)(2,1)S(1)}, f32[16,3072]{1,0:T(8,128)S(1)}) custom-call(s32[4]{0:T(128)S(1)} %copy-done.11, bf16[64,3200]{1,0:T(8,128)(2,1)S(1)} %bitcast.16, bf16[128,3072]{1,0:T(8,128)(2,1)S(1)} %bitcast.17, f32[1,3072]{1,0:T(1,128)S(1)} %bitcast.18, bf16[3072,384]{1,0:T(8,128)(2,1)S(1)} %copy-done, ...), custom_call_target="tpu_custom_call" | custom-call | tf_op jit(solution)/shard_map/qkv/pallas_call | solution.py:198
  54.4 24.6 %all_to_all.31.near_ref = bf16[8,128,256]{2,1,0:T(8,128)(2,1)S(1)} all-to-all(bf16[8,128,256]{2,1,0:T(8,128)(2,1)S(1)} %get-tuple-element.10), channel_id=1, replica_groups=mesh['uly'=8,'blk_y'=8,'blk_z'=4,'blk_c'=2] {'blk_y'}, dimensions={0} | all-to-all | bytes 1048576 | tf_op jit(solution)/shard_map/all_to_all | solution.py:212
  79.0 3.5 %all-to-all-start.1 = ((bf16[4,384,128]{2,1,0:T(8,128)(2,1)}), bf16[4,384,128]{2,1,0:T(8,128)(2,1)S(1)}, u32[]{:S(2)}, u32[]{:S(2)}) async-start(bf16[4,384,128]{2,1,0:T(8,128)(2,1)} %copy-done.5), calls=%async_computation.1 | async-start | bytes 786432 | tf_op jit(solution)/shard_map/all_to_all | solution.py:213
  82.5 1.9 %collective-permute-start = (bf16[8,128,256]{2,1,0:T(8,128)(2,1)S(1)}, bf16[8,128,256]{2,1,0:T(8,128)(2,1)S(1)}, u32[]{:S(2)}, u32[]{:S(2)}) collective-permute-start(bf16[8,128,256]{2,1,0:T(8,128)(2,1)S(1)} %all_to_all.31.near_ref), channel_id=1, source_target_pairs={{0,1},{1,0},{2,3},{3,2},{4,5},{5,4},{6,7},{7,6},{8,9},{9,8},{10,11... | collective-permute-start | bytes 1572872 | tf_op jit(solution)/shard_map/ppermute | solution.py:214
  84.4 10.3 %all-to-all-done.1.q_ref = bf16[4,384,128]{2,1,0:T(8,128)(2,1)S(1)} async-done(((bf16[4,384,128]{2,1,0:T(8,128)(2,1)}), bf16[4,384,128]{2,1,0:T(8,128)(2,1)S(1)}, u32[]{:S(2)}, u32[]{:S(2)}) %all-to-all-start.1) | async-done | bytes 393248 | tf_op jit(solution)/shard_map/all_to_all | solution.py:213
  95.4 14.6 %attend.1 = bf16[4,400,128]{2,1,0:T(8,128)(2,1)S(1)} custom-call(s32[4]{0:T(128)S(1)} %copy-done.12, bf16[4,384,128]{2,1,0:T(8,128)(2,1)S(1)} %all-to-all-done.1.q_ref, bf16[8,128,256]{2,1,0:T(8,128)(2,1)S(1)} %all_to_all.31.near_ref, bf16[8,128,256]{2,1,0:T(8,128)(2,1)S(1)} %collective-permute-done.far_ref), custom_call_target="tpu_custom_call" | custom-call | tf_op jit(solution)/shard_map/attend/pallas_call | solution.py:217
  110.0 14.9 %all_to_all.32.o_ref = bf16[4,400,128]{2,1,0:T(8,128)(2,1)S(1)} all-to-all(bf16[4,400,128]{2,1,0:T(8,128)(2,1)S(1)} %attend.1), channel_id=1, replica_groups=mesh['uly'=8,'blk_y'=8,'blk_z'=4,'blk_c'=2] {'blk_z'}, dimensions={0} | all-to-all | bytes 819200 | tf_op jit(solution)/shard_map/all_to_all | solution.py:233
  124.9 1.7 %copy-done.1 = bf16[3072,384]{1,0:T(8,128)(2,1)S(1)} copy-done((bf16[3072,384]{1,0:T(8,128)(2,1)S(1)}, bf16[3072,384]{1,0:T(8,128)(2,1)}, u32[]{:S(2)}) %copy-start.1) | copy-done | bytes 2359320
  126.5 1.8 %project.1 = bf16[128,3072]{1,0:T(8,128)(2,1)S(1)} custom-call(bf16[4,400,128]{2,1,0:T(8,128)(2,1)S(1)} %all_to_all.32.o_ref, bf16[3072,384]{1,0:T(8,128)(2,1)S(1)} %copy-done.1), custom_call_target="tpu_custom_call" | custom-call | tf_op jit(solution)/shard_map/project/pallas_call | solution.py:235
  128.3 14.7 %all_to_all.33 = bf16[8,16,3072]{2,1,0:T(8,128)(2,1)S(1)} all-to-all(bf16[8,16,3072]{2,1,0:T(8,128)(2,1)S(1)} %bitcast.15), channel_id=1, replica_groups=mesh['uly'=8,'blk_y'=8,'blk_z'=4,'blk_c'=2] {'uly'}, dimensions={0} | all-to-all | bytes 1572864 | tf_op jit(solution)/shard_map/all_to_all | solution.py:246
  143.2 0.7 fusion
  (32 shorter events, 2.6 us)
Async XLA Ops:
  6.5 40.4 %copy-start.2 = (bf16[1,128,3072]{2,1,0:T(8,128)(2,1)S(1)}, bf16[1,128,3072]{2,1,0:T(8,128)(2,1)}, u32[]{:S(2)}) copy-start(bf16[1,128,3072]{2,1,0:T(8,128)(2,1)} %param.8) | copy-start | bytes 2359300
  6.5 40.4 %copy-start = (bf16[3072,384]{1,0:T(8,128)(2,1)S(1)}, bf16[3072,384]{1,0:T(8,128)(2,1)}, u32[]{:S(2)}) copy-start(bf16[3072,384]{1,0:T(8,128)(2,1)} %wq_ref.1) | copy-start | bytes 7077892
  6.5 118.3 %all-gather.2.cloned.1.call-start = ((), (), s32[]{:S(2)}) async-start(), calls=%async_computation.6 | async-start | bytes 2654208 | tf_op jit(solution)/shard_map/all_gather | solution.py:191
  33.6 13.3 %all-to-all-start = ((bf16[8,8,3200]{2,1,0:T(8,128)(2,1)}), bf16[8,8,3200]{2,1,0:T(8,128)(2,1)S(1)}, u32[]{:S(2)}, u32[]{:S(2)}) async-start(bf16[8,8,3200]{2,1,0:T(8,128)(2,1)} %broadcast_in_dim.11), calls=%async_computation | async-start | bytes 819200 | tf_op jit(solution)/shard_map/all_to_all | solution.py:183
  46.9 1.1 copy-start.3
  48.0 1.1 copy-start.4
  49.2 0.8 copy-start.6
  50.0 0.8 copy-start.7
  50.8 0.7 copy-start.10
  51.6 0.7 copy-start.11
  54.4 24.6 %copy-start.5 = (bf16[4,384,128]{2,1,0:T(8,128)(2,1)}, bf16[4,384,128]{2,1,0:T(8,128)(2,1)S(1)}, u32[]{:S(2)}) copy-start(bf16[4,384,128]{2,1,0:T(8,128)(2,1)S(1)} %get-tuple-element.9) | copy-start | bytes 1179652
  54.4 24.6 %copy-start.8 = (f32[16,3072]{1,0:T(8,128)}, f32[16,3072]{1,0:T(8,128)S(1)}, u32[]{:S(2)}) copy-start(f32[16,3072]{1,0:T(8,128)S(1)} %get-tuple-element.8) | copy-start | bytes 589828
  79.0 15.7 %all-to-all-start.1 = ((bf16[4,384,128]{2,1,0:T(8,128)(2,1)}), bf16[4,384,128]{2,1,0:T(8,128)(2,1)S(1)}, u32[]{:S(2)}, u32[]{:S(2)}) async-start(bf16[4,384,128]{2,1,0:T(8,128)(2,1)} %copy-done.5), calls=%async_computation.1 | async-start | bytes 786432 | tf_op jit(solution)/shard_map/all_to_all | solution.py:213
  82.5 12.2 %collective-permute-start = (bf16[8,128,256]{2,1,0:T(8,128)(2,1)S(1)}, bf16[8,128,256]{2,1,0:T(8,128)(2,1)S(1)}, u32[]{:S(2)}, u32[]{:S(2)}) collective-permute-start(bf16[8,128,256]{2,1,0:T(8,128)(2,1)S(1)} %all_to_all.31.near_ref), channel_id=1, source_target_pairs={{0,1},{1,0},{2,3},{3,2},{4,5},{5,4},{6,7},{7,6},{8,9},{9,8},{10,11... | collective-permute-start | bytes 1572872 | tf_op jit(solution)/shard_map/ppermute | solution.py:214
  94.7 0.7 copy-start.12
  124.9 1.7 %copy-start.1 = (bf16[3072,384]{1,0:T(8,128)(2,1)S(1)}, bf16[3072,384]{1,0:T(8,128)(2,1)}, u32[]{:S(2)}) copy-start(bf16[3072,384]{1,0:T(8,128)(2,1)} %all-gather.2.cloned.1.call-done.w_ref) | copy-start | bytes 7077892
  126.5 16.6 %copy-start.9 = (f32[16,3072]{1,0:T(8,128)S(1)}, f32[16,3072]{1,0:T(8,128)}, u32[]{:S(2)}) copy-start(f32[16,3072]{1,0:T(8,128)} %copy-done.8) | copy-start | bytes 589828
Sparse Core Ops, SparseCore 0:
  31.3 47.1 all-gather.1

commit v2 on v1

v2 whole, which is shorter than its diff:
```python
import functools
import math

import jax
import jax.numpy as jnp
from jax import lax
from jax.experimental import pallas as pl
from jax.experimental.pallas import tpu as pltpu
from jax.sharding import Mesh
from jax.sharding import PartitionSpec as P

HEAD = 128
BLK = ("blk_y", "blk_z", "blk_c")
NEG = -(2.0**127)
CHUNK = 4
EXP2_SCALE = math.log2(math.e) / math.sqrt(HEAD)
STAT_ROWS = 16
F32 = jnp.float32
BF16 = jnp.bfloat16


def nt_dot(a, b):
    return lax.dot_general(a, b, (((1,), (1,)), ((), ())), preferred_element_type=F32)


def tn_dot(a, b):
    return lax.dot_general(a, b, (((0,), (0,)), ((), ())), preferred_element_type=F32)


def rope_tables(positions):
    fraction = jnp.arange(0, HEAD, 2).astype(F32) / HEAD
    inverse = jnp.exp(-math.log(500000.0) * fraction)
    angles = positions.astype(F32)[:, None] * inverse[None, :]
    cosine, sine = jnp.cos(angles), jnp.sin(angles)
    return jnp.concatenate([cosine, cosine], axis=1), jnp.concatenate([-sine, sine], axis=1)


def qkv_kernel(img_ref, prompt_ref, gain_ref, table_ref, wq_hbm, wk_hbm, wv_hbm,
               q_ref, kv_ref, own_ref, placed_ref, wq_ref, wk_ref, wv_ref, sems):
    copies = [
        pltpu.make_async_copy(source, target, sems.at[i])
        for i, (source, target) in enumerate(
            [(wk_hbm, wk_ref), (wv_hbm, wv_ref), (wq_hbm, wq_ref)]
        )
    ]
    for copy in copies:
        copy.start()
    length, width = prompt_ref.shape
    own_len = own_ref.shape[0]
    rows = img_ref.shape[0]
    slots = img_ref[:, width : width + 1].astype(F32)
    lanes = lax.broadcasted_iota(jnp.int32, (rows, length), 1).astype(F32)
    flags = jnp.where(slots == lanes, 1.0, 0.0).astype(BF16)
    present = tn_dot(flags, img_ref[:, width:])[:, 1:2] > 0.5
    chosen = tn_dot(flags, img_ref[:, :width])
    placed = jnp.where(present, chosen, prompt_ref[...].astype(F32))
    placed_ref[...] = placed
    mean_square = jnp.mean(placed * placed, axis=1, keepdims=True)
    normed = (placed * lax.rsqrt(mean_square + 1e-05) * gain_ref[...]).astype(BF16)
    first = pl.multiple_of(lax.axis_index("uly") * own_len, own_len)
    own_ref[...] = placed_ref[pl.ds(first, own_len), :]
    cosine, sine = table_ref[:, :HEAD], table_ref[:, HEAD:]

    def rope(v):
        return (v * cosine + pltpu.roll(v, HEAD // 2, 1) * sine).astype(BF16)

    copies[0].wait()
    keys = rope(jnp.dot(normed, wk_ref[...], preferred_element_type=F32))
    copies[1].wait()
    values = jnp.dot(normed, wv_ref[...], preferred_element_type=F32).astype(BF16)
    for i in range(kv_ref.shape[0]):
        kv_ref[i, :, :HEAD] = keys
        kv_ref[i, :, HEAD:] = values
    copies[2].wait()
    queries = jnp.dot(normed, wq_ref[...], preferred_element_type=F32)
    for h in range(wq_ref.shape[1] // HEAD):
        q_ref[h * length : (h + 1) * length, :] = rope(queries[:, h * HEAD : (h + 1) * HEAD])


def in_pieces(values, count):
    pieces = []
    for _ in range(count):
        pieces.append(values.astype(BF16).astype(F32))
        values = values - pieces[-1]
    return pieces


def attend_kernel(*refs):
    n_z = len(refs) - 5
    q_refs = refs[:n_z]
    near_ref, far_ref, o_ref, s_ref, all_q_ref = refs[n_z:]
    y, z, c = (lax.axis_index(a) for a in BLK)
    n_y, length = near_ref.shape[:2]
    rows = q_refs[0].shape[0]
    heads = rows // length
    for d in range(n_z):
        all_q_ref[d] = q_refs[d][...]
    chunks = [(ref, i) for ref in (near_ref, far_ref) for i in range(0, n_y, CHUNK)]
    wide = CHUNK * length

    def folded(s, op):
        return functools.reduce(op, [s[:, i : i + HEAD] for i in range(0, s.shape[1], HEAD)])

    def one_block(d, _):
        zq = lax.rem(z + d, n_z)
        queries = all_q_ref[d]
        column = lax.broadcasted_iota(jnp.int32, (length, HEAD), 1)
        ahead = column - lax.broadcasted_iota(jnp.int32, (length, HEAD), 0)
        ahead = jnp.concatenate([ahead] * heads, axis=0)
        best = jnp.full((rows, HEAD), NEG, F32)
        for k, (ref, i) in enumerate(chunks):
            s = nt_dot(queries, ref[i : i + CHUNK, :, :HEAD].reshape(wide, HEAD))
            core = jnp.int32(0) if ref is near_ref else 2 * c - 1
            for j in range(CHUNK):
                room = ((2 * n_z) * (y - i - j) + 2 * (zq - z) + core) * length
                part = jnp.where(ahead <= room, s[:, j * length : (j + 1) * length], NEG)
                s_ref[k, :, j * length : (j + 1) * length] = part
                best = jnp.maximum(best, part)
        top = jnp.max(best, axis=1, keepdims=True)
        shift = top * EXP2_SCALE
        total = jnp.zeros((rows, HEAD), F32)
        mixed = jnp.zeros((rows, HEAD), F32)
        for k, (ref, i) in enumerate(chunks):
            weights = jnp.exp2(s_ref[k] * EXP2_SCALE - shift)
            total = total + folded(weights, jnp.add)
            values = ref[i : i + CHUNK, :, HEAD:].reshape(wide, HEAD)
            mixed = mixed + jnp.dot(weights.astype(BF16), values, preferred_element_type=F32)
        total = jnp.sum(total, axis=1, keepdims=True)
        tile = jnp.zeros((length, HEAD), F32)
        for h in range(heads):
            part = slice(h * length, (h + 1) * length)
            tile = jnp.where(column == h, top[part], tile)
            tile = jnp.where(column == heads + h, total[part], tile)
        stats = tile.T[: 2 * heads]
        tops, totals = stats[:heads], stats[heads:]
        pieces = [*in_pieces(tops, 3), *in_pieces(totals, 2)]
        pieces.append(jnp.zeros((STAT_ROWS - 5 * heads, length), F32))
        o_ref[zq, :rows, :] = (mixed / total).astype(BF16)
        o_ref[zq, rows:, :] = jnp.concatenate(pieces, axis=0).astype(BF16)
        return 0

    lax.fori_loop(0, n_z, one_block, 0)


def project_kernel(o_ref, w_ref, out_ref, attended_ref):
    parts = o_ref.shape[0]
    rows = o_ref.shape[1] - STAT_ROWS
    length = o_ref.shape[2]
    heads = rows // length

    @pl.when(pl.program_id(0) == 0)
    def _():
        tops, totals = [], []
        for i in range(parts):
            stats = o_ref[i, rows:, :].astype(F32)
            pieces = [stats[k * heads : (k + 1) * heads] for k in range(5)]
            tops.append(pieces[0] + pieces[1] + pieces[2])
            totals.append(pieces[3] + pieces[4])
        best = functools.reduce(jnp.maximum, tops)
        grown = [jnp.exp2((t - best) * EXP2_SCALE) for t in tops]
        grown = [g * t for g, t in zip(grown, totals)]
        whole = sum(grown)
        share = [g / whole for g in grown]
        tile = jnp.concatenate(share + [jnp.zeros((HEAD - parts * heads, length), F32)], axis=0).T
        for h in range(heads):
            part = slice(h * length, (h + 1) * length)
            mixed = sum(
                o_ref[i, part, :].astype(F32) * tile[:, i * heads + h : i * heads + h + 1]
                for i in range(parts)
            )
            attended_ref[:, h * HEAD : (h + 1) * HEAD] = mixed.astype(BF16)

    z = lax.axis_index(BLK[1])
    many, n_c, n_z = w_ref.shape[:3]
    w = jnp.concatenate(
        [w_ref[i, c, lax.rem(zz - z + n_z, n_z)] for i in range(many) for zz in range(n_z) for c in range(n_c)],
        axis=0,
    )
    out_ref[...] = nt_dot(attended_ref[...], w).astype(BF16)


def whole_block(shape):
    return pl.BlockSpec(shape, lambda *_: (0,) * len(shape))


def body(prompt, image_rows, image_slots, norm_gain, w_query, key_matrix, value_matrix, w_out):
    block_len, width = prompt.shape[1:]
    n_uly = lax.axis_size("uly")
    n_y, n_z, n_c = (lax.axis_size(a) for a in BLK)
    own_len = block_len // n_uly
    q_width = w_query.shape[1]
    heads = q_width // HEAD
    y, z, c = (lax.axis_index(a) for a in BLK)
    slot_column = image_slots.reshape(-1, 1).astype(BF16)
    ones = jnp.ones_like(slot_column)
    pad = jnp.zeros((slot_column.shape[0], HEAD - 2), BF16)
    tagged = jnp.concatenate([image_rows[0, 0], slot_column, ones, pad], axis=1)
    tagged = jnp.broadcast_to(tagged[None], (n_uly, *tagged.shape))
    tagged, w_turned = lax.optimization_barrier((tagged, w_out.T))
    images = lax.all_to_all(tagged, "uly", 0, 0, tiled=True).reshape(-1, width + HEAD)

    def from_next(array, axis, d):
        n = lax.axis_size(axis)
        return lax.ppermute(array, axis, [((i + d) % n, i) for i in range(n)])

    w_near = jnp.stack([w_turned] + [from_next(w_turned, BLK[1], d) for d in range(1, n_z)])
    block = (y * n_z + z) * n_c + c
    cosine, sine = rope_tables(block * block_len + jnp.arange(block_len, dtype=jnp.int32))
    table = jnp.concatenate([cosine, sine], axis=1)

    images, table, _ = lax.optimization_barrier((images, table, w_near))
    w_all = lax.all_gather(w_near, (BLK[0], BLK[2]), axis=0, tiled=False)
    w_all = w_all.reshape(n_y, n_c, n_z, *w_near.shape[1:])

    vmem = pl.BlockSpec(memory_space=pltpu.VMEM)
    hbm = pl.BlockSpec(memory_space=pl.ANY)
    rows = heads * block_len
    queries, key_value, own = pl.pallas_call(
        qkv_kernel,
        out_shape=(
            jax.ShapeDtypeStruct((rows, HEAD), BF16),
            jax.ShapeDtypeStruct((n_y, block_len, 2 * HEAD), BF16),
            jax.ShapeDtypeStruct((own_len, width), F32),
        ),
        in_specs=[vmem] * 4 + [hbm] * 3,
        out_specs=[vmem] * 3,
        scratch_shapes=[
            pltpu.VMEM((block_len, width), F32),
            pltpu.VMEM(w_query.shape, BF16),
            pltpu.VMEM(key_matrix.shape, BF16),
            pltpu.VMEM(value_matrix.shape, BF16),
            pltpu.SemaphoreType.DMA((3,)),
        ],
        compiler_params=pltpu.CompilerParams(vmem_limit_bytes=60 << 20),
        name="qkv",
    )(images, prompt[0], norm_gain[None], table, w_query, key_matrix, value_matrix)

    near = lax.all_to_all(key_value, BLK[0], 0, 0, tiled=True)
    asked = [queries] + [from_next(queries, BLK[1], d) for d in range(1, n_z)]
    near, *asked = lax.optimization_barrier((near, *asked))
    far = from_next(near, BLK[2], 1)

    partial = pl.pallas_call(
        attend_kernel,
        out_shape=jax.ShapeDtypeStruct((n_z, rows + STAT_ROWS, HEAD), BF16),
        in_specs=[vmem] * (n_z + 2),
        out_specs=vmem,
        scratch_shapes=[
            pltpu.VMEM((n_c * n_y // CHUNK, rows, CHUNK * block_len), F32),
            pltpu.VMEM((n_z, rows, HEAD), BF16),
        ],
        compiler_params=pltpu.CompilerParams(vmem_limit_bytes=24 << 20),
        name="attend",
    )(*asked, near, far)

    parts = lax.all_to_all(partial, BLK[1], 0, 0, tiled=True)
    piece = w_out.shape[1]
    projected = pl.pallas_call(
        project_kernel,
        out_shape=jax.ShapeDtypeStruct((block_len, width), BF16),
        grid=(n_y // 2,),
        in_specs=[
            whole_block(parts.shape),
            pl.BlockSpec((2, n_c, n_z, piece, q_width), lambda i: (i, 0, 0, 0, 0)),
        ],
        out_specs=pl.BlockSpec((block_len, 2 * width // n_y), lambda i: (0, i)),
        scratch_shapes=[pltpu.VMEM((block_len, q_width), BF16)],
        compiler_params=pltpu.CompilerParams(vmem_limit_bytes=60 << 20),
        name="project",
    )(parts, w_all)

    shares = lax.all_to_all(
        projected.reshape(n_uly, own_len, width), "uly", 0, 0, tiled=True
    )
    return (own + shares.astype(F32).sum(axis=0)).astype(BF16)[None]


def solution(mesh):
    split = Mesh(mesh.devices.reshape(mesh.shape["uly"], 8, 4, 2), ("uly", *BLK))
    placed = (
        P(BLK, None, None),
        P("uly", BLK, None, None),
        P("uly", BLK, None),
        P(),
        P(None, "uly"),
        P(None, "uly"),
        P(None, "uly"),
        P("uly", BLK),
    )
    return jax.shard_map(
        body, mesh=split, in_specs=placed, out_specs=P(BLK, "uly", None), check_vma=False
    )
```

time: 151 us -> 139 us (0.921)
  the two profiles are of different devices: /device:TPU:48 before, /device:TPU:1 now
where the time goes in v2:
time: 139 us; the launch traced here: 137 us
  starting transfers between devices  45.5 us (33%)
  blocking collectives  32.1 us (23%)
  waiting for transfers between devices  19.9 us (14%)
  Pallas kernels  18.7 us (13%)
  between operations  13.5 us (10%)
  other arithmetic  3.98 us (3%)
  local copies, waits for them, and re-layouts  3.42 us (2%)
    ppermute x7, starting transfers between devices, from_next(): return lax.ppermute(array, axis, [((i + d) % n, i) for i in range(n)])  33.3 us
    all_to_all x1, blocking collectives, body(): lax.all_to_all(projected.reshape(n_uly, own_len, width), 'uly', 0, 0, til...  16.3 us
    all_to_all x1, blocking collectives, body(): parts = lax.all_to_all(partial, BLK[1], 0, 0, tiled=True)  15.8 us
    ppermute x7, waiting for transfers between devices, from_next(): return lax.ppermute(array, axis, [((i + d) % n, i) for i in range(n)])  11.2 us
    pallas_call x1, Pallas kernels, body(): pl.pallas_call(attend_kernel, out_shape=jax.ShapeDtypeStruct((n_z, rows +...  9.12 us
    all_to_all x1, starting transfers between devices, body(): near = lax.all_to_all(key_value, BLK[0], 0, 0, tiled=True)  6.83 us
    all_to_all x1, waiting for transfers between devices, body(): lax.all_to_all(tagged, 'uly', 0, 0, tiled=True).reshape(-1, width + HEAD)  5.85 us
    all_to_all x1, starting transfers between devices, body(): lax.all_to_all(tagged, 'uly', 0, 0, tiled=True).reshape(-1, width + HEAD)  5.33 us
  transfers between devices with their start and end apart: 10, of which 6 were waited for; matrix products, arithmetic and copies ran while one was open for 1% of the time, Pallas kernels for 10%

profile of v2, /device:TPU:1, one launch (start us, length us, event | category | flops | bytes accessed | tf_op | source)
XLA Modules:
  0.0 137.0 jit_solution(9037727090221650416)
XLA Ops:
  7.3 0.9 concatenate.6
  8.2 0.8 broadcast_in_dim.18
  9.0 6.6 %collective-permute-start.2 = (bf16[48,384]{1,0:T(8,128)(2,1)}, bf16[48,384]{1,0:T(8,128)(2,1)S(1)}, u32[]{:S(2)}, u32[]{:S(2)}) collective-permute-start(bf16[48,384]{1,0:T(8,128)(2,1)} %bitcast.20), channel_id=1, source_target_pairs={{6,0},{0,2},{2,4},{4,6},{7,1},{1,3},{3,5},{5,7},{14,8},{8,10},{10,... | collective-permute-start | bytes 110600 | tf_op jit(solution)/shard_map/ppermute | solution.py:204
  15.6 8.8 %collective-permute-start.1 = (bf16[48,384]{1,0:T(8,128)(2,1)}, bf16[48,384]{1,0:T(8,128)(2,1)S(1)}, u32[]{:S(2)}, u32[]{:S(2)}) collective-permute-start(bf16[48,384]{1,0:T(8,128)(2,1)} %bitcast.21), channel_id=1, source_target_pairs={{4,0},{6,2},{0,4},{2,6},{5,1},{7,3},{1,5},{3,7},{12,8},{14,10},{8,... | collective-permute-start | bytes 110600 | tf_op jit(solution)/shard_map/ppermute | solution.py:204
  24.5 3.4 %collective-permute-start = (bf16[48,384]{1,0:T(8,128)(2,1)}, bf16[48,384]{1,0:T(8,128)(2,1)S(1)}, u32[]{:S(2)}, u32[]{:S(2)}) collective-permute-start(bf16[48,384]{1,0:T(8,128)(2,1)} %bitcast.22), channel_id=1, source_target_pairs={{2,0},{4,2},{6,4},{0,6},{3,1},{5,3},{7,5},{1,7},{10,8},{12,10},{14... | collective-permute-start | bytes 110600 | tf_op jit(solution)/shard_map/ppermute | solution.py:204
  27.9 2.4 %collective-permute-done = bf16[48,384]{1,0:T(8,128)(2,1)S(1)} collective-permute-done((bf16[48,384]{1,0:T(8,128)(2,1)}, bf16[48,384]{1,0:T(8,128)(2,1)S(1)}, u32[]{:S(2)}, u32[]{:S(2)}) %collective-permute-start) | collective-permute-done | bytes 36896 | tf_op jit(solution)/shard_map/ppermute | solution.py:204
  30.3 1.5 %pad_maximum_fusion = bf16[4,48,384]{2,1,0:T(8,128)(2,1)} fusion(bf16[1,48,384]{2,1,0:T(8,128)(2,1)S(1)} %bitcast.24, bf16[1,48,384]{2,1,0:T(8,128)(2,1)S(1)} %bitcast.25, bf16[1,48,384]{2,1,0:T(8,128)(2,1)S(1)} %bitcast.26, bf16[1,48,384]{2,1,0:T(8,128)(2,1)} %bitcast.23), kind=kLoop, calls=%fused_computation.2 | loop fusion | flops 221184 | bytes 294912 | tf_op jit(solution)/shard_map/stack | solution.py:206
  31.8 5.3 %all-to-all-start = ((bf16[8,8,3200]{2,1,0:T(8,128)(2,1)}), bf16[8,8,3200]{2,1,0:T(8,128)(2,1)S(1)}, u32[]{:S(2)}, u32[]{:S(2)}) async-start(bf16[8,8,3200]{2,1,0:T(8,128)(2,1)} %broadcast_in_dim.18), calls=%async_computation | async-start | bytes 819200 | tf_op jit(solution)/shard_map/all_to_all | solution.py:200
  38.2 5.8 %all-to-all-done = bf16[8,8,3200]{2,1,0:T(8,128)(2,1)S(1)} async-done(((bf16[8,8,3200]{2,1,0:T(8,128)(2,1)}), bf16[8,8,3200]{2,1,0:T(8,128)(2,1)S(1)}, u32[]{:S(2)}, u32[]{:S(2)}) %all-to-all-start) | async-done | bytes 409632 | tf_op jit(solution)/shard_map/all_to_all | solution.py:200
  44.8 4.8 %qkv.1 = (bf16[384,128]{1,0:T(8,128)(2,1)}, bf16[8,128,256]{2,1,0:T(8,128)(2,1)}, f32[16,3072]{1,0:T(8,128)}) custom-call(bf16[64,3200]{1,0:T(8,128)(2,1)} %bitcast.17, bf16[128,3072]{1,0:T(8,128)(2,1)} %bitcast.18, f32[1,3072]{1,0:T(1,128)} %bitcast.27, f32[128,256]{1,0:T(8,128)} %pad_maximum_fusion.1.table_ref, bf16[3072,384]{1,0:T(8,128)(2,1)} %wq_hbm.1, ...), custom_call_target="tpu_custom_call" | custom-call | tf_op jit(solution)/shard_map/qkv/pallas_call | solution.py:218
  49.6 6.8 %all-to-all-start.1 = ((bf16[8,128,256]{2,1,0:T(8,128)(2,1)}), bf16[8,128,256]{2,1,0:T(8,128)(2,1)S(1)}, u32[]{:S(2)}, u32[]{:S(2)}) async-start(bf16[8,128,256]{2,1,0:T(8,128)(2,1)} %get-tuple-element.22), calls=%async_computation.1 | async-start | bytes 1048576 | tf_op jit(solution)/shard_map/all_to_all | solution.py:238
  56.4 4.3 %collective-permute-start.3 = (bf16[384,128]{1,0:T(8,128)(2,1)}, bf16[384,128]{1,0:T(8,128)(2,1)S(1)}, u32[]{:S(2)}, u32[]{:S(2)}) collective-permute-start(bf16[384,128]{1,0:T(8,128)(2,1)} %get-tuple-element.24.refs_0_), channel_id=1, source_target_pairs={{2,0},{4,2},{6,4},{0,6},{3,1},{5,3},{7,5},{1,7},{10,8},{12,10},{14... | collective-permute-start | bytes 294920 | tf_op jit(solution)/shard_map/ppermute | solution.py:204
  60.7 3.7 %collective-permute-start.4 = (bf16[384,128]{1,0:T(8,128)(2,1)}, bf16[384,128]{1,0:T(8,128)(2,1)S(1)}, u32[]{:S(2)}, u32[]{:S(2)}) collective-permute-start(bf16[384,128]{1,0:T(8,128)(2,1)} %get-tuple-element.24.refs_0_), channel_id=1, source_target_pairs={{4,0},{6,2},{0,4},{2,6},{5,1},{7,3},{1,5},{3,7},{12,8},{14,10},{8,... | collective-permute-start | bytes 294920 | tf_op jit(solution)/shard_map/ppermute | solution.py:204
  64.3 2.2 %collective-permute-start.5 = (bf16[384,128]{1,0:T(8,128)(2,1)}, bf16[384,128]{1,0:T(8,128)(2,1)S(1)}, u32[]{:S(2)}, u32[]{:S(2)}) collective-permute-start(bf16[384,128]{1,0:T(8,128)(2,1)} %get-tuple-element.24.refs_0_), channel_id=1, source_target_pairs={{6,0},{0,2},{2,4},{4,6},{7,1},{1,3},{3,5},{5,7},{14,8},{8,10},{10,... | collective-permute-start | bytes 294920 | tf_op jit(solution)/shard_map/ppermute | solution.py:204
  66.6 4.4 %collective-permute-done.4.refs_2_ = bf16[384,128]{1,0:T(8,128)(2,1)S(1)} collective-permute-done((bf16[384,128]{1,0:T(8,128)(2,1)}, bf16[384,128]{1,0:T(8,128)(2,1)S(1)}, u32[]{:S(2)}, u32[]{:S(2)}) %collective-permute-start.4) | collective-permute-done | bytes 98336 | tf_op jit(solution)/shard_map/ppermute | solution.py:204
  71.0 2.9 %collective-permute-done.5.refs_3_ = bf16[384,128]{1,0:T(8,128)(2,1)S(1)} collective-permute-done((bf16[384,128]{1,0:T(8,128)(2,1)}, bf16[384,128]{1,0:T(8,128)(2,1)S(1)}, u32[]{:S(2)}, u32[]{:S(2)}) %collective-permute-start.5) | collective-permute-done | bytes 98336 | tf_op jit(solution)/shard_map/ppermute | solution.py:204
  73.9 2.8 %all-to-all-done.1.refs_4_ = bf16[8,128,256]{2,1,0:T(8,128)(2,1)S(1)} async-done(((bf16[8,128,256]{2,1,0:T(8,128)(2,1)}), bf16[8,128,256]{2,1,0:T(8,128)(2,1)S(1)}, u32[]{:S(2)}, u32[]{:S(2)}) %all-to-all-start.1) | async-done | bytes 524320 | tf_op jit(solution)/shard_map/all_to_all | solution.py:238
  76.7 4.3 %collective-permute-start.6 = (bf16[8,128,256]{2,1,0:T(8,128)(2,1)S(1)}, bf16[8,128,256]{2,1,0:T(8,128)(2,1)S(1)}, u32[]{:S(2)}, u32[]{:S(2)}) collective-permute-start(bf16[8,128,256]{2,1,0:T(8,128)(2,1)S(1)} %all-to-all-done.1.refs_4_), channel_id=1, source_target_pairs={{1,0},{0,1},{3,2},{2,3},{5,4},{4,5},{7,6},{6,7},{9,8},{8,9},{11,10... | collective-permute-start | bytes 1572872 | tf_op jit(solution)/shard_map/ppermute | solution.py:204
  81.0 1.5 %collective-permute-done.6.refs_5_ = bf16[8,128,256]{2,1,0:T(8,128)(2,1)S(1)} collective-permute-done((bf16[8,128,256]{2,1,0:T(8,128)(2,1)S(1)}, bf16[8,128,256]{2,1,0:T(8,128)(2,1)S(1)}, u32[]{:S(2)}, u32[]{:S(2)}) %collective-permute-start.6) | collective-permute-done | bytes 524320 | tf_op jit(solution)/shard_map/ppermute | solution.py:204
  82.5 0.9 copy-done
  83.4 9.1 %attend.1 = bf16[4,400,128]{2,1,0:T(8,128)(2,1)S(1)} custom-call(bf16[384,128]{1,0:T(8,128)(2,1)S(1)} %copy-done, bf16[384,128]{1,0:T(8,128)(2,1)S(1)} %collective-permute-done.3.refs_1_, bf16[384,128]{1,0:T(8,128)(2,1)S(1)} %collective-permute-done.4.refs_2_, bf16[384,128]{1,0:T(8,128)(2,1)S(1)} %collective-permute-done.5.refs_3_, ...), custom_call_target="tpu_custom_call" | custom-call | tf_op jit(solution)/shard_map/attend/pallas_call | solution.py:243
  92.5 15.8 %all_to_all.20.o_ref = bf16[4,400,128]{2,1,0:T(8,128)(2,1)} all-to-all(bf16[4,400,128]{2,1,0:T(8,128)(2,1)S(1)} %attend.1), channel_id=1, replica_groups=mesh['uly'=8,'blk_y'=8,'blk_z'=4,'blk_c'=2] {'blk_z'}, dimensions={0} | all-to-all | bytes 819200 | tf_op jit(solution)/shard_map/all_to_all | solution.py:256
  108.3 4.8 %project.1 = bf16[128,3072]{1,0:T(8,128)(2,1)} custom-call(bf16[4,400,128]{2,1,0:T(8,128)(2,1)} %all_to_all.20.o_ref, bf16[8,2,4,48,384]{4,3,2,1,0:T(8,128)(2,1)} %bitcast.16), custom_call_target="tpu_custom_call" | custom-call | tf_op jit(solution)/shard_map/project/pallas_call | solution.py:258
  113.1 16.3 %all_to_all.21 = bf16[8,16,3072]{2,1,0:T(8,128)(2,1)S(1)} all-to-all(bf16[8,16,3072]{2,1,0:T(8,128)(2,1)} %bitcast.15), channel_id=1, replica_groups=mesh['uly'=8,'blk_y'=8,'blk_z'=4,'blk_c'=2] {'uly'}, dimensions={0} | all-to-all | bytes 1572864 | tf_op jit(solution)/shard_map/all_to_all | solution.py:272
  (21 shorter events, 3.4 us)
Async XLA Ops:
  6.5 101.8 %all-gather.3.cloned.1.call-start = ((), (), s32[]{:S(2)}) async-start(), calls=%async_computation.4 | async-start | bytes 2506752 | tf_op jit(solution)/shard_map/all_gather | solution.py:212
  9.0 18.9 %collective-permute-start.2 = (bf16[48,384]{1,0:T(8,128)(2,1)}, bf16[48,384]{1,0:T(8,128)(2,1)S(1)}, u32[]{:S(2)}, u32[]{:S(2)}) collective-permute-start(bf16[48,384]{1,0:T(8,128)(2,1)} %bitcast.20), channel_id=1, source_target_pairs={{6,0},{0,2},{2,4},{4,6},{7,1},{1,3},{3,5},{5,7},{14,8},{8,10},{10,... | collective-permute-start | bytes 110600 | tf_op jit(solution)/shard_map/ppermute | solution.py:204
  15.6 12.3 %collective-permute-start.1 = (bf16[48,384]{1,0:T(8,128)(2,1)}, bf16[48,384]{1,0:T(8,128)(2,1)S(1)}, u32[]{:S(2)}, u32[]{:S(2)}) collective-permute-start(bf16[48,384]{1,0:T(8,128)(2,1)} %bitcast.21), channel_id=1, source_target_pairs={{4,0},{6,2},{0,4},{2,6},{5,1},{7,3},{1,5},{3,7},{12,8},{14,10},{8,... | collective-permute-start | bytes 110600 | tf_op jit(solution)/shard_map/ppermute | solution.py:204
  24.5 5.8 %collective-permute-start = (bf16[48,384]{1,0:T(8,128)(2,1)}, bf16[48,384]{1,0:T(8,128)(2,1)S(1)}, u32[]{:S(2)}, u32[]{:S(2)}) collective-permute-start(bf16[48,384]{1,0:T(8,128)(2,1)} %bitcast.22), channel_id=1, source_target_pairs={{2,0},{4,2},{6,4},{0,6},{3,1},{5,3},{7,5},{1,7},{10,8},{12,10},{14... | collective-permute-start | bytes 110600 | tf_op jit(solution)/shard_map/ppermute | solution.py:204
  31.8 12.3 %all-to-all-start = ((bf16[8,8,3200]{2,1,0:T(8,128)(2,1)}), bf16[8,8,3200]{2,1,0:T(8,128)(2,1)S(1)}, u32[]{:S(2)}, u32[]{:S(2)}) async-start(bf16[8,8,3200]{2,1,0:T(8,128)(2,1)} %broadcast_in_dim.18), calls=%async_computation | async-start | bytes 819200 | tf_op jit(solution)/shard_map/all_to_all | solution.py:200
  44.0 0.8 copy-start.1
  49.6 27.1 %all-to-all-start.1 = ((bf16[8,128,256]{2,1,0:T(8,128)(2,1)}), bf16[8,128,256]{2,1,0:T(8,128)(2,1)S(1)}, u32[]{:S(2)}, u32[]{:S(2)}) async-start(bf16[8,128,256]{2,1,0:T(8,128)(2,1)} %get-tuple-element.22), calls=%async_computation.1 | async-start | bytes 1048576 | tf_op jit(solution)/shard_map/all_to_all | solution.py:238
  56.4 10.2 %collective-permute-start.3 = (bf16[384,128]{1,0:T(8,128)(2,1)}, bf16[384,128]{1,0:T(8,128)(2,1)S(1)}, u32[]{:S(2)}, u32[]{:S(2)}) collective-permute-start(bf16[384,128]{1,0:T(8,128)(2,1)} %get-tuple-element.24.refs_0_), channel_id=1, source_target_pairs={{2,0},{4,2},{6,4},{0,6},{3,1},{5,3},{7,5},{1,7},{10,8},{12,10},{14... | collective-permute-start | bytes 294920 | tf_op jit(solution)/shard_map/ppermute | solution.py:204
  60.7 10.3 %collective-permute-start.4 = (bf16[384,128]{1,0:T(8,128)(2,1)}, bf16[384,128]{1,0:T(8,128)(2,1)S(1)}, u32[]{:S(2)}, u32[]{:S(2)}) collective-permute-start(bf16[384,128]{1,0:T(8,128)(2,1)} %get-tuple-element.24.refs_0_), channel_id=1, source_target_pairs={{4,0},{6,2},{0,4},{2,6},{5,1},{7,3},{1,5},{3,7},{12,8},{14,10},{8,... | collective-permute-start | bytes 294920 | tf_op jit(solution)/shard_map/ppermute | solution.py:204
  64.3 9.5 %collective-permute-start.5 = (bf16[384,128]{1,0:T(8,128)(2,1)}, bf16[384,128]{1,0:T(8,128)(2,1)S(1)}, u32[]{:S(2)}, u32[]{:S(2)}) collective-permute-start(bf16[384,128]{1,0:T(8,128)(2,1)} %get-tuple-element.24.refs_0_), channel_id=1, source_target_pairs={{6,0},{0,2},{2,4},{4,6},{7,1},{1,3},{3,5},{5,7},{14,8},{8,10},{10,... | collective-permute-start | bytes 294920 | tf_op jit(solution)/shard_map/ppermute | solution.py:204
  76.7 5.8 %collective-permute-start.6 = (bf16[8,128,256]{2,1,0:T(8,128)(2,1)S(1)}, bf16[8,128,256]{2,1,0:T(8,128)(2,1)S(1)}, u32[]{:S(2)}, u32[]{:S(2)}) collective-permute-start(bf16[8,128,256]{2,1,0:T(8,128)(2,1)S(1)} %all-to-all-done.1.refs_4_), channel_id=1, source_target_pairs={{1,0},{0,1},{3,2},{2,3},{5,4},{4,5},{7,6},{6,7},{9,8},{8,9},{11,10... | collective-permute-start | bytes 1572872 | tf_op jit(solution)/shard_map/ppermute | solution.py:204
  82.5 0.9 copy-start
  108.3 21.2 %copy-start.2 = (f32[16,3072]{1,0:T(8,128)S(1)}, f32[16,3072]{1,0:T(8,128)}, u32[]{:S(2)}) copy-start(f32[16,3072]{1,0:T(8,128)} %get-tuple-element.21) | copy-start | bytes 589828
Sparse Core Ops, SparseCore 0:
  31.9 46.9 all-gather.2

commit v3 on v2

--- a/solution.py
+++ b/solution.py
@@ -35,16 +35,11 @@
     return jnp.concatenate([cosine, cosine], axis=1), jnp.concatenate([-sine, sine], axis=1)
 
 
-def qkv_kernel(img_ref, prompt_ref, gain_ref, table_ref, wq_hbm, wk_hbm, wv_hbm,
-               q_ref, kv_ref, own_ref, placed_ref, wq_ref, wk_ref, wv_ref, sems):
-    copies = [
-        pltpu.make_async_copy(source, target, sems.at[i])
-        for i, (source, target) in enumerate(
-            [(wk_hbm, wk_ref), (wv_hbm, wv_ref), (wq_hbm, wq_ref)]
-        )
-    ]
-    for copy in copies:
-        copy.start()
+def rope(v, table_ref):
+    return v * table_ref[:, :HEAD] + pltpu.roll(v, HEAD // 2, 1) * table_ref[:, HEAD:]
+
+
+def kv_kernel(img_ref, prompt_ref, gain_ref, table_ref, w_ref, normed_ref, kv_ref, own_ref, placed_ref):
     length, width = prompt_ref.shape
     own_len = own_ref.shape[0]
     rows = img_ref.shape[0]
@@ -57,24 +52,23 @@
     placed_ref[...] = placed
     mean_square = jnp.mean(placed * placed, axis=1, keepdims=True)
     normed = (placed * lax.rsqrt(mean_square + 1e-05) * gain_ref[...]).astype(BF16)
+    normed_ref[...] = normed
     first = pl.multiple_of(lax.axis_index("uly") * own_len, own_len)
     own_ref[...] = placed_ref[pl.ds(first, own_len), :]
-    cosine, sine = table_ref[:, :HEAD], table_ref[:, HEAD:]
-
-    def rope(v):
-        return (v * cosine + pltpu.roll(v, HEAD // 2, 1) * sine).astype(BF16)
-
-    copies[0].wait()
-    keys = rope(jnp.dot(normed, wk_ref[...], preferred_element_type=F32))
-    copies[1].wait()
-    values = jnp.dot(normed, wv_ref[...], preferred_element_type=F32).astype(BF16)
+    joined = jnp.dot(normed, w_ref[...], preferred_element_type=F32)
+    keys = rope(joined[:, :HEAD], table_ref).T.astype(BF16)
+    values = joined[:, HEAD:].astype(BF16)
     for i in range(kv_ref.shape[0]):
         kv_ref[i, :, :HEAD] = keys
         kv_ref[i, :, HEAD:] = values
-    copies[2].wait()
-    queries = jnp.dot(normed, wq_ref[...], preferred_element_type=F32)
-    for h in range(wq_ref.shape[1] // HEAD):
-        q_ref[h * length : (h + 1) * length, :] = rope(queries[:, h * HEAD : (h + 1) * HEAD])
+
+
+def q_kernel(normed_ref, table_ref, w_ref, q_ref):
+    length = normed_ref.shape[0]
+    queries = jnp.dot(normed_ref[...], w_ref[...], preferred_element_type=F32)
+    for h in range(w_ref.shape[1] // HEAD):
+        part = rope(queries[:, h * HEAD : (h + 1) * HEAD], table_ref)
+        q_ref[h * length : (h + 1) * length, :] = part.astype(BF16)
 
 
 def in_pieces(values, count):
@@ -109,7 +103,8 @@
         ahead = jnp.concatenate([ahead] * heads, axis=0)
         best = jnp.full((rows, HEAD), NEG, F32)
         for k, (ref, i) in enumerate(chunks):
-            s = nt_dot(queries, ref[i : i + CHUNK, :, :HEAD].reshape(wide, HEAD))
+            keys = jnp.concatenate([ref[i + j, :, :HEAD] for j in range(CHUNK)], axis=1)
+            s = jnp.dot(queries, keys, preferred_element_type=F32)
             core = jnp.int32(0) if ref is near_ref else 2 * c - 1
             for j in range(CHUNK):
                 room = ((2 * n_z) * (y - i - j) + 2 * (zq - z) + core) * length
@@ -196,48 +191,50 @@
     pad = jnp.zeros((slot_column.shape[0], HEAD - 2), BF16)
     tagged = jnp.concatenate([image_rows[0, 0], slot_column, ones, pad], axis=1)
     tagged = jnp.broadcast_to(tagged[None], (n_uly, *tagged.shape))
-    tagged, w_turned = lax.optimization_barrier((tagged, w_out.T))
     images = lax.all_to_all(tagged, "uly", 0, 0, tiled=True).reshape(-1, width + HEAD)
 
     def from_next(array, axis, d):
         n = lax.axis_size(axis)
         return lax.ppermute(array, axis, [((i + d) % n, i) for i in range(n)])
 
-    w_near = jnp.stack([w_turned] + [from_next(w_turned, BLK[1], d) for d in range(1, n_z)])
     block = (y * n_z + z) * n_c + c
     cosine, sine = rope_tables(block * block_len + jnp.arange(block_len, dtype=jnp.int32))
     table = jnp.concatenate([cosine, sine], axis=1)
-
-    images, table, _ = lax.optimization_barrier((images, table, w_near))
-    w_all = lax.all_gather(w_near, (BLK[0], BLK[2]), axis=0, tiled=False)
-    w_all = w_all.reshape(n_y, n_c, n_z, *w_near.shape[1:])
-
+    w_kv = jnp.concatenate([key_matrix, value_matrix], axis=1)
     vmem = pl.BlockSpec(memory_space=pltpu.VMEM)
-    hbm = pl.BlockSpec(memory_space=pl.ANY)
     rows = heads * block_len
-    queries, key_value, own = pl.pallas_call(
-        qkv_kernel,
+    normed, key_value, own = pl.pallas_call(
+        kv_kernel,
         out_shape=(
-            jax.ShapeDtypeStruct((rows, HEAD), BF16),
+            jax.ShapeDtypeStruct((block_len, width), BF16),
             jax.ShapeDtypeStruct((n_y, block_len, 2 * HEAD), BF16),
             jax.ShapeDtypeStruct((own_len, width), F32),
         ),
-        in_specs=[vmem] * 4 + [hbm] * 3,
+        in_specs=[vmem] * 5,
         out_specs=[vmem] * 3,
-        scratch_shapes=[
-            pltpu.VMEM((block_len, width), F32),
-            pltpu.VMEM(w_query.shape, BF16),
-            pltpu.VMEM(key_matrix.shape, BF16),
-            pltpu.VMEM(value_matrix.shape, BF16),
-            pltpu.SemaphoreType.DMA((3,)),
-        ],
-        compiler_params=pltpu.CompilerParams(vmem_limit_bytes=60 << 20),
-        name="qkv",
-    )(images, prompt[0], norm_gain[None], table, w_query, key_matrix, value_matrix)
+        scratch_shapes=[pltpu.VMEM((block_len, width), F32)],
+        compiler_params=pltpu.CompilerParams(vmem_limit_bytes=24 << 20),
+        name="kv",
+    )(images, prompt[0], norm_gain[None], table, w_kv)
+    queries = pl.pallas_call(
+        q_kernel,
+        out_shape=jax.ShapeDtypeStruct((rows, HEAD), BF16),
+        in_specs=[vmem] * 3,
+        out_specs=vmem,
+        compiler_params=pltpu.CompilerParams(vmem_limit_bytes=24 << 20),
+        cost_estimate=pl.CostEstimate(
+            flops=2 * block_len * width * q_width, bytes_accessed=2 * width * q_width, transcendentals=0
+        ),
+        name="q",
+    )(normed, table, w_query)
 
     near = lax.all_to_all(key_value, BLK[0], 0, 0, tiled=True)
     asked = [queries] + [from_next(queries, BLK[1], d) for d in range(1, n_z)]
-    near, *asked = lax.optimization_barrier((near, *asked))
+    _, w_turned = lax.optimization_barrier((key_value, w_out.T))
+    w_near = jnp.stack([w_turned] + [from_next(w_turned, BLK[1], d) for d in range(1, n_z)])
+    near, w_near, *asked = lax.optimization_barrier((near, w_near, *asked))
+    w_all = lax.all_gather(w_near, (BLK[0], BLK[2]), axis=0, tiled=False)
+    w_all = w_all.reshape(n_y, n_c, n_z, *w_near.shape[1:])
     far = from_next(near, BLK[2], 1)
 
     partial = pl.pallas_call(
@@ -265,7 +262,7 @@
         ],
         out_specs=pl.BlockSpec((block_len, 2 * width // n_y), lambda i: (0, i)),
         scratch_shapes=[pltpu.VMEM((block_len, q_width), BF16)],
-        compiler_params=pltpu.CompilerParams(vmem_limit_bytes=60 << 20),
+        compiler_params=pltpu.CompilerParams(vmem_limit_bytes=24 << 20),
         name="project",
     )(parts, w_all)
 

time: 139 us -> 142 us (1.022)
  Pallas kernels: 18.7 us -> 13.1 us
  waiting for transfers between devices: 19.9 us -> 23.6 us
  local copies, waits for them, and re-layouts: 3.42 us -> 7.12 us
    all_gather x1, waiting for transfers between devices: 0.01 us -> 10.1 us  [body(): w_all = lax.all_gather(w_near, (BLK[0], BLK[2]), axis=0, tiled=False)]
    unnamed x6 -> x14, local copies, waits for them, and re-layouts: 1.65 us -> 5.35 us
    pallas_call x1, Pallas kernels: 4.79 us -> 1.87 us  [body(): pl.pallas_call(project_kernel, out_shape=jax.ShapeDtypeStruct((block_len,...]
    all_to_all x1, waiting for transfers between devices: 2.81 us -> 0.01 us  [body(): near = lax.all_to_all(key_value, BLK[0], 0, 0, tiled=True)]
    ppermute x7, waiting for transfers between devices: 11.2 us -> 8.59 us  [from_next(): return lax.ppermute(array, axis, [((i + d) % n, i) for i in range(n)])]
    pallas_call x1 -> x2, Pallas kernels: 4.76 us -> 2.89 us  [the longest x1 2.24 us: body(): pl.pallas_call(kv_kernel, out_shape=(jax.ShapeDtypeStruct((block_len, wid...]
    concatenate x0 -> x1, other arithmetic: none -> 1.54 us  [body(): w_kv = jnp.concatenate([key_matrix, value_matrix], axis=1)]
    all_to_all x1, starting transfers between devices: 5.33 us -> 6.79 us  [body(): lax.all_to_all(tagged, 'uly', 0, 0, tiled=True).reshape(-1, width + HEAD)]
  transfers between devices with their start and end apart: 10 -> 10, of which waited for: 6 -> 5; matrix products, arithmetic and copies ran while one was open for 1% -> 2% of each run, Pallas kernels for 10% -> 6%
where the time goes in v3:
time: 142 us; the launch traced here: 141 us
  starting transfers between devices  46.6 us (33%)
  blocking collectives  32.7 us (23%)
  waiting for transfers between devices  23.6 us (17%)
  between operations  13.6 us (10%)
  Pallas kernels  13.1 us (9%)
  local copies, waits for them, and re-layouts  7.12 us (5%)
  other arithmetic  4.1 us (3%)
    ppermute x7, starting transfers between devices, from_next(): return lax.ppermute(array, axis, [((i + d) % n, i) for i in range(n)])  32 us
    all_to_all x1, blocking collectives, body(): lax.all_to_all(projected.reshape(n_uly, own_len, width), 'uly', 0, 0, til...  17 us
    all_to_all x1, blocking collectives, body(): parts = lax.all_to_all(partial, BLK[1], 0, 0, tiled=True)  15.7 us
    all_gather x1, waiting for transfers between devices, body(): w_all = lax.all_gather(w_near, (BLK[0], BLK[2]), axis=0, tiled=False)  10.1 us
    ppermute x7, waiting for transfers between devices, from_next(): return lax.ppermute(array, axis, [((i + d) % n, i) for i in range(n)])  8.59 us
    pallas_call x1, Pallas kernels, body(): pl.pallas_call(attend_kernel, out_shape=jax.ShapeDtypeStruct((n_z, rows +...  8.37 us
    all_to_all x1, starting transfers between devices, body(): near = lax.all_to_all(key_value, BLK[0], 0, 0, tiled=True)  7.84 us
    all_to_all x1, starting transfers between devices, body(): lax.all_to_all(tagged, 'uly', 0, 0, tiled=True).reshape(-1, width + HEAD)  6.79 us
  transfers between devices with their start and end apart: 10, of which 5 were waited for; matrix products, arithmetic and copies ran while one was open for 2% of the time, Pallas kernels for 6%

profile of v3, /device:TPU:1, one launch (start us, length us, event | category | flops | bytes accessed | tf_op | source)
XLA Modules:
  0.0 140.8 jit_solution(6027455074368331333)
XLA Ops:
  7.3 0.9 concatenate.9
  9.0 6.8 %all-to-all-start = ((bf16[8,8,3200]{2,1,0:T(8,128)(2,1)}), bf16[8,8,3200]{2,1,0:T(8,128)(2,1)S(1)}, u32[]{:S(2)}, u32[]{:S(2)}) async-start(bf16[8,8,3200]{2,1,0:T(8,128)(2,1)} %broadcast_in_dim.18), calls=%async_computation | async-start | bytes 819200 | tf_op jit(solution)/shard_map/all_to_all | solution.py:194
  16.2 1.5 %pad_maximum_fusion.w_ref = bf16[3072,256]{1,0:T(8,128)(2,1)S(1)} fusion(bf16[3072,128]{1,0:T(8,128)(2,1)} %param.14, bf16[3072,128]{1,0:T(8,128)(2,1)} %param.13), kind=kLoop, calls=%fused_computation | loop fusion | flops 3145728 | bytes 3145728 | tf_op jit(solution)/shard_map/concatenate | solution.py:203
  17.8 4.9 %all-to-all-done = bf16[8,8,3200]{2,1,0:T(8,128)(2,1)S(1)} async-done(((bf16[8,8,3200]{2,1,0:T(8,128)(2,1)}), bf16[8,8,3200]{2,1,0:T(8,128)(2,1)S(1)}, u32[]{:S(2)}, u32[]{:S(2)}) %all-to-all-start) | async-done | bytes 409632 | tf_op jit(solution)/shard_map/all_to_all | solution.py:194
  22.7 2.2 %kv.1 = (bf16[128,3072]{1,0:T(8,128)(2,1)S(1)}, bf16[8,128,256]{2,1,0:T(8,128)(2,1)}, f32[16,3072]{1,0:T(8,128)S(1)}) custom-call(bf16[64,3200]{1,0:T(8,128)(2,1)S(1)} %bitcast.17, bf16[128,3072]{1,0:T(8,128)(2,1)S(1)} %bitcast.18, f32[1,3072]{1,0:T(1,128)S(1)} %bitcast.19, f32[128,256]{1,0:T(8,128)S(1)} %pad_maximum_fusion.2.table_ref, ...), custom_call_target="tpu_custom_call" | custom-call | tf_op jit(solution)/shard_map/kv/pallas_call | solution.py:206
  24.9 0.9 copy-done.3
  25.8 7.8 %all-to-all-start.1 = ((bf16[8,128,256]{2,1,0:T(8,128)(2,1)}), bf16[8,128,256]{2,1,0:T(8,128)(2,1)S(1)}, u32[]{:S(2)}, u32[]{:S(2)}) async-start(bf16[8,128,256]{2,1,0:T(8,128)(2,1)} %get-tuple-element.16), calls=%async_computation.1 | async-start | bytes 1048576 | tf_op jit(solution)/shard_map/all_to_all | solution.py:231
  33.7 5.8 %collective-permute-start.2 = (bf16[48,384]{1,0:T(8,128)(2,1)S(1)}, bf16[48,384]{1,0:T(8,128)(2,1)S(1)}, u32[]{:S(2)}, u32[]{:S(2)}) collective-permute-start(bf16[48,384]{1,0:T(8,128)(2,1)S(1)} %bitcast.21), channel_id=1, source_target_pairs={{6,0},{0,2},{2,4},{4,6},{7,1},{1,3},{3,5},{5,7},{14,8},{8,10},{10,... | collective-permute-start | bytes 110600 | tf_op jit(solution)/shard_map/ppermute | solution.py:198
  39.5 7.9 %collective-permute-start.1 = (bf16[48,384]{1,0:T(8,128)(2,1)S(1)}, bf16[48,384]{1,0:T(8,128)(2,1)S(1)}, u32[]{:S(2)}, u32[]{:S(2)}) collective-permute-start(bf16[48,384]{1,0:T(8,128)(2,1)S(1)} %bitcast.22), channel_id=1, source_target_pairs={{4,0},{6,2},{0,4},{2,6},{5,1},{7,3},{1,5},{3,7},{12,8},{14,10},{8,... | collective-permute-start | bytes 110600 | tf_op jit(solution)/shard_map/ppermute | solution.py:198
  47.5 3.4 %collective-permute-start = (bf16[48,384]{1,0:T(8,128)(2,1)S(1)}, bf16[48,384]{1,0:T(8,128)(2,1)S(1)}, u32[]{:S(2)}, u32[]{:S(2)}) collective-permute-start(bf16[48,384]{1,0:T(8,128)(2,1)S(1)} %bitcast.23), channel_id=1, source_target_pairs={{2,0},{4,2},{6,4},{0,6},{3,1},{5,3},{7,5},{1,7},{10,8},{12,10},{14... | collective-permute-start | bytes 110600 | tf_op jit(solution)/shard_map/ppermute | solution.py:198
  50.9 1.7 %copy-done = bf16[3072,384]{1,0:T(8,128)(2,1)S(1)} copy-done((bf16[3072,384]{1,0:T(8,128)(2,1)S(1)}, bf16[3072,384]{1,0:T(8,128)(2,1)}, u32[]{:S(2)}) %copy-start) | copy-done | bytes 2359320
  52.5 1.1 copy-done.4
  54.3 1.9 %collective-permute-start.3 = (bf16[384,128]{1,0:T(8,128)(2,1)S(1)}, bf16[384,128]{1,0:T(8,128)(2,1)S(1)}, u32[]{:S(2)}, u32[]{:S(2)}) collective-permute-start(bf16[384,128]{1,0:T(8,128)(2,1)S(1)} %q.1.refs_0_), channel_id=1, source_target_pairs={{2,0},{4,2},{6,4},{0,6},{3,1},{5,3},{7,5},{1,7},{10,8},{12,10},{14... | collective-permute-start | bytes 294920 | tf_op jit(solution)/shard_map/ppermute | solution.py:198
  56.2 6.1 %collective-permute-start.4 = (bf16[384,128]{1,0:T(8,128)(2,1)S(1)}, bf16[384,128]{1,0:T(8,128)(2,1)S(1)}, u32[]{:S(2)}, u32[]{:S(2)}) collective-permute-start(bf16[384,128]{1,0:T(8,128)(2,1)S(1)} %q.1.refs_0_), channel_id=1, source_target_pairs={{4,0},{6,2},{0,4},{2,6},{5,1},{7,3},{1,5},{3,7},{12,8},{14,10},{8,... | collective-permute-start | bytes 294920 | tf_op jit(solution)/shard_map/ppermute | solution.py:198
  62.3 1.9 %collective-permute-start.5 = (bf16[384,128]{1,0:T(8,128)(2,1)S(1)}, bf16[384,128]{1,0:T(8,128)(2,1)S(1)}, u32[]{:S(2)}, u32[]{:S(2)}) collective-permute-start(bf16[384,128]{1,0:T(8,128)(2,1)S(1)} %q.1.refs_0_), channel_id=1, source_target_pairs={{6,0},{0,2},{2,4},{4,6},{7,1},{1,3},{3,5},{5,7},{14,8},{8,10},{10,... | collective-permute-start | bytes 294920 | tf_op jit(solution)/shard_map/ppermute | solution.py:198
  65.6 6.4 %collective-permute-done.5.refs_3_ = bf16[384,128]{1,0:T(8,128)(2,1)S(1)} collective-permute-done((bf16[384,128]{1,0:T(8,128)(2,1)S(1)}, bf16[384,128]{1,0:T(8,128)(2,1)S(1)}, u32[]{:S(2)}, u32[]{:S(2)}) %collective-permute-start.5) | collective-permute-done | bytes 98336 | tf_op jit(solution)/shard_map/ppermute | solution.py:198
  72.1 4.9 %collective-permute-start.6 = (bf16[8,128,256]{2,1,0:T(8,128)(2,1)S(1)}, bf16[8,128,256]{2,1,0:T(8,128)(2,1)S(1)}, u32[]{:S(2)}, u32[]{:S(2)}) collective-permute-start(bf16[8,128,256]{2,1,0:T(8,128)(2,1)S(1)} %all-to-all-done.1.refs_4_), channel_id=1, source_target_pairs={{1,0},{0,1},{3,2},{2,3},{5,4},{4,5},{7,6},{6,7},{9,8},{8,9},{11,10... | collective-permute-start | bytes 1572872 | tf_op jit(solution)/shard_map/ppermute | solution.py:198
  77.0 1.5 %collective-permute-done.6.refs_5_ = bf16[8,128,256]{2,1,0:T(8,128)(2,1)S(1)} collective-permute-done((bf16[8,128,256]{2,1,0:T(8,128)(2,1)S(1)}, bf16[8,128,256]{2,1,0:T(8,128)(2,1)S(1)}, u32[]{:S(2)}, u32[]{:S(2)}) %collective-permute-start.6) | collective-permute-done | bytes 524320 | tf_op jit(solution)/shard_map/ppermute | solution.py:198
  78.5 8.4 %attend.1 = bf16[4,400,128]{2,1,0:T(8,128)(2,1)S(1)} custom-call(bf16[384,128]{1,0:T(8,128)(2,1)S(1)} %q.1.refs_0_, bf16[384,128]{1,0:T(8,128)(2,1)S(1)} %collective-permute-done.3.refs_1_, bf16[384,128]{1,0:T(8,128)(2,1)S(1)} %collective-permute-done.4.refs_2_, bf16[384,128]{1,0:T(8,128)(2,1)S(1)} %collective-permute-done.5.refs_3_, ...), custom_call_target="tpu_custom_call" | custom-call | tf_op jit(solution)/shard_map/attend/pallas_call | solution.py:240
  86.9 15.7 %all_to_all.20.o_ref = bf16[4,400,128]{2,1,0:T(8,128)(2,1)S(1)} all-to-all(bf16[4,400,128]{2,1,0:T(8,128)(2,1)S(1)} %attend.1), channel_id=1, replica_groups=mesh['uly'=8,'blk_y'=8,'blk_z'=4,'blk_c'=2] {'blk_z'}, dimensions={0} | all-to-all | bytes 819200 | tf_op jit(solution)/shard_map/all_to_all | solution.py:253
  102.6 10.1 %all-gather.3.cloned.1.call-done = bf16[64,48,384]{2,1,0:T(8,128)(2,1)} async-done(((bf16[4,48,384]{2,1,0:T(8,128)(2,1)}), bf16[64,48,384]{2,1,0:T(8,128)(2,1)}) %all-gather.3.cloned.1.call-update) | async-done | bytes 2359312 | tf_op jit(solution)/shard_map/all_gather | solution.py:236
  112.6 1.7 %copy-done.1 = bf16[64,48,384]{2,1,0:T(8,128)(2,1)S(1)} copy-done((bf16[64,48,384]{2,1,0:T(8,128)(2,1)S(1)}, bf16[64,48,384]{2,1,0:T(8,128)(2,1)}, u32[]{:S(2)}) %copy-start.1) | copy-done | bytes 2359320
  114.3 1.9 %project.1 = bf16[128,3072]{1,0:T(8,128)(2,1)S(1)} custom-call(bf16[4,400,128]{2,1,0:T(8,128)(2,1)S(1)} %all_to_all.20.o_ref, bf16[8,2,4,48,384]{4,3,2,1,0:T(8,128)(2,1)S(1)} %bitcast.16), custom_call_target="tpu_custom_call" | custom-call | tf_op jit(solution)/shard_map/project/pallas_call | solution.py:255
  116.2 17.0 %all_to_all.21 = bf16[8,16,3072]{2,1,0:T(8,128)(2,1)S(1)} all-to-all(bf16[8,16,3072]{2,1,0:T(8,128)(2,1)S(1)} %bitcast.15), channel_id=1, replica_groups=mesh['uly'=8,'blk_y'=8,'blk_z'=4,'blk_c'=2] {'uly'}, dimensions={0} | all-to-all | bytes 1572864 | tf_op jit(solution)/shard_map/all_to_all | solution.py:269
  (31 shorter events, 4.8 us)
Async XLA Ops:
  9.0 13.7 %copy-start.2 = (bf16[1,128,3072]{2,1,0:T(8,128)(2,1)S(1)}, bf16[1,128,3072]{2,1,0:T(8,128)(2,1)}, u32[]{:S(2)}) copy-start(bf16[1,128,3072]{2,1,0:T(8,128)(2,1)} %param.8) | copy-start | bytes 2359300
  9.0 13.7 %copy-start.5 = (f32[3072]{0:T(1024)S(1)}, f32[3072]{0:T(1024)}, u32[]{:S(2)}) copy-start(f32[3072]{0:T(1024)} %param.11) | copy-start | bytes 36868
  9.0 13.7 %all-to-all-start = ((bf16[8,8,3200]{2,1,0:T(8,128)(2,1)}), bf16[8,8,3200]{2,1,0:T(8,128)(2,1)S(1)}, u32[]{:S(2)}, u32[]{:S(2)}) async-start(bf16[8,8,3200]{2,1,0:T(8,128)(2,1)} %broadcast_in_dim.18), calls=%async_computation | async-start | bytes 819200 | tf_op jit(solution)/shard_map/all_to_all | solution.py:194
  17.8 15.9 %copy-start.6 = (bf16[384,48]{0,1:T(8,128)(2,1)S(1)}, bf16[384,48]{0,1:T(8,128)(2,1)}, u32[]{:S(2)}) copy-start(bf16[384,48]{0,1:T(8,128)(2,1)} %param.15) | copy-start | bytes 110596
  24.9 0.9 copy-start.3
  25.8 46.2 %all-to-all-start.1 = ((bf16[8,128,256]{2,1,0:T(8,128)(2,1)}), bf16[8,128,256]{2,1,0:T(8,128)(2,1)S(1)}, u32[]{:S(2)}, u32[]{:S(2)}) async-start(bf16[8,128,256]{2,1,0:T(8,128)(2,1)} %get-tuple-element.16), calls=%async_computation.1 | async-start | bytes 1048576 | tf_op jit(solution)/shard_map/all_to_all | solution.py:231
  33.7 79.0 %all-gather.3.cloned.1.call-start = ((), (), s32[]{:S(2)}) async-start(), calls=%async_computation.4 | async-start | bytes 2506752 | tf_op jit(solution)/shard_map/all_gather | solution.py:236
  33.7 28.6 %collective-permute-start.2 = (bf16[48,384]{1,0:T(8,128)(2,1)S(1)}, bf16[48,384]{1,0:T(8,128)(2,1)S(1)}, u32[]{:S(2)}, u32[]{:S(2)}) collective-permute-start(bf16[48,384]{1,0:T(8,128)(2,1)S(1)} %bitcast.21), channel_id=1, source_target_pairs={{6,0},{0,2},{2,4},{4,6},{7,1},{1,3},{3,5},{5,7},{14,8},{8,10},{10,... | collective-permute-start | bytes 110600 | tf_op jit(solution)/shard_map/ppermute | solution.py:198
  39.5 24.8 %collective-permute-start.1 = (bf16[48,384]{1,0:T(8,128)(2,1)S(1)}, bf16[48,384]{1,0:T(8,128)(2,1)S(1)}, u32[]{:S(2)}, u32[]{:S(2)}) collective-permute-start(bf16[48,384]{1,0:T(8,128)(2,1)S(1)} %bitcast.22), channel_id=1, source_target_pairs={{4,0},{6,2},{0,4},{2,6},{5,1},{7,3},{1,5},{3,7},{12,8},{14,10},{8,... | collective-permute-start | bytes 110600 | tf_op jit(solution)/shard_map/ppermute | solution.py:198
  47.5 16.8 %collective-permute-start = (bf16[48,384]{1,0:T(8,128)(2,1)S(1)}, bf16[48,384]{1,0:T(8,128)(2,1)S(1)}, u32[]{:S(2)}, u32[]{:S(2)}) collective-permute-start(bf16[48,384]{1,0:T(8,128)(2,1)S(1)} %bitcast.23), channel_id=1, source_target_pairs={{2,0},{4,2},{6,4},{0,6},{3,1},{5,3},{7,5},{1,7},{10,8},{12,10},{14... | collective-permute-start | bytes 110600 | tf_op jit(solution)/shard_map/ppermute | solution.py:198
  50.9 1.7 %copy-start = (bf16[3072,384]{1,0:T(8,128)(2,1)S(1)}, bf16[3072,384]{1,0:T(8,128)(2,1)}, u32[]{:S(2)}) copy-start(bf16[3072,384]{1,0:T(8,128)(2,1)} %w_ref.1) | copy-start | bytes 7077892
  52.5 1.1 copy-start.4
  54.3 10.7 %collective-permute-start.3 = (bf16[384,128]{1,0:T(8,128)(2,1)S(1)}, bf16[384,128]{1,0:T(8,128)(2,1)S(1)}, u32[]{:S(2)}, u32[]{:S(2)}) collective-permute-start(bf16[384,128]{1,0:T(8,128)(2,1)S(1)} %q.1.refs_0_), channel_id=1, source_target_pairs={{2,0},{4,2},{6,4},{0,6},{3,1},{5,3},{7,5},{1,7},{10,8},{12,10},{14... | collective-permute-start | bytes 294920 | tf_op jit(solution)/shard_map/ppermute | solution.py:198
  56.2 9.4 %collective-permute-start.4 = (bf16[384,128]{1,0:T(8,128)(2,1)S(1)}, bf16[384,128]{1,0:T(8,128)(2,1)S(1)}, u32[]{:S(2)}, u32[]{:S(2)}) collective-permute-start(bf16[384,128]{1,0:T(8,128)(2,1)S(1)} %q.1.refs_0_), channel_id=1, source_target_pairs={{4,0},{6,2},{0,4},{2,6},{5,1},{7,3},{1,5},{3,7},{12,8},{14,10},{8,... | collective-permute-start | bytes 294920 | tf_op jit(solution)/shard_map/ppermute | solution.py:198
  62.3 9.7 %collective-permute-start.5 = (bf16[384,128]{1,0:T(8,128)(2,1)S(1)}, bf16[384,128]{1,0:T(8,128)(2,1)S(1)}, u32[]{:S(2)}, u32[]{:S(2)}) collective-permute-start(bf16[384,128]{1,0:T(8,128)(2,1)S(1)} %q.1.refs_0_), channel_id=1, source_target_pairs={{6,0},{0,2},{2,4},{4,6},{7,1},{1,3},{3,5},{5,7},{14,8},{8,10},{10,... | collective-permute-start | bytes 294920 | tf_op jit(solution)/shard_map/ppermute | solution.py:198
  72.1 6.4 %collective-permute-start.6 = (bf16[8,128,256]{2,1,0:T(8,128)(2,1)S(1)}, bf16[8,128,256]{2,1,0:T(8,128)(2,1)S(1)}, u32[]{:S(2)}, u32[]{:S(2)}) collective-permute-start(bf16[8,128,256]{2,1,0:T(8,128)(2,1)S(1)} %all-to-all-done.1.refs_4_), channel_id=1, source_target_pairs={{1,0},{0,1},{3,2},{2,3},{5,4},{4,5},{7,6},{6,7},{9,8},{8,9},{11,10... | collective-permute-start | bytes 1572872 | tf_op jit(solution)/shard_map/ppermute | solution.py:198
  112.6 1.7 %copy-start.1 = (bf16[64,48,384]{2,1,0:T(8,128)(2,1)S(1)}, bf16[64,48,384]{2,1,0:T(8,128)(2,1)}, u32[]{:S(2)}) copy-start(bf16[64,48,384]{2,1,0:T(8,128)(2,1)} %all-gather.3.cloned.1.call-done) | copy-start | bytes 7077892
Sparse Core Ops, SparseCore 0:
  72.2 40.3 all-gather.2

commit v4 on v3

--- a/solution.py
+++ b/solution.py
@@ -13,6 +13,7 @@
 BLK = ("blk_y", "blk_z", "blk_c")
 NEG = -(2.0**127)
 CHUNK = 4
+W_REPEATS = 4
 EXP2_SCALE = math.log2(math.e) / math.sqrt(HEAD)
 STAT_ROWS = 16
 F32 = jnp.float32
@@ -67,8 +68,9 @@
     length = normed_ref.shape[0]
     queries = jnp.dot(normed_ref[...], w_ref[...], preferred_element_type=F32)
     for h in range(w_ref.shape[1] // HEAD):
-        part = rope(queries[:, h * HEAD : (h + 1) * HEAD], table_ref)
-        q_ref[h * length : (h + 1) * length, :] = part.astype(BF16)
+        part = rope(queries[:, h * HEAD : (h + 1) * HEAD], table_ref).astype(BF16)
+        for i in range(q_ref.shape[0]):
+            q_ref[i, h * length : (h + 1) * length, :] = part
 
 
 def in_pieces(values, count):
@@ -79,25 +81,19 @@
     return pieces
 
 
-def attend_kernel(*refs):
-    n_z = len(refs) - 5
-    q_refs = refs[:n_z]
-    near_ref, far_ref, o_ref, s_ref, all_q_ref = refs[n_z:]
+def attend_kernel(q_ref, near_ref, far_ref, o_ref, s_ref):
     y, z, c = (lax.axis_index(a) for a in BLK)
     n_y, length = near_ref.shape[:2]
-    rows = q_refs[0].shape[0]
+    n_z, rows = q_ref.shape[:2]
     heads = rows // length
-    for d in range(n_z):
-        all_q_ref[d] = q_refs[d][...]
     chunks = [(ref, i) for ref in (near_ref, far_ref) for i in range(0, n_y, CHUNK)]
     wide = CHUNK * length
 
     def folded(s, op):
         return functools.reduce(op, [s[:, i : i + HEAD] for i in range(0, s.shape[1], HEAD)])
 
-    def one_block(d, _):
-        zq = lax.rem(z + d, n_z)
-        queries = all_q_ref[d]
+    def one_block(zq, _):
+        queries = q_ref[zq]
         column = lax.broadcasted_iota(jnp.int32, (length, HEAD), 1)
         ahead = column - lax.broadcasted_iota(jnp.int32, (length, HEAD), 0)
         ahead = jnp.concatenate([ahead] * heads, axis=0)
@@ -165,11 +161,9 @@
             )
             attended_ref[:, h * HEAD : (h + 1) * HEAD] = mixed.astype(BF16)
 
-    z = lax.axis_index(BLK[1])
     many, n_c, n_z = w_ref.shape[:3]
     w = jnp.concatenate(
-        [w_ref[i, c, lax.rem(zz - z + n_z, n_z)] for i in range(many) for zz in range(n_z) for c in range(n_c)],
-        axis=0,
+        [w_ref[i, c, z] for i in range(many) for z in range(n_z) for c in range(n_c)], axis=0
     )
     out_ref[...] = nt_dot(attended_ref[...], w).astype(BF16)
 
@@ -186,16 +180,20 @@
     q_width = w_query.shape[1]
     heads = q_width // HEAD
     y, z, c = (lax.axis_index(a) for a in BLK)
-    slot_column = image_slots.reshape(-1, 1).astype(BF16)
-    ones = jnp.ones_like(slot_column)
-    pad = jnp.zeros((slot_column.shape[0], HEAD - 2), BF16)
-    tagged = jnp.concatenate([image_rows[0, 0], slot_column, ones, pad], axis=1)
-    tagged = jnp.broadcast_to(tagged[None], (n_uly, *tagged.shape))
-    images = lax.all_to_all(tagged, "uly", 0, 0, tiled=True).reshape(-1, width + HEAD)
-
-    def from_next(array, axis, d):
-        n = lax.axis_size(axis)
-        return lax.ppermute(array, axis, [((i + d) % n, i) for i in range(n)])
+    w_turned = w_out.T
+    repeated = lax.optimization_barrier(jnp.broadcast_to(w_turned[None], (W_REPEATS, *w_turned.shape)))
+    w_near = lax.all_gather(repeated, BLK[1:], axis=0, tiled=False).reshape(n_z, n_c, W_REPEATS, *w_turned.shape)
+    w_near = lax.dynamic_slice(
+        w_near, (0, c, 0, 0, 0), (n_z, 1, 1, *w_turned.shape)
+    ).reshape(n_z, *w_turned.shape)
+
+    slots = image_slots.reshape(-1, 1).astype(BF16)
+    tagged = jnp.pad(image_rows[0, 0], ((0, 0), (0, HEAD)))
+    lane = lax.broadcasted_iota(jnp.int32, tagged.shape, 1)
+    tagged = jnp.where(lane == width, slots, jnp.where(lane == width + 1, jnp.ones_like(slots), tagged))
+    images = lax.all_to_all(
+        jnp.broadcast_to(tagged[None], (n_uly, *tagged.shape)), "uly", 0, 0, tiled=True
+    ).reshape(-1, width + HEAD)
 
     block = (y * n_z + z) * n_c + c
     cosine, sine = rope_tables(block * block_len + jnp.arange(block_len, dtype=jnp.int32))
@@ -218,7 +216,7 @@
     )(images, prompt[0], norm_gain[None], table, w_kv)
     queries = pl.pallas_call(
         q_kernel,
-        out_shape=jax.ShapeDtypeStruct((rows, HEAD), BF16),
+        out_shape=jax.ShapeDtypeStruct((n_z, rows, HEAD), BF16),
         in_specs=[vmem] * 3,
         out_specs=vmem,
         compiler_params=pltpu.CompilerParams(vmem_limit_bytes=24 << 20),
@@ -229,26 +227,21 @@
     )(normed, table, w_query)
 
     near = lax.all_to_all(key_value, BLK[0], 0, 0, tiled=True)
-    asked = [queries] + [from_next(queries, BLK[1], d) for d in range(1, n_z)]
-    _, w_turned = lax.optimization_barrier((key_value, w_out.T))
-    w_near = jnp.stack([w_turned] + [from_next(w_turned, BLK[1], d) for d in range(1, n_z)])
-    near, w_near, *asked = lax.optimization_barrier((near, w_near, *asked))
+    near, queries = lax.optimization_barrier((near, queries))
     w_all = lax.all_gather(w_near, (BLK[0], BLK[2]), axis=0, tiled=False)
     w_all = w_all.reshape(n_y, n_c, n_z, *w_near.shape[1:])
-    far = from_next(near, BLK[2], 1)
+    asked = lax.all_to_all(queries, BLK[1], 0, 0, tiled=True)
+    far = lax.ppermute(near, BLK[2], [((i + 1) % n_c, i) for i in range(n_c)])
 
     partial = pl.pallas_call(
         attend_kernel,
         out_shape=jax.ShapeDtypeStruct((n_z, rows + STAT_ROWS, HEAD), BF16),
-        in_specs=[vmem] * (n_z + 2),
+        in_specs=[vmem] * 3,
         out_specs=vmem,
-        scratch_shapes=[
-            pltpu.VMEM((n_c * n_y // CHUNK, rows, CHUNK * block_len), F32),
-            pltpu.VMEM((n_z, rows, HEAD), BF16),
-        ],
+        scratch_shapes=[pltpu.VMEM((n_c * n_y // CHUNK, rows, CHUNK * block_len), F32)],
         compiler_params=pltpu.CompilerParams(vmem_limit_bytes=24 << 20),
         name="attend",
-    )(*asked, near, far)
+    )(asked, near, far)
 
     parts = lax.all_to_all(partial, BLK[1], 0, 0, tiled=True)
     piece = w_out.shape[1]

time: 142 us -> 163 us (1.15)
  the two profiles are of different devices: /device:TPU:1 before, /device:TPU:48 now
where the time goes in v4:
time: 163 us; the launch traced here: 162 us
  waiting for transfers between devices  72 us (44%)
  blocking collectives  31.5 us (19%)
  starting transfers between devices  19.2 us (12%)
  Pallas kernels  13.7 us (8%)
  between operations  13.5 us (8%)
  local copies, waits for them, and re-layouts  8.38 us (5%)
  other arithmetic  4.07 us (2%)
    all_gather x1, waiting for transfers between devices, body(): lax.all_gather(repeated, BLK[1:], axis=0, tiled=False)  39.7 us
    all_to_all x1, blocking collectives, body(): parts = lax.all_to_all(partial, BLK[1], 0, 0, tiled=True)  16.1 us
    all_to_all x1, blocking collectives, body(): lax.all_to_all(projected.reshape(n_uly, own_len, width), 'uly', 0, 0, til...  15.4 us
    all_to_all x1, waiting for transfers between devices, body(): near = lax.all_to_all(key_value, BLK[0], 0, 0, tiled=True)  14.1 us
    all_to_all x1, waiting for transfers between devices, body(): asked = lax.all_to_all(queries, BLK[1], 0, 0, tiled=True)  8.74 us
    pallas_call x1, Pallas kernels, body(): pl.pallas_call(attend_kernel, out_shape=jax.ShapeDtypeStruct((n_z, rows +...  8.34 us
    all_to_all x1, waiting for transfers between devices, body(): lax.all_to_all(jnp.broadcast_to(tagged[None], (n_uly, *tagged.shape)), 'u...  7.45 us
    all_to_all x1, starting transfers between devices, body(): near = lax.all_to_all(key_value, BLK[0], 0, 0, tiled=True)  7.16 us
  transfers between devices with their start and end apart: 6, of which 5 were waited for; matrix products, arithmetic and copies ran while one was open for 3% of the time, Pallas kernels for 7%

profile of v4, /device:TPU:48, one launch (start us, length us, event | category | flops | bytes accessed | tf_op | source)
XLA Modules:
  0.0 162.4 jit_solution(8285517947816953380)
XLA Ops:
  6.5 1.5 broadcast_in_dim.37
  8.1 39.7 %all-gather.5.cloned.1.call-done = bf16[32,48,384]{2,1,0:T(8,128)(2,1)} async-done(((bf16[4,48,384]{2,1,0:T(8,128)(2,1)}), bf16[32,48,384]{2,1,0:T(8,128)(2,1)}) %all-gather.5.cloned.1.call-update) | async-done | bytes 1179664 | tf_op jit(solution)/shard_map/all_gather | solution.py:185
  47.9 1.6 constant_dynamic-slice_fusion
  50.1 0.9 select_select_fusion
  51.0 0.8 broadcast_in_dim.35
  51.8 4.3 %all-to-all-start = ((bf16[8,8,3200]{2,1,0:T(8,128)(2,1)}), bf16[8,8,3200]{2,1,0:T(8,128)(2,1)S(1)}, u32[]{:S(2)}, u32[]{:S(2)}) async-start(bf16[8,8,3200]{2,1,0:T(8,128)(2,1)} %broadcast_in_dim.35), calls=%async_computation | async-start | bytes 819200 | tf_op jit(solution)/shard_map/all_to_all | solution.py:194
  56.5 1.3 pad_maximum_fusion.w_ref
  57.9 7.5 %all-to-all-done = bf16[8,8,3200]{2,1,0:T(8,128)(2,1)S(1)} async-done(((bf16[8,8,3200]{2,1,0:T(8,128)(2,1)}), bf16[8,8,3200]{2,1,0:T(8,128)(2,1)S(1)}, u32[]{:S(2)}, u32[]{:S(2)}) %all-to-all-start) | async-done | bytes 409632 | tf_op jit(solution)/shard_map/all_to_all | solution.py:194
  65.3 1.1 copy-done.2
  66.5 2.2 %kv.1 = (bf16[128,3072]{1,0:T(8,128)(2,1)S(1)}, bf16[8,128,256]{2,1,0:T(8,128)(2,1)}, f32[16,3072]{1,0:T(8,128)S(1)}) custom-call(bf16[64,3200]{1,0:T(8,128)(2,1)S(1)} %bitcast.14, bf16[128,3072]{1,0:T(8,128)(2,1)S(1)} %bitcast.15, f32[1,3072]{1,0:T(1,128)S(1)} %bitcast.16, f32[128,256]{1,0:T(8,128)S(1)} %pad_maximum_fusion.1.table_ref, ...), custom_call_target="tpu_custom_call" | custom-call | tf_op jit(solution)/shard_map/kv/pallas_call | solution.py:204
  68.7 7.2 %all-to-all-start.1 = ((bf16[8,128,256]{2,1,0:T(8,128)(2,1)}), bf16[8,128,256]{2,1,0:T(8,128)(2,1)S(1)}, u32[]{:S(2)}, u32[]{:S(2)}) async-start(bf16[8,128,256]{2,1,0:T(8,128)(2,1)} %get-tuple-element.11), calls=%async_computation.1 | async-start | bytes 1048576 | tf_op jit(solution)/shard_map/all_to_all | solution.py:229
  75.8 1.7 %copy-done = bf16[3072,384]{1,0:T(8,128)(2,1)S(1)} copy-done((bf16[3072,384]{1,0:T(8,128)(2,1)S(1)}, bf16[3072,384]{1,0:T(8,128)(2,1)}, u32[]{:S(2)}) %copy-start) | copy-done | bytes 2359320
  77.5 1.4 q.1
  78.9 14.1 %all-to-all-done.1.near_ref = bf16[8,128,256]{2,1,0:T(8,128)(2,1)S(1)} async-done(((bf16[8,128,256]{2,1,0:T(8,128)(2,1)}), bf16[8,128,256]{2,1,0:T(8,128)(2,1)S(1)}, u32[]{:S(2)}, u32[]{:S(2)}) %all-to-all-start.1) | async-done | bytes 524320 | tf_op jit(solution)/shard_map/all_to_all | solution.py:229
  93.1 5.8 %all-to-all-start.2 = ((bf16[4,384,128]{2,1,0:T(8,128)(2,1)}), bf16[4,384,128]{2,1,0:T(8,128)(2,1)S(1)}, u32[]{:S(2)}, u32[]{:S(2)}) async-start(bf16[4,384,128]{2,1,0:T(8,128)(2,1)} %q.1), calls=%async_computation.2 | async-start | bytes 786432 | tf_op jit(solution)/shard_map/all_to_all | solution.py:233
  98.9 1.9 %collective-permute-start = (bf16[8,128,256]{2,1,0:T(8,128)(2,1)S(1)}, bf16[8,128,256]{2,1,0:T(8,128)(2,1)S(1)}, u32[]{:S(2)}, u32[]{:S(2)}) collective-permute-start(bf16[8,128,256]{2,1,0:T(8,128)(2,1)S(1)} %all-to-all-done.1.near_ref), channel_id=1, source_target_pairs={{1,0},{0,1},{3,2},{2,3},{5,4},{4,5},{7,6},{6,7},{9,8},{8,9},{11,10... | collective-permute-start | bytes 1572872 | tf_op jit(solution)/shard_map/ppermute | solution.py:234
  100.8 1.9 %collective-permute-done.far_ref = bf16[8,128,256]{2,1,0:T(8,128)(2,1)S(1)} collective-permute-done((bf16[8,128,256]{2,1,0:T(8,128)(2,1)S(1)}, bf16[8,128,256]{2,1,0:T(8,128)(2,1)S(1)}, u32[]{:S(2)}, u32[]{:S(2)}) %collective-permute-start) | collective-permute-done | bytes 524320 | tf_op jit(solution)/shard_map/ppermute | solution.py:234
  102.6 8.7 %all-to-all-done.2.q_ref = bf16[4,384,128]{2,1,0:T(8,128)(2,1)S(1)} async-done(((bf16[4,384,128]{2,1,0:T(8,128)(2,1)}), bf16[4,384,128]{2,1,0:T(8,128)(2,1)S(1)}, u32[]{:S(2)}, u32[]{:S(2)}) %all-to-all-start.2) | async-done | bytes 393248 | tf_op jit(solution)/shard_map/all_to_all | solution.py:233
  111.4 8.3 %attend.1 = bf16[4,400,128]{2,1,0:T(8,128)(2,1)S(1)} custom-call(bf16[4,384,128]{2,1,0:T(8,128)(2,1)S(1)} %all-to-all-done.2.q_ref, bf16[8,128,256]{2,1,0:T(8,128)(2,1)S(1)} %all-to-all-done.1.near_ref, bf16[8,128,256]{2,1,0:T(8,128)(2,1)S(1)} %collective-permute-done.far_ref), custom_call_target="tpu_custom_call" | custom-call | tf_op jit(solution)/shard_map/attend/pallas_call | solution.py:236
  119.7 16.1 %all_to_all.25.o_ref = bf16[4,400,128]{2,1,0:T(8,128)(2,1)S(1)} all-to-all(bf16[4,400,128]{2,1,0:T(8,128)(2,1)S(1)} %attend.1), channel_id=1, replica_groups=mesh['uly'=8,'blk_y'=8,'blk_z'=4,'blk_c'=2] {'blk_z'}, dimensions={0} | all-to-all | bytes 819200 | tf_op jit(solution)/shard_map/all_to_all | solution.py:246
  135.8 1.7 %copy-done.1 = bf16[64,1,1,48,384]{4,3,2,1,0:T(8,128)(2,1)S(1)} copy-done((bf16[64,1,1,48,384]{4,3,2,1,0:T(8,128)(2,1)S(1)}, bf16[64,1,1,48,384]{4,3,2,1,0:T(8,128)(2,1)}, u32[]{:S(2)}) %copy-start.1) | copy-done | bytes 2359320
  137.5 1.8 %project.1 = bf16[128,3072]{1,0:T(8,128)(2,1)S(1)} custom-call(bf16[4,400,128]{2,1,0:T(8,128)(2,1)S(1)} %all_to_all.25.o_ref, bf16[8,2,4,48,384]{4,3,2,1,0:T(8,128)(2,1)S(1)} %bitcast.13), custom_call_target="tpu_custom_call" | custom-call | tf_op jit(solution)/shard_map/project/pallas_call | solution.py:248
  139.3 15.4 %all_to_all.26 = bf16[8,16,3072]{2,1,0:T(8,128)(2,1)S(1)} all-to-all(bf16[8,16,3072]{2,1,0:T(8,128)(2,1)S(1)} %bitcast.12), channel_id=1, replica_groups=mesh['uly'=8,'blk_y'=8,'blk_z'=4,'blk_c'=2] {'uly'}, dimensions={0} | all-to-all | bytes 1572864 | tf_op jit(solution)/shard_map/all_to_all | solution.py:262
  154.9 0.7 fusion
  (19 shorter events, 1.3 us)
Async XLA Ops:
  6.5 50.0 %copy-start.4 = (bf16[3072,128]{1,0:T(8,128)(2,1)S(1)}, bf16[3072,128]{1,0:T(8,128)(2,1)}, u32[]{:S(2)}) copy-start(bf16[3072,128]{1,0:T(8,128)(2,1)} %param.14) | copy-start | bytes 2359300
  6.5 41.3 %all-gather.5.cloned.1.call-start = ((), (), s32[]{:S(2)}) async-start(), calls=%async_computation.5 | async-start | bytes 1327104 | tf_op jit(solution)/shard_map/all_gather | solution.py:185
  8.1 127.8 %all-gather.7.cloned.1.call-start = ((), (), s32[]{:S(2)}) async-start(), calls=%async_computation.6 | async-start | bytes 2506752 | tf_op jit(solution)/shard_map/all_gather | solution.py:231
  51.8 13.5 %all-to-all-start = ((bf16[8,8,3200]{2,1,0:T(8,128)(2,1)}), bf16[8,8,3200]{2,1,0:T(8,128)(2,1)S(1)}, u32[]{:S(2)}, u32[]{:S(2)}) async-start(bf16[8,8,3200]{2,1,0:T(8,128)(2,1)} %broadcast_in_dim.35), calls=%async_computation | async-start | bytes 819200 | tf_op jit(solution)/shard_map/all_to_all | solution.py:194
  56.5 8.8 %copy-start.3 = (f32[3072]{0:T(1024)S(1)}, f32[3072]{0:T(1024)}, u32[]{:S(2)}) copy-start(f32[3072]{0:T(1024)} %param.11) | copy-start | bytes 36868
  65.3 1.1 copy-start.2
  68.7 24.4 %all-to-all-start.1 = ((bf16[8,128,256]{2,1,0:T(8,128)(2,1)}), bf16[8,128,256]{2,1,0:T(8,128)(2,1)S(1)}, u32[]{:S(2)}, u32[]{:S(2)}) async-start(bf16[8,128,256]{2,1,0:T(8,128)(2,1)} %get-tuple-element.11), calls=%async_computation.1 | async-start | bytes 1048576 | tf_op jit(solution)/shard_map/all_to_all | solution.py:229
  75.8 1.7 %copy-start = (bf16[3072,384]{1,0:T(8,128)(2,1)S(1)}, bf16[3072,384]{1,0:T(8,128)(2,1)}, u32[]{:S(2)}) copy-start(bf16[3072,384]{1,0:T(8,128)(2,1)} %w_ref.1) | copy-start | bytes 7077892
  93.1 18.3 %all-to-all-start.2 = ((bf16[4,384,128]{2,1,0:T(8,128)(2,1)}), bf16[4,384,128]{2,1,0:T(8,128)(2,1)S(1)}, u32[]{:S(2)}, u32[]{:S(2)}) async-start(bf16[4,384,128]{2,1,0:T(8,128)(2,1)} %q.1), calls=%async_computation.2 | async-start | bytes 786432 | tf_op jit(solution)/shard_map/all_to_all | solution.py:233
  98.9 3.8 %collective-permute-start = (bf16[8,128,256]{2,1,0:T(8,128)(2,1)S(1)}, bf16[8,128,256]{2,1,0:T(8,128)(2,1)S(1)}, u32[]{:S(2)}, u32[]{:S(2)}) collective-permute-start(bf16[8,128,256]{2,1,0:T(8,128)(2,1)S(1)} %all-to-all-done.1.near_ref), channel_id=1, source_target_pairs={{1,0},{0,1},{3,2},{2,3},{5,4},{4,5},{7,6},{6,7},{9,8},{8,9},{11,10... | collective-permute-start | bytes 1572872 | tf_op jit(solution)/shard_map/ppermute | solution.py:234
  135.8 1.7 %copy-start.1 = (bf16[64,1,1,48,384]{4,3,2,1,0:T(8,128)(2,1)S(1)}, bf16[64,1,1,48,384]{4,3,2,1,0:T(8,128)(2,1)}, u32[]{:S(2)}) copy-start(bf16[64,1,1,48,384]{4,3,2,1,0:T(8,128)(2,1)} %all-gather.7.cloned.1.call-done) | copy-start | bytes 7077892
Sparse Core Ops, SparseCore 0:
  9.5 38.3 all-gather.4
  50.0 43.5 all-gather.6

commit v5 on v4

--- a/solution.py
+++ b/solution.py
@@ -12,7 +12,8 @@
 HEAD = 128
 BLK = ("blk_y", "blk_z", "blk_c")
 NEG = -(2.0**127)
-CHUNK = 4
+CHUNK = 2
+HIDE = 3.0e38
 W_REPEATS = 4
 EXP2_SCALE = math.log2(math.e) / math.sqrt(HEAD)
 STAT_ROWS = 16
@@ -57,8 +58,8 @@
     first = pl.multiple_of(lax.axis_index("uly") * own_len, own_len)
     own_ref[...] = placed_ref[pl.ds(first, own_len), :]
     joined = jnp.dot(normed, w_ref[...], preferred_element_type=F32)
-    keys = rope(joined[:, :HEAD], table_ref).T.astype(BF16)
-    values = joined[:, HEAD:].astype(BF16)
+    keys = rope(joined[:, :HEAD], table_ref).astype(BF16)
+    values = joined[:, HEAD:].T.astype(BF16)
     for i in range(kv_ref.shape[0]):
         kv_ref[i, :, :HEAD] = keys
         kv_ref[i, :, HEAD:] = values
@@ -68,9 +69,9 @@
     length = normed_ref.shape[0]
     queries = jnp.dot(normed_ref[...], w_ref[...], preferred_element_type=F32)
     for h in range(w_ref.shape[1] // HEAD):
-        part = rope(queries[:, h * HEAD : (h + 1) * HEAD], table_ref).astype(BF16)
+        part = rope(queries[:, h * HEAD : (h + 1) * HEAD], table_ref).T.astype(BF16)
         for i in range(q_ref.shape[0]):
-            q_ref[i, h * length : (h + 1) * length, :] = part
+            q_ref[i, :, h * length : (h + 1) * length] = part
 
 
 def in_pieces(values, count):
@@ -84,50 +85,60 @@
 def attend_kernel(q_ref, near_ref, far_ref, o_ref, s_ref):
     y, z, c = (lax.axis_index(a) for a in BLK)
     n_y, length = near_ref.shape[:2]
-    n_z, rows = q_ref.shape[:2]
+    n_z, _, rows = q_ref.shape
     heads = rows // length
-    chunks = [(ref, i) for ref in (near_ref, far_ref) for i in range(0, n_y, CHUNK)]
+    refs = (near_ref, far_ref)
+    blocks = [(core, i) for core in range(len(refs)) for i in range(n_y)]
     wide = CHUNK * length
 
     def folded(s, op):
-        return functools.reduce(op, [s[:, i : i + HEAD] for i in range(0, s.shape[1], HEAD)])
+        return op(s.reshape(-1, 8, rows), axis=0)
 
     def one_block(zq, _):
         queries = q_ref[zq]
-        column = lax.broadcasted_iota(jnp.int32, (length, HEAD), 1)
-        ahead = column - lax.broadcasted_iota(jnp.int32, (length, HEAD), 0)
-        ahead = jnp.concatenate([ahead] * heads, axis=0)
-        best = jnp.full((rows, HEAD), NEG, F32)
-        for k, (ref, i) in enumerate(chunks):
-            keys = jnp.concatenate([ref[i + j, :, :HEAD] for j in range(CHUNK)], axis=1)
-            s = jnp.dot(queries, keys, preferred_element_type=F32)
-            core = jnp.int32(0) if ref is near_ref else 2 * c - 1
-            for j in range(CHUNK):
-                room = ((2 * n_z) * (y - i - j) + 2 * (zq - z) + core) * length
-                part = jnp.where(ahead <= room, s[:, j * length : (j + 1) * length], NEG)
-                s_ref[k, :, j * length : (j + 1) * length] = part
-                best = jnp.maximum(best, part)
-        top = jnp.max(best, axis=1, keepdims=True)
+        best = jnp.full((8, rows), NEG, F32)
+        for core, ref in enumerate(refs):
+            for i in range(0, n_y, CHUNK):
+                keys = ref[i : i + CHUNK, :, :HEAD].reshape(wide, HEAD)
+                s = jnp.dot(keys, queries, preferred_element_type=F32)
+                for j in range(CHUNK):
+                    part = s[j * length : (j + 1) * length]
+                    s_ref[core, i + j] = part
+                    hidden = jnp.where(i + j < y, 0.0, NEG)
+                    best = jnp.maximum(best, folded(part, jnp.max) + hidden)
+        ahead = lax.broadcasted_iota(jnp.int32, (length, length), 0)
+        ahead = ahead - lax.broadcasted_iota(jnp.int32, (length, length), 1)
+        ahead = jnp.concatenate([ahead] * heads, axis=1)
+        for core in range(len(refs)):
+            room = (2 * (zq - z) + core * (2 * c - 1)) * length
+            part = jnp.where(ahead <= room, s_ref[core, y], NEG)
+            s_ref[core, y] = part
+            best = jnp.maximum(best, folded(part, jnp.max))
+        top = jnp.max(best, axis=0, keepdims=True)
         shift = top * EXP2_SCALE
-        total = jnp.zeros((rows, HEAD), F32)
-        mixed = jnp.zeros((rows, HEAD), F32)
-        for k, (ref, i) in enumerate(chunks):
-            weights = jnp.exp2(s_ref[k] * EXP2_SCALE - shift)
-            total = total + folded(weights, jnp.add)
-            values = ref[i : i + CHUNK, :, HEAD:].reshape(wide, HEAD)
-            mixed = mixed + jnp.dot(weights.astype(BF16), values, preferred_element_type=F32)
-        total = jnp.sum(total, axis=1, keepdims=True)
-        tile = jnp.zeros((length, HEAD), F32)
+        total = jnp.zeros((8, rows), F32)
+        mixed = jnp.zeros((HEAD, rows), F32)
+        for core, ref in enumerate(refs):
+            for i in range(0, n_y, CHUNK):
+                weights = []
+                for j in range(CHUNK):
+                    hidden = jnp.where(i + j <= y, 0.0, HIDE)
+                    part = jnp.exp2(s_ref[core, i + j] * EXP2_SCALE - (shift + hidden))
+                    total = total + folded(part, jnp.sum)
+                    weights.append(part.astype(BF16))
+                values = jnp.concatenate([ref[i + j, :, HEAD:] for j in range(CHUNK)], axis=1)
+                mixed = mixed + jnp.dot(
+                    values, jnp.concatenate(weights, axis=0), preferred_element_type=F32
+                )
+        total = jnp.sum(total, axis=0, keepdims=True)
+        mixed = (mixed * (1.0 / total)).astype(BF16)
+        pieces = [*in_pieces(top, 3), *in_pieces(total, 2)]
+        across = [slice(h * length, (h + 1) * length) for h in range(heads)]
         for h in range(heads):
-            part = slice(h * length, (h + 1) * length)
-            tile = jnp.where(column == h, top[part], tile)
-            tile = jnp.where(column == heads + h, total[part], tile)
-        stats = tile.T[: 2 * heads]
-        tops, totals = stats[:heads], stats[heads:]
-        pieces = [*in_pieces(tops, 3), *in_pieces(totals, 2)]
-        pieces.append(jnp.zeros((STAT_ROWS - 5 * heads, length), F32))
-        o_ref[zq, :rows, :] = (mixed / total).astype(BF16)
-        o_ref[zq, rows:, :] = jnp.concatenate(pieces, axis=0).astype(BF16)
+            o_ref[zq, h * HEAD : (h + 1) * HEAD, :] = mixed[:, across[h]]
+        stats = [piece[:, across[h]] for piece in pieces for h in range(heads)]
+        stats.append(jnp.zeros((STAT_ROWS - len(stats), length), F32))
+        o_ref[zq, rows:, :] = jnp.concatenate(stats, axis=0).astype(BF16)
         return 0
 
     lax.fori_loop(0, n_z, one_block, 0)
@@ -152,14 +163,12 @@
         grown = [g * t for g, t in zip(grown, totals)]
         whole = sum(grown)
         share = [g / whole for g in grown]
-        tile = jnp.concatenate(share + [jnp.zeros((HEAD - parts * heads, length), F32)], axis=0).T
         for h in range(heads):
-            part = slice(h * length, (h + 1) * length)
+            part = slice(h * HEAD, (h + 1) * HEAD)
             mixed = sum(
-                o_ref[i, part, :].astype(F32) * tile[:, i * heads + h : i * heads + h + 1]
-                for i in range(parts)
+                o_ref[i, part, :].astype(F32) * share[i][h : h + 1] for i in range(parts)
             )
-            attended_ref[:, h * HEAD : (h + 1) * HEAD] = mixed.astype(BF16)
+            attended_ref[:, part] = mixed.T.astype(BF16)
 
     many, n_c, n_z = w_ref.shape[:3]
     w = jnp.concatenate(
@@ -216,7 +225,7 @@
     )(images, prompt[0], norm_gain[None], table, w_kv)
     queries = pl.pallas_call(
         q_kernel,
-        out_shape=jax.ShapeDtypeStruct((n_z, rows, HEAD), BF16),
+        out_shape=jax.ShapeDtypeStruct((n_z, HEAD, rows), BF16),
         in_specs=[vmem] * 3,
         out_specs=vmem,
         compiler_params=pltpu.CompilerParams(vmem_limit_bytes=24 << 20),
@@ -227,7 +236,7 @@
     )(normed, table, w_query)
 
     near = lax.all_to_all(key_value, BLK[0], 0, 0, tiled=True)
-    near, queries = lax.optimization_barrier((near, queries))
+    near, w_near, queries = lax.optimization_barrier((near, w_near, queries))
     w_all = lax.all_gather(w_near, (BLK[0], BLK[2]), axis=0, tiled=False)
     w_all = w_all.reshape(n_y, n_c, n_z, *w_near.shape[1:])
     asked = lax.all_to_all(queries, BLK[1], 0, 0, tiled=True)
@@ -238,7 +247,7 @@
         out_shape=jax.ShapeDtypeStruct((n_z, rows + STAT_ROWS, HEAD), BF16),
         in_specs=[vmem] * 3,
         out_specs=vmem,
-        scratch_shapes=[pltpu.VMEM((n_c * n_y // CHUNK, rows, CHUNK * block_len), F32)],
+        scratch_shapes=[pltpu.VMEM((n_c, n_y, block_len, rows), F32)],
         compiler_params=pltpu.CompilerParams(vmem_limit_bytes=24 << 20),
         name="attend",
     )(asked, near, far)

time: 163 us -> 121 us (0.74)
  the two profiles are of different devices: /device:TPU:48 before, /device:TPU:1 now
where the time goes in v5:
time: 121 us; the launch traced here: 120 us
  blocking collectives  31.5 us (26%)
  starting transfers between devices  28.7 us (24%)
  waiting for transfers between devices  22.7 us (19%)
  between operations  13.5 us (11%)
  Pallas kernels  11.3 us (9%)
  local copies, waits for them, and re-layouts  8.34 us (7%)
  other arithmetic  4.07 us (3%)
    all_to_all x1, blocking collectives, body(): lax.all_to_all(projected.reshape(n_uly, own_len, width), 'uly', 0, 0, til...  17 us
    all_to_all x1, blocking collectives, body(): parts = lax.all_to_all(partial, BLK[1], 0, 0, tiled=True)  14.5 us
    all_gather x1, waiting for transfers between devices, body(): lax.all_gather(repeated, BLK[1:], axis=0, tiled=False)  10.6 us
    all_to_all x1, starting transfers between devices, body(): asked = lax.all_to_all(queries, BLK[1], 0, 0, tiled=True)  9.07 us
    all_to_all x1, starting transfers between devices, body(): near = lax.all_to_all(key_value, BLK[0], 0, 0, tiled=True)  7.84 us
    all_to_all x1, starting transfers between devices, body(): lax.all_to_all(jnp.broadcast_to(tagged[None], (n_uly, *tagged.shape)), 'u...  6.66 us
    pallas_call x1, Pallas kernels, body(): pl.pallas_call(attend_kernel, out_shape=jax.ShapeDtypeStruct((n_z, rows +...  5.97 us
    ppermute x1, starting transfers between devices, body(): far = lax.ppermute(near, BLK[2], [((i + 1) % n_c, i) for i in range(n_c)])  5.13 us
  transfers between devices with their start and end apart: 6, of which 6 were waited for; matrix products, arithmetic and copies ran while one was open for 5% of the time, Pallas kernels for 8%

profile of v5, /device:TPU:1, one launch (start us, length us, event | category | flops | bytes accessed | tf_op | source)
XLA Modules:
  0.0 120.1 jit_solution(397525957765499900)
XLA Ops:
  6.5 1.5 %broadcast_in_dim.37 = bf16[4,48,384]{2,1,0:T(8,128)(2,1)} broadcast(bf16[48,384]{1,0:T(8,128)(2,1)} %bitcast.20), dimensions={1,2} | broadcast | bytes 184320 | tf_op jit(solution)/shard_map/broadcast_in_dim | solution.py:193
  8.7 0.9 select_select_fusion
  9.6 0.8 broadcast_in_dim.35
  10.4 6.7 %all-to-all-start = ((bf16[8,8,3200]{2,1,0:T(8,128)(2,1)}), bf16[8,8,3200]{2,1,0:T(8,128)(2,1)S(1)}, u32[]{:S(2)}, u32[]{:S(2)}) async-start(bf16[8,8,3200]{2,1,0:T(8,128)(2,1)} %broadcast_in_dim.35), calls=%async_computation | async-start | bytes 819200 | tf_op jit(solution)/shard_map/all_to_all | solution.py:203
  17.5 1.3 %pad_maximum_fusion.w_ref = bf16[3072,256]{1,0:T(8,128)(2,1)S(1)} fusion(bf16[3072,128]{1,0:T(8,128)(2,1)S(1)} %copy-done.4, bf16[3072,128]{1,0:T(8,128)(2,1)} %param.13), kind=kLoop, calls=%fused_computation | loop fusion | flops 3145728 | bytes 3145728 | tf_op jit(solution)/shard_map/concatenate | solution.py:210
  18.9 5.1 %all-to-all-done = bf16[8,8,3200]{2,1,0:T(8,128)(2,1)S(1)} async-done(((bf16[8,8,3200]{2,1,0:T(8,128)(2,1)}), bf16[8,8,3200]{2,1,0:T(8,128)(2,1)S(1)}, u32[]{:S(2)}, u32[]{:S(2)}) %all-to-all-start) | async-done | bytes 409632 | tf_op jit(solution)/shard_map/all_to_all | solution.py:203
  24.0 1.1 copy-done.2
  25.1 2.2 %kv.1 = (bf16[128,3072]{1,0:T(8,128)(2,1)S(1)}, bf16[8,128,256]{2,1,0:T(8,128)(2,1)}, f32[16,3072]{1,0:T(8,128)S(1)}) custom-call(bf16[64,3200]{1,0:T(8,128)(2,1)S(1)} %bitcast.16, bf16[128,3072]{1,0:T(8,128)(2,1)S(1)} %bitcast.17, f32[1,3072]{1,0:T(1,128)S(1)} %bitcast.18, f32[128,256]{1,0:T(8,128)S(1)} %pad_maximum_fusion.1.table_ref, ...), custom_call_target="tpu_custom_call" | custom-call | tf_op jit(solution)/shard_map/kv/pallas_call | solution.py:213
  27.3 7.8 %all-to-all-start.1 = ((bf16[8,128,256]{2,1,0:T(8,128)(2,1)}), bf16[8,128,256]{2,1,0:T(8,128)(2,1)S(1)}, u32[]{:S(2)}, u32[]{:S(2)}) async-start(bf16[8,128,256]{2,1,0:T(8,128)(2,1)} %get-tuple-element.12), calls=%async_computation.1 | async-start | bytes 1048576 | tf_op jit(solution)/shard_map/all_to_all | solution.py:238
  35.2 1.7 %copy-done = bf16[3072,384]{1,0:T(8,128)(2,1)S(1)} copy-done((bf16[3072,384]{1,0:T(8,128)(2,1)S(1)}, bf16[3072,384]{1,0:T(8,128)(2,1)}, u32[]{:S(2)}) %copy-start) | copy-done | bytes 2359320
  36.9 1.6 %q.1 = bf16[4,128,384]{2,1,0:T(8,128)(2,1)} custom-call(bf16[128,3072]{1,0:T(8,128)(2,1)S(1)} %get-tuple-element.13.normed_ref, f32[128,256]{1,0:T(8,128)S(1)} %pad_maximum_fusion.1.table_ref, bf16[3072,384]{1,0:T(8,128)(2,1)S(1)} %copy-done), custom_call_target="tpu_custom_call" | custom-call | flops 301989888 | bytes 2359296 | tf_op jit(solution)/shard_map/q/pallas_call | solution.py:226
  38.5 10.6 %all-gather.5.cloned.1.call-done = bf16[32,48,384]{2,1,0:T(8,128)(2,1)} async-done(((bf16[4,48,384]{2,1,0:T(8,128)(2,1)}), bf16[32,48,384]{2,1,0:T(8,128)(2,1)}) %all-gather.5.cloned.1.call-update) | async-done | bytes 1179664 | tf_op jit(solution)/shard_map/all_gather | solution.py:194
  49.1 1.6 %dynamic-slice_bitcast_fusion = bf16[4,48,384]{2,1,0:T(8,128)(2,1)} fusion(bf16[4,2,4,48,384]{4,3,2,1,0:T(8,128)(2,1)} %bitcast.21, s32[]{:T(128)S(6)} %select_n.12), kind=kLoop, calls=%fused_computation.3 | loop fusion | bytes 294916 | tf_op jit(solution)/shard_map/reshape | solution.py:195
  50.8 9.1 %all-to-all-start.2 = ((bf16[4,128,384]{2,1,0:T(8,128)(2,1)}), bf16[4,128,384]{2,1,0:T(8,128)(2,1)S(1)}, u32[]{:S(2)}, u32[]{:S(2)}) async-start(bf16[4,128,384]{2,1,0:T(8,128)(2,1)} %q.1), calls=%async_computation.2 | async-start | bytes 786432 | tf_op jit(solution)/shard_map/all_to_all | solution.py:242
  59.8 5.1 %collective-permute-start = (bf16[8,128,256]{2,1,0:T(8,128)(2,1)S(1)}, bf16[8,128,256]{2,1,0:T(8,128)(2,1)S(1)}, u32[]{:S(2)}, u32[]{:S(2)}) collective-permute-start(bf16[8,128,256]{2,1,0:T(8,128)(2,1)S(1)} %all-to-all-done.1.near_ref), channel_id=1, source_target_pairs={{1,0},{0,1},{3,2},{2,3},{5,4},{4,5},{7,6},{6,7},{9,8},{8,9},{11,10... | collective-permute-start | bytes 1572872 | tf_op jit(solution)/shard_map/ppermute | solution.py:243
  65.0 1.5 %collective-permute-done.far_ref = bf16[8,128,256]{2,1,0:T(8,128)(2,1)S(1)} collective-permute-done((bf16[8,128,256]{2,1,0:T(8,128)(2,1)S(1)}, bf16[8,128,256]{2,1,0:T(8,128)(2,1)S(1)}, u32[]{:S(2)}, u32[]{:S(2)}) %collective-permute-start) | collective-permute-done | bytes 524320 | tf_op jit(solution)/shard_map/ppermute | solution.py:243
  66.5 2.2 %all-to-all-done.2.q_ref = bf16[4,128,384]{2,1,0:T(8,128)(2,1)S(1)} async-done(((bf16[4,128,384]{2,1,0:T(8,128)(2,1)}), bf16[4,128,384]{2,1,0:T(8,128)(2,1)S(1)}, u32[]{:S(2)}, u32[]{:S(2)}) %all-to-all-start.2) | async-done | bytes 393248 | tf_op jit(solution)/shard_map/all_to_all | solution.py:242
  68.7 6.0 %attend.1 = bf16[4,400,128]{2,1,0:T(8,128)(2,1)S(1)} custom-call(bf16[4,128,384]{2,1,0:T(8,128)(2,1)S(1)} %all-to-all-done.2.q_ref, bf16[8,128,256]{2,1,0:T(8,128)(2,1)S(1)} %all-to-all-done.1.near_ref, bf16[8,128,256]{2,1,0:T(8,128)(2,1)S(1)} %collective-permute-done.far_ref), custom_call_target="tpu_custom_call" | custom-call | tf_op jit(solution)/shard_map/attend/pallas_call | solution.py:245
  74.6 14.5 %all_to_all.25.o_ref = bf16[4,400,128]{2,1,0:T(8,128)(2,1)S(1)} all-to-all(bf16[4,400,128]{2,1,0:T(8,128)(2,1)S(1)} %attend.1), channel_id=1, replica_groups=mesh['uly'=8,'blk_y'=8,'blk_z'=4,'blk_c'=2] {'blk_z'}, dimensions={0} | all-to-all | bytes 819200 | tf_op jit(solution)/shard_map/all_to_all | solution.py:255
  89.1 3.1 %all-gather.7.cloned.1.call-done = bf16[64,48,384]{2,1,0:T(8,128)(2,1)} async-done(((bf16[4,48,384]{2,1,0:T(8,128)(2,1)}), bf16[64,48,384]{2,1,0:T(8,128)(2,1)}) %all-gather.7.cloned.1.call-update) | async-done | bytes 2359312 | tf_op jit(solution)/shard_map/all_gather | solution.py:240
  92.2 1.7 %copy-done.1 = bf16[64,48,384]{2,1,0:T(8,128)(2,1)S(1)} copy-done((bf16[64,48,384]{2,1,0:T(8,128)(2,1)S(1)}, bf16[64,48,384]{2,1,0:T(8,128)(2,1)}, u32[]{:S(2)}) %copy-start.1) | copy-done | bytes 2359320
  93.9 1.5 %project.1 = bf16[128,3072]{1,0:T(8,128)(2,1)S(1)} custom-call(bf16[4,400,128]{2,1,0:T(8,128)(2,1)S(1)} %all_to_all.25.o_ref, bf16[8,2,4,48,384]{4,3,2,1,0:T(8,128)(2,1)S(1)} %bitcast.15), custom_call_target="tpu_custom_call" | custom-call | tf_op jit(solution)/shard_map/project/pallas_call | solution.py:257
  95.4 17.0 %all_to_all.26 = bf16[8,16,3072]{2,1,0:T(8,128)(2,1)S(1)} all-to-all(bf16[8,16,3072]{2,1,0:T(8,128)(2,1)S(1)} %bitcast.14), channel_id=1, replica_groups=mesh['uly'=8,'blk_y'=8,'blk_z'=4,'blk_c'=2] {'uly'}, dimensions={0} | all-to-all | bytes 1572864 | tf_op jit(solution)/shard_map/all_to_all | solution.py:271
  112.5 0.7 fusion
  (19 shorter events, 1.4 us)
Async XLA Ops:
  6.5 11.0 %copy-start.4 = (bf16[3072,128]{1,0:T(8,128)(2,1)S(1)}, bf16[3072,128]{1,0:T(8,128)(2,1)}, u32[]{:S(2)}) copy-start(bf16[3072,128]{1,0:T(8,128)(2,1)} %param.14) | copy-start | bytes 2359300
  6.5 42.5 %all-gather.5.cloned.1.call-start = ((), (), s32[]{:S(2)}) async-start(), calls=%async_computation.5 | async-start | bytes 1327104 | tf_op jit(solution)/shard_map/all_gather | solution.py:194
  10.4 13.6 %all-to-all-start = ((bf16[8,8,3200]{2,1,0:T(8,128)(2,1)}), bf16[8,8,3200]{2,1,0:T(8,128)(2,1)S(1)}, u32[]{:S(2)}, u32[]{:S(2)}) async-start(bf16[8,8,3200]{2,1,0:T(8,128)(2,1)} %broadcast_in_dim.35), calls=%async_computation | async-start | bytes 819200 | tf_op jit(solution)/shard_map/all_to_all | solution.py:203
  17.5 6.5 %copy-start.3 = (f32[3072]{0:T(1024)S(1)}, f32[3072]{0:T(1024)}, u32[]{:S(2)}) copy-start(f32[3072]{0:T(1024)} %param.11) | copy-start | bytes 36868
  24.0 1.1 copy-start.2
  27.3 23.4 %all-to-all-start.1 = ((bf16[8,128,256]{2,1,0:T(8,128)(2,1)}), bf16[8,128,256]{2,1,0:T(8,128)(2,1)S(1)}, u32[]{:S(2)}, u32[]{:S(2)}) async-start(bf16[8,128,256]{2,1,0:T(8,128)(2,1)} %get-tuple-element.12), calls=%async_computation.1 | async-start | bytes 1048576 | tf_op jit(solution)/shard_map/all_to_all | solution.py:238
  35.2 57.0 %all-gather.7.cloned.1.call-start = ((), (), s32[]{:S(2)}) async-start(), calls=%async_computation.6 | async-start | bytes 2506752 | tf_op jit(solution)/shard_map/all_gather | solution.py:240
  35.2 1.7 %copy-start = (bf16[3072,384]{1,0:T(8,128)(2,1)S(1)}, bf16[3072,384]{1,0:T(8,128)(2,1)}, u32[]{:S(2)}) copy-start(bf16[3072,384]{1,0:T(8,128)(2,1)} %w_ref.1) | copy-start | bytes 7077892
  50.8 17.9 %all-to-all-start.2 = ((bf16[4,128,384]{2,1,0:T(8,128)(2,1)}), bf16[4,128,384]{2,1,0:T(8,128)(2,1)S(1)}, u32[]{:S(2)}, u32[]{:S(2)}) async-start(bf16[4,128,384]{2,1,0:T(8,128)(2,1)} %q.1), calls=%async_computation.2 | async-start | bytes 786432 | tf_op jit(solution)/shard_map/all_to_all | solution.py:242
  59.8 6.6 %collective-permute-start = (bf16[8,128,256]{2,1,0:T(8,128)(2,1)S(1)}, bf16[8,128,256]{2,1,0:T(8,128)(2,1)S(1)}, u32[]{:S(2)}, u32[]{:S(2)}) collective-permute-start(bf16[8,128,256]{2,1,0:T(8,128)(2,1)S(1)} %all-to-all-done.1.near_ref), channel_id=1, source_target_pairs={{1,0},{0,1},{3,2},{2,3},{5,4},{4,5},{7,6},{6,7},{9,8},{8,9},{11,10... | collective-permute-start | bytes 1572872 | tf_op jit(solution)/shard_map/ppermute | solution.py:243
  92.2 1.7 %copy-start.1 = (bf16[64,48,384]{2,1,0:T(8,128)(2,1)S(1)}, bf16[64,48,384]{2,1,0:T(8,128)(2,1)}, u32[]{:S(2)}) copy-start(bf16[64,48,384]{2,1,0:T(8,128)(2,1)} %all-gather.7.cloned.1.call-done) | copy-start | bytes 7077892
Sparse Core Ops, SparseCore 0:
  9.5 39.5 all-gather.4
  51.2 40.9 all-gather.6

commit v6 on v5

--- a/solution.py
+++ b/solution.py
@@ -13,6 +13,7 @@
 BLK = ("blk_y", "blk_z", "blk_c")
 NEG = -(2.0**127)
 CHUNK = 2
+STEPS = 4
 HIDE = 3.0e38
 W_REPEATS = 4
 EXP2_SCALE = math.log2(math.e) / math.sqrt(HEAD)
@@ -41,7 +42,10 @@
     return v * table_ref[:, :HEAD] + pltpu.roll(v, HEAD // 2, 1) * table_ref[:, HEAD:]
 
 
-def kv_kernel(img_ref, prompt_ref, gain_ref, table_ref, w_ref, normed_ref, kv_ref, own_ref, placed_ref):
+def kv_kernel(img_ref, prompt_hbm, gain_ref, table_ref, w_ref, normed_ref, kv_ref, own_ref,
+              placed_ref, prompt_ref, sem):
+    fetch = pltpu.make_async_copy(prompt_hbm, prompt_ref, sem)
+    fetch.start()
     length, width = prompt_ref.shape
     own_len = own_ref.shape[0]
     rows = img_ref.shape[0]
@@ -50,6 +54,7 @@
     flags = jnp.where(slots == lanes, 1.0, 0.0).astype(BF16)
     present = tn_dot(flags, img_ref[:, width:])[:, 1:2] > 0.5
     chosen = tn_dot(flags, img_ref[:, :width])
+    fetch.wait()
     placed = jnp.where(present, chosen, prompt_ref[...].astype(F32))
     placed_ref[...] = placed
     mean_square = jnp.mean(placed * placed, axis=1, keepdims=True)
@@ -82,7 +87,7 @@
     return pieces
 
 
-def attend_kernel(q_ref, near_ref, far_ref, o_ref, s_ref):
+def attend_kernel(q_ref, near_ref, far_ref, o_ref, mine_ref, s_ref):
     y, z, c = (lax.axis_index(a) for a in BLK)
     n_y, length = near_ref.shape[:2]
     n_z, _, rows = q_ref.shape
@@ -131,11 +136,17 @@
                     values, jnp.concatenate(weights, axis=0), preferred_element_type=F32
                 )
         total = jnp.sum(total, axis=0, keepdims=True)
-        mixed = (mixed * (1.0 / total)).astype(BF16)
+        mixed = mixed * (1.0 / total)
         pieces = [*in_pieces(top, 3), *in_pieces(total, 2)]
         across = [slice(h * length, (h + 1) * length) for h in range(heads)]
         for h in range(heads):
-            o_ref[zq, h * HEAD : (h + 1) * HEAD, :] = mixed[:, across[h]]
+            o_ref[zq, h * HEAD : (h + 1) * HEAD, :] = mixed[:, across[h]].astype(BF16)
+
+        @pl.when(zq == z)
+        def _():
+            for h in range(heads):
+                mine_ref[h * HEAD : (h + 1) * HEAD, :] = mixed[:, across[h]]
+
         stats = [piece[:, across[h]] for piece in pieces for h in range(heads)]
         stats.append(jnp.zeros((STAT_ROWS - len(stats), length), F32))
         o_ref[zq, rows:, :] = jnp.concatenate(stats, axis=0).astype(BF16)
@@ -144,41 +155,49 @@
     lax.fori_loop(0, n_z, one_block, 0)
 
 
-def project_kernel(o_ref, w_ref, out_ref, attended_ref):
-    parts = o_ref.shape[0]
+def project_kernel(o_ref, mine_ref, w_hbm, out_ref, attended_ref, w_ref, sems):
+    n_y, n_c, n_z, piece = w_ref.shape[:4]
+    half = n_y // STEPS
+    fetches = [
+        pltpu.make_async_copy(w_hbm.at[pl.ds(i * half, half)], w_ref.at[pl.ds(i * half, half)], sems.at[i])
+        for i in range(STEPS)
+    ]
+    for fetch in fetches:
+        fetch.start()
+    own = lax.axis_index(BLK[1])
     rows = o_ref.shape[1] - STAT_ROWS
     length = o_ref.shape[2]
     heads = rows // length
-
-    @pl.when(pl.program_id(0) == 0)
-    def _():
-        tops, totals = [], []
-        for i in range(parts):
-            stats = o_ref[i, rows:, :].astype(F32)
-            pieces = [stats[k * heads : (k + 1) * heads] for k in range(5)]
-            tops.append(pieces[0] + pieces[1] + pieces[2])
-            totals.append(pieces[3] + pieces[4])
-        best = functools.reduce(jnp.maximum, tops)
-        grown = [jnp.exp2((t - best) * EXP2_SCALE) for t in tops]
-        grown = [g * t for g, t in zip(grown, totals)]
-        whole = sum(grown)
-        share = [g / whole for g in grown]
-        for h in range(heads):
-            part = slice(h * HEAD, (h + 1) * HEAD)
-            mixed = sum(
-                o_ref[i, part, :].astype(F32) * share[i][h : h + 1] for i in range(parts)
-            )
-            attended_ref[:, part] = mixed.T.astype(BF16)
-
-    many, n_c, n_z = w_ref.shape[:3]
-    w = jnp.concatenate(
-        [w_ref[i, c, z] for i in range(many) for z in range(n_z) for c in range(n_c)], axis=0
-    )
-    out_ref[...] = nt_dot(attended_ref[...], w).astype(BF16)
-
-
-def whole_block(shape):
-    return pl.BlockSpec(shape, lambda *_: (0,) * len(shape))
+    tops, totals = [], []
+    for i in range(n_z):
+        stats = o_ref[i, rows:, :].astype(F32)
+        pieces = [stats[k * heads : (k + 1) * heads] for k in range(5)]
+        tops.append(pieces[0] + pieces[1] + pieces[2])
+        totals.append(pieces[3] + pieces[4])
+    best = functools.reduce(jnp.maximum, tops)
+    grown = [jnp.exp2((t - best) * EXP2_SCALE) * total for t, total in zip(tops, totals)]
+    whole = sum(grown)
+    share = [g / whole for g in grown]
+    for h in range(heads):
+        part = slice(h * HEAD, (h + 1) * HEAD)
+        mixed = sum(
+            jnp.where(own == i, mine_ref[part, :], o_ref[i, part, :].astype(F32)) * share[i][h : h + 1]
+            for i in range(n_z)
+        )
+        attended_ref[:, part] = mixed.T.astype(BF16)
+    columns = half * n_z * n_c * piece
+    for i, fetch in enumerate(fetches):
+        fetch.wait()
+        w = jnp.concatenate(
+            [
+                w_ref[i * half + j, c, z]
+                for j in range(half)
+                for z in range(n_z)
+                for c in range(n_c)
+            ],
+            axis=0,
+        )
+        out_ref[:, i * columns : (i + 1) * columns] = nt_dot(attended_ref[...], w).astype(BF16)
 
 
 def body(prompt, image_rows, image_slots, norm_gain, w_query, key_matrix, value_matrix, w_out):
@@ -209,6 +228,7 @@
     table = jnp.concatenate([cosine, sine], axis=1)
     w_kv = jnp.concatenate([key_matrix, value_matrix], axis=1)
     vmem = pl.BlockSpec(memory_space=pltpu.VMEM)
+    hbm = pl.BlockSpec(memory_space=pltpu.HBM)
     rows = heads * block_len
     normed, key_value, own = pl.pallas_call(
         kv_kernel,
@@ -217,12 +237,16 @@
             jax.ShapeDtypeStruct((n_y, block_len, 2 * HEAD), BF16),
             jax.ShapeDtypeStruct((own_len, width), F32),
         ),
-        in_specs=[vmem] * 5,
+        in_specs=[vmem, hbm, vmem, vmem, vmem],
         out_specs=[vmem] * 3,
-        scratch_shapes=[pltpu.VMEM((block_len, width), F32)],
+        scratch_shapes=[
+            pltpu.VMEM((block_len, width), F32),
+            pltpu.VMEM((block_len, width), BF16),
+            pltpu.SemaphoreType.DMA,
+        ],
         compiler_params=pltpu.CompilerParams(vmem_limit_bytes=24 << 20),
         name="kv",
-    )(images, prompt[0], norm_gain[None], table, w_kv)
+    )(images, pltpu.with_memory_space_constraint(prompt[0], pltpu.HBM), norm_gain[None], table, w_kv)
     queries = pl.pallas_call(
         q_kernel,
         out_shape=jax.ShapeDtypeStruct((n_z, HEAD, rows), BF16),
@@ -242,31 +266,33 @@
     asked = lax.all_to_all(queries, BLK[1], 0, 0, tiled=True)
     far = lax.ppermute(near, BLK[2], [((i + 1) % n_c, i) for i in range(n_c)])
 
-    partial = pl.pallas_call(
+    partial, mine = pl.pallas_call(
         attend_kernel,
-        out_shape=jax.ShapeDtypeStruct((n_z, rows + STAT_ROWS, HEAD), BF16),
+        out_shape=(
+            jax.ShapeDtypeStruct((n_z, rows + STAT_ROWS, HEAD), BF16),
+            jax.ShapeDtypeStruct((rows, HEAD), F32),
+        ),
         in_specs=[vmem] * 3,
-        out_specs=vmem,
+        out_specs=[vmem] * 2,
         scratch_shapes=[pltpu.VMEM((n_c, n_y, block_len, rows), F32)],
         compiler_params=pltpu.CompilerParams(vmem_limit_bytes=24 << 20),
         name="attend",
     )(asked, near, far)
 
     parts = lax.all_to_all(partial, BLK[1], 0, 0, tiled=True)
-    piece = w_out.shape[1]
     projected = pl.pallas_call(
         project_kernel,
         out_shape=jax.ShapeDtypeStruct((block_len, width), BF16),
-        grid=(n_y // 2,),
-        in_specs=[
-            whole_block(parts.shape),
-            pl.BlockSpec((2, n_c, n_z, piece, q_width), lambda i: (i, 0, 0, 0, 0)),
+        in_specs=[vmem, vmem, hbm],
+        out_specs=vmem,
+        scratch_shapes=[
+            pltpu.VMEM((block_len, q_width), BF16),
+            pltpu.VMEM(w_all.shape, BF16),
+            pltpu.SemaphoreType.DMA((STEPS,)),
         ],
-        out_specs=pl.BlockSpec((block_len, 2 * width // n_y), lambda i: (0, i)),
-        scratch_shapes=[pltpu.VMEM((block_len, q_width), BF16)],
         compiler_params=pltpu.CompilerParams(vmem_limit_bytes=24 << 20),
         name="project",
-    )(parts, w_all)
+    )(parts, mine, pltpu.with_memory_space_constraint(w_all, pltpu.HBM))
 
     shares = lax.all_to_all(
         projected.reshape(n_uly, own_len, width), "uly", 0, 0, tiled=True

time: 121 us -> 120 us (level)
  local copies, waits for them, and re-layouts: 8.34 us -> 5.55 us
  Pallas kernels: 11.3 us -> 13.2 us
    unnamed x10 -> x6, local copies, waits for them, and re-layouts: 4.47 us -> 1.67 us
    pallas_call x1, Pallas kernels: 2.19 us -> 3.46 us  [body(): pl.pallas_call(kv_kernel, out_shape=(jax.ShapeDtypeStruct((block_len, wid...]
  transfers between devices with their start and end apart: 6 -> 6, of which waited for: 6 -> 6; matrix products, arithmetic and copies ran while one was open for 5% -> 5% of each run, Pallas kernels for 8% -> 9%
where the time goes in v6:
time: 120 us
  blocking collectives  31.3 us (26%)
  starting transfers between devices  28.7 us (24%)
  waiting for transfers between devices  23.2 us (19%)
  between operations  13.5 us (11%)
  Pallas kernels  13.2 us (11%)
  local copies, waits for them, and re-layouts  5.55 us (5%)
  other arithmetic  4.07 us (3%)
    all_to_all x1, blocking collectives, body(): lax.all_to_all(projected.reshape(n_uly, own_len, width), 'uly', 0, 0, til...  17 us
    all_to_all x1, blocking collectives, body(): parts = lax.all_to_all(partial, BLK[1], 0, 0, tiled=True)  14.2 us
    all_gather x1, waiting for transfers between devices, body(): lax.all_gather(repeated, BLK[1:], axis=0, tiled=False)  10.5 us
    all_to_all x1, starting transfers between devices, body(): asked = lax.all_to_all(queries, BLK[1], 0, 0, tiled=True)  9.2 us
    all_to_all x1, starting transfers between devices, body(): near = lax.all_to_all(key_value, BLK[0], 0, 0, tiled=True)  7.85 us
    all_to_all x1, starting transfers between devices, body(): lax.all_to_all(jnp.broadcast_to(tagged[None], (n_uly, *tagged.shape)), 'u...  6.66 us
    pallas_call x1, Pallas kernels, body(): pl.pallas_call(attend_kernel, out_shape=(jax.ShapeDtypeStruct((n_z, rows...  5.45 us
    all_to_all x1, waiting for transfers between devices, body(): lax.all_to_all(jnp.broadcast_to(tagged[None], (n_uly, *tagged.shape)), 'u...  5.13 us
  transfers between devices with their start and end apart: 6, of which 6 were waited for; matrix products, arithmetic and copies ran while one was open for 5% of the time, Pallas kernels for 9%

profile of v6, /device:TPU:1, one launch (start us, length us, event | category | flops | bytes accessed | tf_op | source)
XLA Modules:
  0.0 119.5 jit_solution(10751781433814480518)
XLA Ops:
  6.5 1.5 %broadcast_in_dim.37 = bf16[4,48,384]{2,1,0:T(8,128)(2,1)} broadcast(bf16[48,384]{1,0:T(8,128)(2,1)} %bitcast.20), dimensions={1,2} | broadcast | bytes 184320 | tf_op jit(solution)/shard_map/broadcast_in_dim | solution.py:212
  8.1 0.7 convert_bitcast_fusion
  8.7 0.9 select_select_fusion
  9.6 0.8 broadcast_in_dim.35
  10.4 6.7 %all-to-all-start = ((bf16[8,8,3200]{2,1,0:T(8,128)(2,1)}), bf16[8,8,3200]{2,1,0:T(8,128)(2,1)S(1)}, u32[]{:S(2)}, u32[]{:S(2)}) async-start(bf16[8,8,3200]{2,1,0:T(8,128)(2,1)} %broadcast_in_dim.35), calls=%async_computation | async-start | bytes 819200 | tf_op jit(solution)/shard_map/all_to_all | solution.py:222
  17.1 0.3 multiply_cosine_fusion
  17.5 1.3 %pad_maximum_fusion.w_ref = bf16[3072,256]{1,0:T(8,128)(2,1)S(1)} fusion(bf16[3072,128]{1,0:T(8,128)(2,1)S(1)} %copy-done.2, bf16[3072,128]{1,0:T(8,128)(2,1)} %param.13), kind=kLoop, calls=%fused_computation | loop fusion | flops 3145728 | bytes 3145728 | tf_op jit(solution)/shard_map/concatenate | solution.py:229
  18.9 5.1 %all-to-all-done = bf16[8,8,3200]{2,1,0:T(8,128)(2,1)S(1)} async-done(((bf16[8,8,3200]{2,1,0:T(8,128)(2,1)}), bf16[8,8,3200]{2,1,0:T(8,128)(2,1)S(1)}, u32[]{:S(2)}, u32[]{:S(2)}) %all-to-all-start) | async-done | bytes 409632 | tf_op jit(solution)/shard_map/all_to_all | solution.py:222
  24.0 3.5 %kv.1 = (bf16[128,3072]{1,0:T(8,128)(2,1)S(1)}, bf16[8,128,256]{2,1,0:T(8,128)(2,1)}, f32[16,3072]{1,0:T(8,128)S(1)}) custom-call(bf16[64,3200]{1,0:T(8,128)(2,1)S(1)} %bitcast.15, bf16[128,3072]{1,0:T(8,128)(2,1)} %bitcast.18, f32[1,3072]{1,0:T(1,128)S(1)} %bitcast.16, f32[128,256]{1,0:T(8,128)S(1)} %pad_maximum_fusion.1.table_ref, ...), custom_call_target="tpu_custom_call" | custom-call | tf_op jit(solution)/shard_map/kv/pallas_call | solution.py:233
  27.5 7.9 %all-to-all-start.1 = ((bf16[8,128,256]{2,1,0:T(8,128)(2,1)}), bf16[8,128,256]{2,1,0:T(8,128)(2,1)S(1)}, u32[]{:S(2)}, u32[]{:S(2)}) async-start(bf16[8,128,256]{2,1,0:T(8,128)(2,1)} %get-tuple-element.14), calls=%async_computation.1 | async-start | bytes 1048576 | tf_op jit(solution)/shard_map/all_to_all | solution.py:262
  35.4 1.7 %copy-done = bf16[3072,384]{1,0:T(8,128)(2,1)S(1)} copy-done((bf16[3072,384]{1,0:T(8,128)(2,1)S(1)}, bf16[3072,384]{1,0:T(8,128)(2,1)}, u32[]{:S(2)}) %copy-start) | copy-done | bytes 2359320
  37.0 1.6 %q.1 = bf16[4,128,384]{2,1,0:T(8,128)(2,1)} custom-call(bf16[128,3072]{1,0:T(8,128)(2,1)S(1)} %get-tuple-element.15.normed_ref, f32[128,256]{1,0:T(8,128)S(1)} %pad_maximum_fusion.1.table_ref, bf16[3072,384]{1,0:T(8,128)(2,1)S(1)} %copy-done), custom_call_target="tpu_custom_call" | custom-call | flops 301989888 | bytes 2359296 | tf_op jit(solution)/shard_map/q/pallas_call | solution.py:250
  38.6 10.5 %all-gather.5.cloned.1.call-done = bf16[32,48,384]{2,1,0:T(8,128)(2,1)} async-done(((bf16[4,48,384]{2,1,0:T(8,128)(2,1)}), bf16[32,48,384]{2,1,0:T(8,128)(2,1)}) %all-gather.5.cloned.1.call-update) | async-done | bytes 1179664 | tf_op jit(solution)/shard_map/all_gather | solution.py:213
  49.1 1.6 %dynamic-slice_bitcast_fusion = bf16[4,48,384]{2,1,0:T(8,128)(2,1)} fusion(bf16[4,2,4,48,384]{4,3,2,1,0:T(8,128)(2,1)} %bitcast.21, s32[]{:T(128)S(6)} %select_n.12), kind=kLoop, calls=%fused_computation.3 | loop fusion | bytes 294916 | tf_op jit(solution)/shard_map/reshape | solution.py:214
  50.9 9.2 %all-to-all-start.2 = ((bf16[4,128,384]{2,1,0:T(8,128)(2,1)}), bf16[4,128,384]{2,1,0:T(8,128)(2,1)S(1)}, u32[]{:S(2)}, u32[]{:S(2)}) async-start(bf16[4,128,384]{2,1,0:T(8,128)(2,1)} %q.1), calls=%async_computation.2 | async-start | bytes 786432 | tf_op jit(solution)/shard_map/all_to_all | solution.py:266
  60.1 5.0 %collective-permute-start = (bf16[8,128,256]{2,1,0:T(8,128)(2,1)S(1)}, bf16[8,128,256]{2,1,0:T(8,128)(2,1)S(1)}, u32[]{:S(2)}, u32[]{:S(2)}) collective-permute-start(bf16[8,128,256]{2,1,0:T(8,128)(2,1)S(1)} %all-to-all-done.1.near_ref), channel_id=1, source_target_pairs={{1,0},{0,1},{3,2},{2,3},{5,4},{4,5},{7,6},{6,7},{9,8},{8,9},{11,10... | collective-permute-start | bytes 1572872 | tf_op jit(solution)/shard_map/ppermute | solution.py:267
  65.1 1.5 %collective-permute-done.far_ref = bf16[8,128,256]{2,1,0:T(8,128)(2,1)S(1)} collective-permute-done((bf16[8,128,256]{2,1,0:T(8,128)(2,1)S(1)}, bf16[8,128,256]{2,1,0:T(8,128)(2,1)S(1)}, u32[]{:S(2)}, u32[]{:S(2)}) %collective-permute-start) | collective-permute-done | bytes 524320 | tf_op jit(solution)/shard_map/ppermute | solution.py:267
  66.6 2.4 %all-to-all-done.2.q_ref = bf16[4,128,384]{2,1,0:T(8,128)(2,1)S(1)} async-done(((bf16[4,128,384]{2,1,0:T(8,128)(2,1)}), bf16[4,128,384]{2,1,0:T(8,128)(2,1)S(1)}, u32[]{:S(2)}, u32[]{:S(2)}) %all-to-all-start.2) | async-done | bytes 393248 | tf_op jit(solution)/shard_map/all_to_all | solution.py:266
  69.0 5.5 %attend.1 = (bf16[4,400,128]{2,1,0:T(8,128)(2,1)S(1)}, f32[384,128]{1,0:T(8,128)S(1)}) custom-call(bf16[4,128,384]{2,1,0:T(8,128)(2,1)S(1)} %all-to-all-done.2.q_ref, bf16[8,128,256]{2,1,0:T(8,128)(2,1)S(1)} %all-to-all-done.1.near_ref, bf16[8,128,256]{2,1,0:T(8,128)(2,1)S(1)} %collective-permute-done.far_ref), custom_call_target="tpu_custom_call" | custom-call | tf_op jit(solution)/shard_map/attend/pallas_call | solution.py:269
  74.5 14.2 %all_to_all.25.o_ref = bf16[4,400,128]{2,1,0:T(8,128)(2,1)S(1)} all-to-all(bf16[4,400,128]{2,1,0:T(8,128)(2,1)S(1)} %get-tuple-element.18), channel_id=1, replica_groups=mesh['uly'=8,'blk_y'=8,'blk_z'=4,'blk_c'=2] {'blk_z'}, dimensions={0} | all-to-all | bytes 819200 | tf_op jit(solution)/shard_map/all_to_all | solution.py:282
  88.7 3.5 %all-gather.7.cloned.1.call-done = bf16[64,48,384]{2,1,0:T(8,128)(2,1)} async-done(((bf16[4,48,384]{2,1,0:T(8,128)(2,1)}), bf16[64,48,384]{2,1,0:T(8,128)(2,1)}) %all-gather.7.cloned.1.call-update) | async-done | bytes 2359312 | tf_op jit(solution)/shard_map/all_gather | solution.py:264
  92.2 2.7 %project.1 = bf16[128,3072]{1,0:T(8,128)(2,1)S(1)} custom-call(bf16[4,400,128]{2,1,0:T(8,128)(2,1)S(1)} %all_to_all.25.o_ref, f32[384,128]{1,0:T(8,128)S(1)} %get-tuple-element.19.mine_ref, bf16[8,2,4,48,384]{4,3,2,1,0:T(8,128)(2,1)} %bitcast.17), custom_call_target="tpu_custom_call" | custom-call | tf_op jit(solution)/shard_map/project/pallas_call | solution.py:283
  94.9 17.0 %all_to_all.26 = bf16[8,16,3072]{2,1,0:T(8,128)(2,1)S(1)} all-to-all(bf16[8,16,3072]{2,1,0:T(8,128)(2,1)S(1)} %bitcast.14), channel_id=1, replica_groups=mesh['uly'=8,'blk_y'=8,'blk_z'=4,'blk_c'=2] {'uly'}, dimensions={0} | all-to-all | bytes 1572864 | tf_op jit(solution)/shard_map/all_to_all | solution.py:297
  112.0 0.7 fusion
  (15 shorter events, 0.5 us)
Async XLA Ops:
  6.5 11.0 %copy-start.2 = (bf16[3072,128]{1,0:T(8,128)(2,1)S(1)}, bf16[3072,128]{1,0:T(8,128)(2,1)}, u32[]{:S(2)}) copy-start(bf16[3072,128]{1,0:T(8,128)(2,1)} %param.14) | copy-start | bytes 2359300
  6.5 42.6 %all-gather.5.cloned.1.call-start = ((), (), s32[]{:S(2)}) async-start(), calls=%async_computation.5 | async-start | bytes 1327104 | tf_op jit(solution)/shard_map/all_gather | solution.py:213
  10.4 13.6 %all-to-all-start = ((bf16[8,8,3200]{2,1,0:T(8,128)(2,1)}), bf16[8,8,3200]{2,1,0:T(8,128)(2,1)S(1)}, u32[]{:S(2)}, u32[]{:S(2)}) async-start(bf16[8,8,3200]{2,1,0:T(8,128)(2,1)} %broadcast_in_dim.35), calls=%async_computation | async-start | bytes 819200 | tf_op jit(solution)/shard_map/all_to_all | solution.py:222
  17.5 6.5 %copy-start.1 = (f32[3072]{0:T(1024)S(1)}, f32[3072]{0:T(1024)}, u32[]{:S(2)}) copy-start(f32[3072]{0:T(1024)} %param.11) | copy-start | bytes 36868
  27.5 23.4 %all-to-all-start.1 = ((bf16[8,128,256]{2,1,0:T(8,128)(2,1)}), bf16[8,128,256]{2,1,0:T(8,128)(2,1)S(1)}, u32[]{:S(2)}, u32[]{:S(2)}) async-start(bf16[8,128,256]{2,1,0:T(8,128)(2,1)} %get-tuple-element.14), calls=%async_computation.1 | async-start | bytes 1048576 | tf_op jit(solution)/shard_map/all_to_all | solution.py:262
  35.3 56.9 %all-gather.7.cloned.1.call-start = ((), (), s32[]{:S(2)}) async-start(), calls=%async_computation.6 | async-start | bytes 2506752 | tf_op jit(solution)/shard_map/all_gather | solution.py:264
  35.4 1.7 %copy-start = (bf16[3072,384]{1,0:T(8,128)(2,1)S(1)}, bf16[3072,384]{1,0:T(8,128)(2,1)}, u32[]{:S(2)}) copy-start(bf16[3072,384]{1,0:T(8,128)(2,1)} %w_ref.1) | copy-start | bytes 7077892
  50.9 18.1 %all-to-all-start.2 = ((bf16[4,128,384]{2,1,0:T(8,128)(2,1)}), bf16[4,128,384]{2,1,0:T(8,128)(2,1)S(1)}, u32[]{:S(2)}, u32[]{:S(2)}) async-start(bf16[4,128,384]{2,1,0:T(8,128)(2,1)} %q.1), calls=%async_computation.2 | async-start | bytes 786432 | tf_op jit(solution)/shard_map/all_to_all | solution.py:266
  60.1 6.5 %collective-permute-start = (bf16[8,128,256]{2,1,0:T(8,128)(2,1)S(1)}, bf16[8,128,256]{2,1,0:T(8,128)(2,1)S(1)}, u32[]{:S(2)}, u32[]{:S(2)}) collective-permute-start(bf16[8,128,256]{2,1,0:T(8,128)(2,1)S(1)} %all-to-all-done.1.near_ref), channel_id=1, source_target_pairs={{1,0},{0,1},{3,2},{2,3},{5,4},{4,5},{7,6},{6,7},{9,8},{8,9},{11,10... | collective-permute-start | bytes 1572872 | tf_op jit(solution)/shard_map/ppermute | solution.py:267
Sparse Core Ops, SparseCore 0:
  9.5 39.6 all-gather.4
  51.2 40.9 all-gather.6

commit v7 on v6

--- a/solution.py
+++ b/solution.py
@@ -14,7 +14,7 @@
 NEG = -(2.0**127)
 CHUNK = 2
 STEPS = 4
-HIDE = 3.0e38
+HIDE = float("inf")
 W_REPEATS = 4
 EXP2_SCALE = math.log2(math.e) / math.sqrt(HEAD)
 STAT_ROWS = 16
@@ -156,10 +156,10 @@
 
 
 def project_kernel(o_ref, mine_ref, w_hbm, out_ref, attended_ref, w_ref, sems):
-    n_y, n_c, n_z, piece = w_ref.shape[:4]
+    n_c, n_y, n_z, piece = w_ref.shape[:4]
     half = n_y // STEPS
     fetches = [
-        pltpu.make_async_copy(w_hbm.at[pl.ds(i * half, half)], w_ref.at[pl.ds(i * half, half)], sems.at[i])
+        pltpu.make_async_copy(w_hbm.at[:, pl.ds(i * half, half)], w_ref.at[:, pl.ds(i * half, half)], sems.at[i])
         for i in range(STEPS)
     ]
     for fetch in fetches:
@@ -190,7 +190,7 @@
         fetch.wait()
         w = jnp.concatenate(
             [
-                w_ref[i * half + j, c, z]
+                w_ref[c, i * half + j, z]
                 for j in range(half)
                 for z in range(n_z)
                 for c in range(n_c)
@@ -261,8 +261,8 @@
 
     near = lax.all_to_all(key_value, BLK[0], 0, 0, tiled=True)
     near, w_near, queries = lax.optimization_barrier((near, w_near, queries))
-    w_all = lax.all_gather(w_near, (BLK[0], BLK[2]), axis=0, tiled=False)
-    w_all = w_all.reshape(n_y, n_c, n_z, *w_near.shape[1:])
+    w_all = lax.all_gather(w_near, (BLK[2], BLK[0]), axis=0, tiled=False)
+    w_all = w_all.reshape(n_c, n_y, n_z, *w_near.shape[1:])
     asked = lax.all_to_all(queries, BLK[1], 0, 0, tiled=True)
     far = lax.ppermute(near, BLK[2], [((i + 1) % n_c, i) for i in range(n_c)])
 

time: 120 us -> 120 us (level)
  no operation moved by 1% of the time
where the time goes in v7:
time: 120 us
  blocking collectives  31.1 us (26%)
  starting transfers between devices  28.7 us (24%)
  waiting for transfers between devices  23.4 us (20%)
  between operations  13.5 us (11%)
  Pallas kernels  13.2 us (11%)
  local copies, waits for them, and re-layouts  5.55 us (5%)
  other arithmetic  4.07 us (3%)
    all_to_all x1, blocking collectives, body(): lax.all_to_all(projected.reshape(n_uly, own_len, width), 'uly', 0, 0, til...  16.9 us
    all_to_all x1, blocking collectives, body(): parts = lax.all_to_all(partial, BLK[1], 0, 0, tiled=True)  14.2 us
    all_gather x1, waiting for transfers between devices, body(): lax.all_gather(repeated, BLK[1:], axis=0, tiled=False)  10.5 us
    all_to_all x1, starting transfers between devices, body(): asked = lax.all_to_all(queries, BLK[1], 0, 0, tiled=True)  9.2 us
    all_to_all x1, starting transfers between devices, body(): near = lax.all_to_all(key_value, BLK[0], 0, 0, tiled=True)  7.85 us
    all_to_all x1, starting transfers between devices, body(): lax.all_to_all(jnp.broadcast_to(tagged[None], (n_uly, *tagged.shape)), 'u...  6.66 us
    pallas_call x1, Pallas kernels, body(): pl.pallas_call(attend_kernel, out_shape=(jax.ShapeDtypeStruct((n_z, rows...  5.45 us
    all_to_all x1, waiting for transfers between devices, body(): lax.all_to_all(jnp.broadcast_to(tagged[None], (n_uly, *tagged.shape)), 'u...  5.13 us
  transfers between devices with their start and end apart: 6, of which 6 were waited for; matrix products, arithmetic and copies ran while one was open for 5% of the time, Pallas kernels for 9%

profile of v7, /device:TPU:1, one launch (start us, length us, event | category | flops | bytes accessed | tf_op | source)
XLA Modules:
  0.0 119.5 jit_solution(15844930286550406307)
XLA Ops:
  6.5 1.5 %broadcast_in_dim.37 = bf16[4,48,384]{2,1,0:T(8,128)(2,1)} broadcast(bf16[48,384]{1,0:T(8,128)(2,1)} %bitcast.20), dimensions={1,2} | broadcast | bytes 184320 | tf_op jit(solution)/shard_map/broadcast_in_dim | solution.py:212
  8.1 0.7 convert_bitcast_fusion
  8.7 0.9 select_select_fusion
  9.6 0.8 broadcast_in_dim.35
  10.4 6.7 %all-to-all-start = ((bf16[8,8,3200]{2,1,0:T(8,128)(2,1)}), bf16[8,8,3200]{2,1,0:T(8,128)(2,1)S(1)}, u32[]{:S(2)}, u32[]{:S(2)}) async-start(bf16[8,8,3200]{2,1,0:T(8,128)(2,1)} %broadcast_in_dim.35), calls=%async_computation | async-start | bytes 819200 | tf_op jit(solution)/shard_map/all_to_all | solution.py:222
  17.1 0.3 multiply_cosine_fusion
  17.5 1.3 %pad_maximum_fusion.w_ref = bf16[3072,256]{1,0:T(8,128)(2,1)S(1)} fusion(bf16[3072,128]{1,0:T(8,128)(2,1)S(1)} %copy-done.2, bf16[3072,128]{1,0:T(8,128)(2,1)} %param.13), kind=kLoop, calls=%fused_computation | loop fusion | flops 3145728 | bytes 3145728 | tf_op jit(solution)/shard_map/concatenate | solution.py:229
  18.9 5.1 %all-to-all-done = bf16[8,8,3200]{2,1,0:T(8,128)(2,1)S(1)} async-done(((bf16[8,8,3200]{2,1,0:T(8,128)(2,1)}), bf16[8,8,3200]{2,1,0:T(8,128)(2,1)S(1)}, u32[]{:S(2)}, u32[]{:S(2)}) %all-to-all-start) | async-done | bytes 409632 | tf_op jit(solution)/shard_map/all_to_all | solution.py:222
  24.0 3.5 %kv.1 = (bf16[128,3072]{1,0:T(8,128)(2,1)S(1)}, bf16[8,128,256]{2,1,0:T(8,128)(2,1)}, f32[16,3072]{1,0:T(8,128)S(1)}) custom-call(bf16[64,3200]{1,0:T(8,128)(2,1)S(1)} %bitcast.15, bf16[128,3072]{1,0:T(8,128)(2,1)} %bitcast.18, f32[1,3072]{1,0:T(1,128)S(1)} %bitcast.16, f32[128,256]{1,0:T(8,128)S(1)} %pad_maximum_fusion.1.table_ref, ...), custom_call_target="tpu_custom_call" | custom-call | tf_op jit(solution)/shard_map/kv/pallas_call | solution.py:233
  27.5 7.9 %all-to-all-start.1 = ((bf16[8,128,256]{2,1,0:T(8,128)(2,1)}), bf16[8,128,256]{2,1,0:T(8,128)(2,1)S(1)}, u32[]{:S(2)}, u32[]{:S(2)}) async-start(bf16[8,128,256]{2,1,0:T(8,128)(2,1)} %get-tuple-element.14), calls=%async_computation.1 | async-start | bytes 1048576 | tf_op jit(solution)/shard_map/all_to_all | solution.py:262
  35.4 1.7 %copy-done = bf16[3072,384]{1,0:T(8,128)(2,1)S(1)} copy-done((bf16[3072,384]{1,0:T(8,128)(2,1)S(1)}, bf16[3072,384]{1,0:T(8,128)(2,1)}, u32[]{:S(2)}) %copy-start) | copy-done | bytes 2359320
  37.0 1.6 %q.1 = bf16[4,128,384]{2,1,0:T(8,128)(2,1)} custom-call(bf16[128,3072]{1,0:T(8,128)(2,1)S(1)} %get-tuple-element.15.normed_ref, f32[128,256]{1,0:T(8,128)S(1)} %pad_maximum_fusion.1.table_ref, bf16[3072,384]{1,0:T(8,128)(2,1)S(1)} %copy-done), custom_call_target="tpu_custom_call" | custom-call | flops 301989888 | bytes 2359296 | tf_op jit(solution)/shard_map/q/pallas_call | solution.py:250
  38.6 10.5 %all-gather.5.cloned.1.call-done = bf16[32,48,384]{2,1,0:T(8,128)(2,1)} async-done(((bf16[4,48,384]{2,1,0:T(8,128)(2,1)}), bf16[32,48,384]{2,1,0:T(8,128)(2,1)}) %all-gather.5.cloned.1.call-update) | async-done | bytes 1179664 | tf_op jit(solution)/shard_map/all_gather | solution.py:213
  49.1 1.6 %dynamic-slice_bitcast_fusion = bf16[4,48,384]{2,1,0:T(8,128)(2,1)} fusion(bf16[4,2,4,48,384]{4,3,2,1,0:T(8,128)(2,1)} %bitcast.21, s32[]{:T(128)S(6)} %select_n.12), kind=kLoop, calls=%fused_computation.3 | loop fusion | bytes 294916 | tf_op jit(solution)/shard_map/reshape | solution.py:214
  50.9 9.2 %all-to-all-start.2 = ((bf16[4,128,384]{2,1,0:T(8,128)(2,1)}), bf16[4,128,384]{2,1,0:T(8,128)(2,1)S(1)}, u32[]{:S(2)}, u32[]{:S(2)}) async-start(bf16[4,128,384]{2,1,0:T(8,128)(2,1)} %q.1), calls=%async_computation.2 | async-start | bytes 786432 | tf_op jit(solution)/shard_map/all_to_all | solution.py:266
  60.1 5.0 %collective-permute-start = (bf16[8,128,256]{2,1,0:T(8,128)(2,1)S(1)}, bf16[8,128,256]{2,1,0:T(8,128)(2,1)S(1)}, u32[]{:S(2)}, u32[]{:S(2)}) collective-permute-start(bf16[8,128,256]{2,1,0:T(8,128)(2,1)S(1)} %all-to-all-done.1.near_ref), channel_id=1, source_target_pairs={{1,0},{0,1},{3,2},{2,3},{5,4},{4,5},{7,6},{6,7},{9,8},{8,9},{11,10... | collective-permute-start | bytes 1572872 | tf_op jit(solution)/shard_map/ppermute | solution.py:267
  65.1 1.5 %collective-permute-done.far_ref = bf16[8,128,256]{2,1,0:T(8,128)(2,1)S(1)} collective-permute-done((bf16[8,128,256]{2,1,0:T(8,128)(2,1)S(1)}, bf16[8,128,256]{2,1,0:T(8,128)(2,1)S(1)}, u32[]{:S(2)}, u32[]{:S(2)}) %collective-permute-start) | collective-permute-done | bytes 524320 | tf_op jit(solution)/shard_map/ppermute | solution.py:267
  66.6 2.4 %all-to-all-done.2.q_ref = bf16[4,128,384]{2,1,0:T(8,128)(2,1)S(1)} async-done(((bf16[4,128,384]{2,1,0:T(8,128)(2,1)}), bf16[4,128,384]{2,1,0:T(8,128)(2,1)S(1)}, u32[]{:S(2)}, u32[]{:S(2)}) %all-to-all-start.2) | async-done | bytes 393248 | tf_op jit(solution)/shard_map/all_to_all | solution.py:266
  69.0 5.5 %attend.1 = (bf16[4,400,128]{2,1,0:T(8,128)(2,1)S(1)}, f32[384,128]{1,0:T(8,128)S(1)}) custom-call(bf16[4,128,384]{2,1,0:T(8,128)(2,1)S(1)} %all-to-all-done.2.q_ref, bf16[8,128,256]{2,1,0:T(8,128)(2,1)S(1)} %all-to-all-done.1.near_ref, bf16[8,128,256]{2,1,0:T(8,128)(2,1)S(1)} %collective-permute-done.far_ref), custom_call_target="tpu_custom_call" | custom-call | tf_op jit(solution)/shard_map/attend/pallas_call | solution.py:269
  74.5 14.2 %all_to_all.25.o_ref = bf16[4,400,128]{2,1,0:T(8,128)(2,1)S(1)} all-to-all(bf16[4,400,128]{2,1,0:T(8,128)(2,1)S(1)} %get-tuple-element.18), channel_id=1, replica_groups=mesh['uly'=8,'blk_y'=8,'blk_z'=4,'blk_c'=2] {'blk_z'}, dimensions={0} | all-to-all | bytes 819200 | tf_op jit(solution)/shard_map/all_to_all | solution.py:282
  88.7 3.6 %all-gather.7.cloned.1.call-done = bf16[64,48,384]{2,1,0:T(8,128)(2,1)} async-done(((bf16[4,48,384]{2,1,0:T(8,128)(2,1)}), bf16[64,48,384]{2,1,0:T(8,128)(2,1)}) %all-gather.7.cloned.1.call-update) | async-done | bytes 2359312 | tf_op jit(solution)/shard_map/all_gather | solution.py:264
  92.4 2.7 %project.1 = bf16[128,3072]{1,0:T(8,128)(2,1)S(1)} custom-call(bf16[4,400,128]{2,1,0:T(8,128)(2,1)S(1)} %all_to_all.25.o_ref, f32[384,128]{1,0:T(8,128)S(1)} %get-tuple-element.19.mine_ref, bf16[2,8,4,48,384]{4,3,2,1,0:T(8,128)(2,1)} %bitcast.17), custom_call_target="tpu_custom_call" | custom-call | tf_op jit(solution)/shard_map/project/pallas_call | solution.py:283
  95.1 16.9 %all_to_all.26 = bf16[8,16,3072]{2,1,0:T(8,128)(2,1)S(1)} all-to-all(bf16[8,16,3072]{2,1,0:T(8,128)(2,1)S(1)} %bitcast.14), channel_id=1, replica_groups=mesh['uly'=8,'blk_y'=8,'blk_z'=4,'blk_c'=2] {'uly'}, dimensions={0} | all-to-all | bytes 1572864 | tf_op jit(solution)/shard_map/all_to_all | solution.py:297
  112.0 0.7 fusion
  (15 shorter events, 0.5 us)
Async XLA Ops:
  6.5 11.0 %copy-start.2 = (bf16[3072,128]{1,0:T(8,128)(2,1)S(1)}, bf16[3072,128]{1,0:T(8,128)(2,1)}, u32[]{:S(2)}) copy-start(bf16[3072,128]{1,0:T(8,128)(2,1)} %param.14) | copy-start | bytes 2359300
  6.5 42.6 %all-gather.5.cloned.1.call-start = ((), (), s32[]{:S(2)}) async-start(), calls=%async_computation.5 | async-start | bytes 1327104 | tf_op jit(solution)/shard_map/all_gather | solution.py:213
  10.4 13.6 %all-to-all-start = ((bf16[8,8,3200]{2,1,0:T(8,128)(2,1)}), bf16[8,8,3200]{2,1,0:T(8,128)(2,1)S(1)}, u32[]{:S(2)}, u32[]{:S(2)}) async-start(bf16[8,8,3200]{2,1,0:T(8,128)(2,1)} %broadcast_in_dim.35), calls=%async_computation | async-start | bytes 819200 | tf_op jit(solution)/shard_map/all_to_all | solution.py:222
  17.5 6.5 %copy-start.1 = (f32[3072]{0:T(1024)S(1)}, f32[3072]{0:T(1024)}, u32[]{:S(2)}) copy-start(f32[3072]{0:T(1024)} %param.11) | copy-start | bytes 36868
  27.5 23.4 %all-to-all-start.1 = ((bf16[8,128,256]{2,1,0:T(8,128)(2,1)}), bf16[8,128,256]{2,1,0:T(8,128)(2,1)S(1)}, u32[]{:S(2)}, u32[]{:S(2)}) async-start(bf16[8,128,256]{2,1,0:T(8,128)(2,1)} %get-tuple-element.14), calls=%async_computation.1 | async-start | bytes 1048576 | tf_op jit(solution)/shard_map/all_to_all | solution.py:262
  35.3 57.1 %all-gather.7.cloned.1.call-start = ((), (), s32[]{:S(2)}) async-start(), calls=%async_computation.6 | async-start | bytes 2506752 | tf_op jit(solution)/shard_map/all_gather | solution.py:264
  35.4 1.7 %copy-start = (bf16[3072,384]{1,0:T(8,128)(2,1)S(1)}, bf16[3072,384]{1,0:T(8,128)(2,1)}, u32[]{:S(2)}) copy-start(bf16[3072,384]{1,0:T(8,128)(2,1)} %w_ref.1) | copy-start | bytes 7077892
  50.9 18.1 %all-to-all-start.2 = ((bf16[4,128,384]{2,1,0:T(8,128)(2,1)}), bf16[4,128,384]{2,1,0:T(8,128)(2,1)S(1)}, u32[]{:S(2)}, u32[]{:S(2)}) async-start(bf16[4,128,384]{2,1,0:T(8,128)(2,1)} %q.1), calls=%async_computation.2 | async-start | bytes 786432 | tf_op jit(solution)/shard_map/all_to_all | solution.py:266
  60.1 6.5 %collective-permute-start = (bf16[8,128,256]{2,1,0:T(8,128)(2,1)S(1)}, bf16[8,128,256]{2,1,0:T(8,128)(2,1)S(1)}, u32[]{:S(2)}, u32[]{:S(2)}) collective-permute-start(bf16[8,128,256]{2,1,0:T(8,128)(2,1)S(1)} %all-to-all-done.1.near_ref), channel_id=1, source_target_pairs={{1,0},{0,1},{3,2},{2,3},{5,4},{4,5},{7,6},{6,7},{9,8},{8,9},{11,10... | collective-permute-start | bytes 1572872 | tf_op jit(solution)/shard_map/ppermute | solution.py:267
Sparse Core Ops, SparseCore 0:
  9.5 39.6 all-gather.4
  51.2 41.0 all-gather.6

commit v8 on v6

--- a/solution.py
+++ b/solution.py
@@ -36,6 +36,18 @@
     angles = positions.astype(F32)[:, None] * inverse[None, :]
     cosine, sine = jnp.cos(angles), jnp.sin(angles)
     return jnp.concatenate([cosine, cosine], axis=1), jnp.concatenate([-sine, sine], axis=1)
+
+
+def tag_kernel(img_ref, slot_ref, out_ref):
+    count, width = img_ref.shape
+    row = lax.broadcasted_iota(jnp.int32, (count, count), 0)
+    own = row == lax.broadcasted_iota(jnp.int32, (count, count), 1)
+    slots = jnp.where(own, slot_ref[...].astype(F32), 0.0).sum(axis=1, keepdims=True)
+    lane = lax.broadcasted_iota(jnp.int32, (count, HEAD), 1)
+    tags = jnp.where(lane == 0, slots, jnp.where(lane == 1, 1.0, 0.0)).astype(BF16)
+    for i in range(out_ref.shape[0]):
+        out_ref[i, :, :width] = img_ref[...]
+        out_ref[i, :, width:] = tags
 
 
 def rope(v, table_ref):
@@ -215,19 +227,21 @@
         w_near, (0, c, 0, 0, 0), (n_z, 1, 1, *w_turned.shape)
     ).reshape(n_z, *w_turned.shape)
 
-    slots = image_slots.reshape(-1, 1).astype(BF16)
-    tagged = jnp.pad(image_rows[0, 0], ((0, 0), (0, HEAD)))
-    lane = lax.broadcasted_iota(jnp.int32, tagged.shape, 1)
-    tagged = jnp.where(lane == width, slots, jnp.where(lane == width + 1, jnp.ones_like(slots), tagged))
-    images = lax.all_to_all(
-        jnp.broadcast_to(tagged[None], (n_uly, *tagged.shape)), "uly", 0, 0, tiled=True
-    ).reshape(-1, width + HEAD)
+    vmem = pl.BlockSpec(memory_space=pltpu.VMEM)
+    tagged = pl.pallas_call(
+        tag_kernel,
+        out_shape=jax.ShapeDtypeStruct((n_uly, image_rows.shape[2], width + HEAD), BF16),
+        in_specs=[vmem] * 2,
+        out_specs=vmem,
+        compiler_params=pltpu.CompilerParams(vmem_limit_bytes=60 << 20),
+        name="tag",
+    )(image_rows[0, 0], image_slots[0])
+    images = lax.all_to_all(tagged, "uly", 0, 0, tiled=True).reshape(-1, width + HEAD)
 
     block = (y * n_z + z) * n_c + c
     cosine, sine = rope_tables(block * block_len + jnp.arange(block_len, dtype=jnp.int32))
     table = jnp.concatenate([cosine, sine], axis=1)
     w_kv = jnp.concatenate([key_matrix, value_matrix], axis=1)
-    vmem = pl.BlockSpec(memory_space=pltpu.VMEM)
     hbm = pl.BlockSpec(memory_space=pltpu.HBM)
     rows = heads * block_len
     normed, key_value, own = pl.pallas_call(

time: 120 us -> 120 us (level)
  Pallas kernels: 13.2 us -> 14.8 us
  other arithmetic: 4.07 us -> 2.53 us
  waiting for transfers between devices: 23.2 us -> 24.5 us
    pallas_call x0 -> x1, Pallas kernels: none -> 1.65 us  [body(): pl.pallas_call(tag_kernel, out_shape=jax.ShapeDtypeStruct((n_uly, image_r...]
  transfers between devices with their start and end apart: 6 -> 6, of which waited for: 6 -> 5; matrix products, arithmetic and copies ran while one was open for 5% -> 3% of each run, Pallas kernels for 9% -> 10%
where the time goes in v8:
time: 120 us
  blocking collectives  31.1 us (26%)
  starting transfers between devices  28.4 us (24%)
  waiting for transfers between devices  24.5 us (20%)
  Pallas kernels  14.8 us (12%)
  between operations  13.5 us (11%)
  local copies, waits for them, and re-layouts  4.77 us (4%)
  other arithmetic  2.53 us (2%)
    all_to_all x1, blocking collectives, body(): lax.all_to_all(projected.reshape(n_uly, own_len, width), 'uly', 0, 0, til...  16.8 us
    all_to_all x1, blocking collectives, body(): parts = lax.all_to_all(partial, BLK[1], 0, 0, tiled=True)  14.3 us
    all_gather x1, waiting for transfers between devices, body(): lax.all_gather(repeated, BLK[1:], axis=0, tiled=False)  11 us
    all_to_all x1, starting transfers between devices, body(): asked = lax.all_to_all(queries, BLK[1], 0, 0, tiled=True)  8.73 us
    all_to_all x1, starting transfers between devices, body(): near = lax.all_to_all(key_value, BLK[0], 0, 0, tiled=True)  7.85 us
    all_to_all x1, starting transfers between devices, body(): lax.all_to_all(tagged, 'uly', 0, 0, tiled=True).reshape(-1, width + HEAD)  6.66 us
    pallas_call x1, Pallas kernels, body(): pl.pallas_call(attend_kernel, out_shape=(jax.ShapeDtypeStruct((n_z, rows...  5.46 us
    all_to_all x1, waiting for transfers between devices, body(): lax.all_to_all(tagged, 'uly', 0, 0, tiled=True).reshape(-1, width + HEAD)  5.12 us
  transfers between devices with their start and end apart: 6, of which 5 were waited for; matrix products, arithmetic and copies ran while one was open for 3% of the time, Pallas kernels for 10%

profile of v8, /device:TPU:1, one launch (start us, length us, event | category | flops | bytes accessed | tf_op | source)
XLA Modules:
  0.0 119.6 jit_solution(6960494990581987353)
XLA Ops:
  6.5 1.5 %broadcast_in_dim.7 = bf16[4,48,384]{2,1,0:T(8,128)(2,1)} broadcast(bf16[48,384]{1,0:T(8,128)(2,1)} %bitcast.19), dimensions={1,2} | broadcast | bytes 184320 | tf_op jit(solution)/shard_map/broadcast_in_dim | solution.py:224
  8.1 1.6 %tag.1 = bf16[8,8,3200]{2,1,0:T(8,128)(2,1)} custom-call(bf16[8,3072]{1,0:T(8,128)(2,1)} %bitcast.18, s32[1,8]{1,0:T(1,128)} %bitcast.21), custom_call_target="tpu_custom_call" | custom-call | tf_op jit(solution)/shard_map/tag/pallas_call | solution.py:231
  9.7 6.7 %all-to-all-start = ((bf16[8,8,3200]{2,1,0:T(8,128)(2,1)}), bf16[8,8,3200]{2,1,0:T(8,128)(2,1)S(1)}, u32[]{:S(2)}, u32[]{:S(2)}) async-start(bf16[8,8,3200]{2,1,0:T(8,128)(2,1)} %tag.1), calls=%async_computation | async-start | bytes 819200 | tf_op jit(solution)/shard_map/all_to_all | solution.py:239
  16.4 0.3 multiply_cosine_fusion
  16.7 0.1 pad_maximum_fusion.1.table_ref
  16.9 1.3 %pad_maximum_fusion.w_ref = bf16[3072,256]{1,0:T(8,128)(2,1)S(1)} fusion(bf16[3072,128]{1,0:T(8,128)(2,1)S(1)} %copy-done.2, bf16[3072,128]{1,0:T(8,128)(2,1)} %param.13), kind=kLoop, calls=%fused_computation | loop fusion | flops 3145728 | bytes 3145728 | tf_op jit(solution)/shard_map/concatenate | solution.py:244
  18.2 5.1 %all-to-all-done = bf16[8,8,3200]{2,1,0:T(8,128)(2,1)S(1)} async-done(((bf16[8,8,3200]{2,1,0:T(8,128)(2,1)}), bf16[8,8,3200]{2,1,0:T(8,128)(2,1)S(1)}, u32[]{:S(2)}, u32[]{:S(2)}) %all-to-all-start) | async-done | bytes 409632 | tf_op jit(solution)/shard_map/all_to_all | solution.py:239
  23.3 3.5 %kv.1 = (bf16[128,3072]{1,0:T(8,128)(2,1)S(1)}, bf16[8,128,256]{2,1,0:T(8,128)(2,1)}, f32[16,3072]{1,0:T(8,128)S(1)}) custom-call(bf16[64,3200]{1,0:T(8,128)(2,1)S(1)} %bitcast.14, bf16[128,3072]{1,0:T(8,128)(2,1)} %bitcast.17, f32[1,3072]{1,0:T(1,128)S(1)} %bitcast.15, f32[128,256]{1,0:T(8,128)S(1)} %pad_maximum_fusion.1.table_ref, ...), custom_call_target="tpu_custom_call" | custom-call | tf_op jit(solution)/shard_map/kv/pallas_call | solution.py:247
  26.8 7.8 %all-to-all-start.1 = ((bf16[8,128,256]{2,1,0:T(8,128)(2,1)}), bf16[8,128,256]{2,1,0:T(8,128)(2,1)S(1)}, u32[]{:S(2)}, u32[]{:S(2)}) async-start(bf16[8,128,256]{2,1,0:T(8,128)(2,1)} %get-tuple-element.14), calls=%async_computation.1 | async-start | bytes 1048576 | tf_op jit(solution)/shard_map/all_to_all | solution.py:276
  34.7 1.7 %copy-done = bf16[3072,384]{1,0:T(8,128)(2,1)S(1)} copy-done((bf16[3072,384]{1,0:T(8,128)(2,1)S(1)}, bf16[3072,384]{1,0:T(8,128)(2,1)}, u32[]{:S(2)}) %copy-start) | copy-done | bytes 2359320
  36.3 1.6 %q.1 = bf16[4,128,384]{2,1,0:T(8,128)(2,1)} custom-call(bf16[128,3072]{1,0:T(8,128)(2,1)S(1)} %get-tuple-element.15.normed_ref, f32[128,256]{1,0:T(8,128)S(1)} %pad_maximum_fusion.1.table_ref, bf16[3072,384]{1,0:T(8,128)(2,1)S(1)} %copy-done), custom_call_target="tpu_custom_call" | custom-call | flops 301989888 | bytes 2359296 | tf_op jit(solution)/shard_map/q/pallas_call | solution.py:264
  37.9 11.0 %all-gather.5.cloned.1.call-done = bf16[32,48,384]{2,1,0:T(8,128)(2,1)} async-done(((bf16[4,48,384]{2,1,0:T(8,128)(2,1)}), bf16[32,48,384]{2,1,0:T(8,128)(2,1)}) %all-gather.5.cloned.1.call-update) | async-done | bytes 1179664 | tf_op jit(solution)/shard_map/all_gather | solution.py:225
  49.0 1.6 %dynamic-slice_bitcast_fusion = bf16[4,48,384]{2,1,0:T(8,128)(2,1)} fusion(bf16[4,2,4,48,384]{4,3,2,1,0:T(8,128)(2,1)} %bitcast.20, s32[]{:T(128)S(6)} %select_n.3), kind=kLoop, calls=%fused_computation.3 | loop fusion | bytes 294916 | tf_op jit(solution)/shard_map/reshape | solution.py:226
  50.6 8.7 %all-to-all-start.2 = ((bf16[4,128,384]{2,1,0:T(8,128)(2,1)}), bf16[4,128,384]{2,1,0:T(8,128)(2,1)S(1)}, u32[]{:S(2)}, u32[]{:S(2)}) async-start(bf16[4,128,384]{2,1,0:T(8,128)(2,1)} %q.1), calls=%async_computation.2 | async-start | bytes 786432 | tf_op jit(solution)/shard_map/all_to_all | solution.py:280
  59.3 5.1 %collective-permute-start = (bf16[8,128,256]{2,1,0:T(8,128)(2,1)S(1)}, bf16[8,128,256]{2,1,0:T(8,128)(2,1)S(1)}, u32[]{:S(2)}, u32[]{:S(2)}) collective-permute-start(bf16[8,128,256]{2,1,0:T(8,128)(2,1)S(1)} %all-to-all-done.1.near_ref), channel_id=1, source_target_pairs={{1,0},{0,1},{3,2},{2,3},{5,4},{4,5},{7,6},{6,7},{9,8},{8,9},{11,10... | collective-permute-start | bytes 1572872 | tf_op jit(solution)/shard_map/ppermute | solution.py:281
  64.4 1.5 %collective-permute-done.far_ref = bf16[8,128,256]{2,1,0:T(8,128)(2,1)S(1)} collective-permute-done((bf16[8,128,256]{2,1,0:T(8,128)(2,1)S(1)}, bf16[8,128,256]{2,1,0:T(8,128)(2,1)S(1)}, u32[]{:S(2)}, u32[]{:S(2)}) %collective-permute-start) | collective-permute-done | bytes 524320 | tf_op jit(solution)/shard_map/ppermute | solution.py:281
  65.9 2.4 %all-to-all-done.2.q_ref = bf16[4,128,384]{2,1,0:T(8,128)(2,1)S(1)} async-done(((bf16[4,128,384]{2,1,0:T(8,128)(2,1)}), bf16[4,128,384]{2,1,0:T(8,128)(2,1)S(1)}, u32[]{:S(2)}, u32[]{:S(2)}) %all-to-all-start.2) | async-done | bytes 393248 | tf_op jit(solution)/shard_map/all_to_all | solution.py:280
  68.3 5.5 %attend.1 = (bf16[4,400,128]{2,1,0:T(8,128)(2,1)S(1)}, f32[384,128]{1,0:T(8,128)S(1)}) custom-call(bf16[4,128,384]{2,1,0:T(8,128)(2,1)S(1)} %all-to-all-done.2.q_ref, bf16[8,128,256]{2,1,0:T(8,128)(2,1)S(1)} %all-to-all-done.1.near_ref, bf16[8,128,256]{2,1,0:T(8,128)(2,1)S(1)} %collective-permute-done.far_ref), custom_call_target="tpu_custom_call" | custom-call | tf_op jit(solution)/shard_map/attend/pallas_call | solution.py:283
  73.8 14.3 %all_to_all.25.o_ref = bf16[4,400,128]{2,1,0:T(8,128)(2,1)S(1)} all-to-all(bf16[4,400,128]{2,1,0:T(8,128)(2,1)S(1)} %get-tuple-element.18), channel_id=1, replica_groups=mesh['uly'=8,'blk_y'=8,'blk_z'=4,'blk_c'=2] {'blk_z'}, dimensions={0} | all-to-all | bytes 819200 | tf_op jit(solution)/shard_map/all_to_all | solution.py:296
  88.1 4.4 %all-gather.7.cloned.1.call-done = bf16[64,48,384]{2,1,0:T(8,128)(2,1)} async-done(((bf16[4,48,384]{2,1,0:T(8,128)(2,1)}), bf16[64,48,384]{2,1,0:T(8,128)(2,1)}) %all-gather.7.cloned.1.call-update) | async-done | bytes 2359312 | tf_op jit(solution)/shard_map/all_gather | solution.py:278
  92.4 2.7 %project.1 = bf16[128,3072]{1,0:T(8,128)(2,1)S(1)} custom-call(bf16[4,400,128]{2,1,0:T(8,128)(2,1)S(1)} %all_to_all.25.o_ref, f32[384,128]{1,0:T(8,128)S(1)} %get-tuple-element.19.mine_ref, bf16[8,2,4,48,384]{4,3,2,1,0:T(8,128)(2,1)} %bitcast.16), custom_call_target="tpu_custom_call" | custom-call | tf_op jit(solution)/shard_map/project/pallas_call | solution.py:297
  95.1 16.8 %all_to_all.26 = bf16[8,16,3072]{2,1,0:T(8,128)(2,1)S(1)} all-to-all(bf16[8,16,3072]{2,1,0:T(8,128)(2,1)S(1)} %bitcast.13), channel_id=1, replica_groups=mesh['uly'=8,'blk_y'=8,'blk_z'=4,'blk_c'=2] {'uly'}, dimensions={0} | all-to-all | bytes 1572864 | tf_op jit(solution)/shard_map/all_to_all | solution.py:311
  112.0 0.1 convert_reduce_fusion
  112.1 0.7 fusion
  (12 shorter events, 0.1 us)
Async XLA Ops:
  6.5 10.3 %copy-start.2 = (bf16[3072,128]{1,0:T(8,128)(2,1)S(1)}, bf16[3072,128]{1,0:T(8,128)(2,1)}, u32[]{:S(2)}) copy-start(bf16[3072,128]{1,0:T(8,128)(2,1)} %param.14) | copy-start | bytes 2359300
  6.5 42.4 %all-gather.5.cloned.1.call-start = ((), (), s32[]{:S(2)}) async-start(), calls=%async_computation.5 | async-start | bytes 1327104 | tf_op jit(solution)/shard_map/all_gather | solution.py:225
  9.7 13.6 %all-to-all-start = ((bf16[8,8,3200]{2,1,0:T(8,128)(2,1)}), bf16[8,8,3200]{2,1,0:T(8,128)(2,1)S(1)}, u32[]{:S(2)}, u32[]{:S(2)}) async-start(bf16[8,8,3200]{2,1,0:T(8,128)(2,1)} %tag.1), calls=%async_computation | async-start | bytes 819200 | tf_op jit(solution)/shard_map/all_to_all | solution.py:239
  16.8 6.5 %copy-start.1 = (f32[3072]{0:T(1024)S(1)}, f32[3072]{0:T(1024)}, u32[]{:S(2)}) copy-start(f32[3072]{0:T(1024)} %param.11) | copy-start | bytes 36868
  26.8 23.8 %all-to-all-start.1 = ((bf16[8,128,256]{2,1,0:T(8,128)(2,1)}), bf16[8,128,256]{2,1,0:T(8,128)(2,1)S(1)}, u32[]{:S(2)}, u32[]{:S(2)}) async-start(bf16[8,128,256]{2,1,0:T(8,128)(2,1)} %get-tuple-element.14), calls=%async_computation.1 | async-start | bytes 1048576 | tf_op jit(solution)/shard_map/all_to_all | solution.py:276
  34.6 57.8 %all-gather.7.cloned.1.call-start = ((), (), s32[]{:S(2)}) async-start(), calls=%async_computation.6 | async-start | bytes 2506752 | tf_op jit(solution)/shard_map/all_gather | solution.py:278
  34.7 1.7 %copy-start = (bf16[3072,384]{1,0:T(8,128)(2,1)S(1)}, bf16[3072,384]{1,0:T(8,128)(2,1)}, u32[]{:S(2)}) copy-start(bf16[3072,384]{1,0:T(8,128)(2,1)} %w_ref.1) | copy-start | bytes 7077892
  50.6 17.7 %all-to-all-start.2 = ((bf16[4,128,384]{2,1,0:T(8,128)(2,1)}), bf16[4,128,384]{2,1,0:T(8,128)(2,1)S(1)}, u32[]{:S(2)}, u32[]{:S(2)}) async-start(bf16[4,128,384]{2,1,0:T(8,128)(2,1)} %q.1), calls=%async_computation.2 | async-start | bytes 786432 | tf_op jit(solution)/shard_map/all_to_all | solution.py:280
  59.3 6.6 %collective-permute-start = (bf16[8,128,256]{2,1,0:T(8,128)(2,1)S(1)}, bf16[8,128,256]{2,1,0:T(8,128)(2,1)S(1)}, u32[]{:S(2)}, u32[]{:S(2)}) collective-permute-start(bf16[8,128,256]{2,1,0:T(8,128)(2,1)S(1)} %all-to-all-done.1.near_ref), channel_id=1, source_target_pairs={{1,0},{0,1},{3,2},{2,3},{5,4},{4,5},{7,6},{6,7},{9,8},{8,9},{11,10... | collective-permute-start | bytes 1572872 | tf_op jit(solution)/shard_map/ppermute | solution.py:281
Sparse Core Ops, SparseCore 0:
  9.5 39.4 all-gather.4
  51.1 41.3 all-gather.6

commit v9 on v8

--- a/solution.py
+++ b/solution.py
@@ -38,7 +38,9 @@
     return jnp.concatenate([cosine, cosine], axis=1), jnp.concatenate([-sine, sine], axis=1)
 
 
-def tag_kernel(img_ref, slot_ref, out_ref):
+def tag_kernel(img_ref, slot_ref, w_ref, out_ref, again_ref):
+    for i in range(again_ref.shape[0]):
+        again_ref[i] = w_ref[...]
     count, width = img_ref.shape
     row = lax.broadcasted_iota(jnp.int32, (count, count), 0)
     own = row == lax.broadcasted_iota(jnp.int32, (count, count), 1)
@@ -221,21 +223,22 @@
     heads = q_width // HEAD
     y, z, c = (lax.axis_index(a) for a in BLK)
     w_turned = w_out.T
-    repeated = lax.optimization_barrier(jnp.broadcast_to(w_turned[None], (W_REPEATS, *w_turned.shape)))
+    vmem = pl.BlockSpec(memory_space=pltpu.VMEM)
+    tagged, repeated = pl.pallas_call(
+        tag_kernel,
+        out_shape=(
+            jax.ShapeDtypeStruct((n_uly, image_rows.shape[2], width + HEAD), BF16),
+            jax.ShapeDtypeStruct((W_REPEATS, *w_turned.shape), BF16),
+        ),
+        in_specs=[vmem] * 3,
+        out_specs=[vmem] * 2,
+        compiler_params=pltpu.CompilerParams(vmem_limit_bytes=60 << 20),
+        name="tag",
+    )(image_rows[0, 0], image_slots[0], w_turned)
     w_near = lax.all_gather(repeated, BLK[1:], axis=0, tiled=False).reshape(n_z, n_c, W_REPEATS, *w_turned.shape)
     w_near = lax.dynamic_slice(
         w_near, (0, c, 0, 0, 0), (n_z, 1, 1, *w_turned.shape)
     ).reshape(n_z, *w_turned.shape)
-
-    vmem = pl.BlockSpec(memory_space=pltpu.VMEM)
-    tagged = pl.pallas_call(
-        tag_kernel,
-        out_shape=jax.ShapeDtypeStruct((n_uly, image_rows.shape[2], width + HEAD), BF16),
-        in_specs=[vmem] * 2,
-        out_specs=vmem,
-        compiler_params=pltpu.CompilerParams(vmem_limit_bytes=60 << 20),
-        name="tag",
-    )(image_rows[0, 0], image_slots[0])
     images = lax.all_to_all(tagged, "uly", 0, 0, tiled=True).reshape(-1, width + HEAD)
 
     block = (y * n_z + z) * n_c + c

time: 120 us -> 120 us (level)
  waiting for transfers between devices: 24.5 us -> 27.2 us
  local copies, waits for them, and re-layouts: 4.77 us -> 3.26 us
  starting transfers between devices: 28.4 us -> 26.9 us
    all_gather x1, waiting for transfers between devices: 11 us -> 12.6 us  [body(): lax.all_gather(repeated, BLK[1:], axis=0, tiled=False)]
    broadcast_in_dim x1 -> x0, local copies, waits for them, and re-layouts: 1.51 us -> none  [body(): jnp.broadcast_to(w_turned[None], (W_REPEATS, *w_turned.shape))]
    all_to_all x1, starting transfers between devices: 8.73 us -> 7.25 us  [body(): asked = lax.all_to_all(queries, BLK[1], 0, 0, tiled=True)]
  transfers between devices with their start and end apart: 6 -> 6, of which waited for: 5 -> 5; matrix products, arithmetic and copies ran while one was open for 3% -> 3% of each run, Pallas kernels for 10% -> 9%
where the time goes in v9:
time: 120 us
  blocking collectives  31.4 us (26%)
  waiting for transfers between devices  27.2 us (23%)
  starting transfers between devices  26.9 us (22%)
  Pallas kernels  14.9 us (12%)
  between operations  13.5 us (11%)
  local copies, waits for them, and re-layouts  3.26 us (3%)
  other arithmetic  2.53 us (2%)
    all_to_all x1, blocking collectives, body(): lax.all_to_all(projected.reshape(n_uly, own_len, width), 'uly', 0, 0, til...  17.2 us
    all_to_all x1, blocking collectives, body(): parts = lax.all_to_all(partial, BLK[1], 0, 0, tiled=True)  14.3 us
    all_gather x1, waiting for transfers between devices, body(): lax.all_gather(repeated, BLK[1:], axis=0, tiled=False)  12.6 us
    all_to_all x1, starting transfers between devices, body(): near = lax.all_to_all(key_value, BLK[0], 0, 0, tiled=True)  7.85 us
    all_to_all x1, starting transfers between devices, body(): asked = lax.all_to_all(queries, BLK[1], 0, 0, tiled=True)  7.25 us
    all_to_all x1, starting transfers between devices, body(): lax.all_to_all(tagged, 'uly', 0, 0, tiled=True).reshape(-1, width + HEAD)  6.67 us
    all_gather x1, waiting for transfers between devices, body(): w_all = lax.all_gather(w_near, (BLK[0], BLK[2]), axis=0, tiled=False)  5.57 us
    pallas_call x1, Pallas kernels, body(): pl.pallas_call(attend_kernel, out_shape=(jax.ShapeDtypeStruct((n_z, rows...  5.46 us
  transfers between devices with their start and end apart: 6, of which 5 were waited for; matrix products, arithmetic and copies ran while one was open for 3% of the time, Pallas kernels for 9%

profile of v9, /device:TPU:1, one launch (start us, length us, event | category | flops | bytes accessed | tf_op | source)
XLA Modules:
  0.0 119.7 jit_solution(5040230676007542471)
XLA Ops:
  6.5 1.7 %tag.1 = (bf16[8,8,3200]{2,1,0:T(8,128)(2,1)}, bf16[4,48,384]{2,1,0:T(8,128)(2,1)}) custom-call(bf16[8,3072]{1,0:T(8,128)(2,1)} %bitcast.18, s32[1,8]{1,0:T(1,128)} %bitcast.21, bf16[48,384]{1,0:T(8,128)(2,1)} %bitcast.19), custom_call_target="tpu_custom_call" | custom-call | tf_op jit(solution)/shard_map/tag/pallas_call | solution.py:227
  8.3 6.7 %all-to-all-start = ((bf16[8,8,3200]{2,1,0:T(8,128)(2,1)}), bf16[8,8,3200]{2,1,0:T(8,128)(2,1)S(1)}, u32[]{:S(2)}, u32[]{:S(2)}) async-start(bf16[8,8,3200]{2,1,0:T(8,128)(2,1)} %get-tuple-element.15), calls=%async_computation | async-start | bytes 819200 | tf_op jit(solution)/shard_map/all_to_all | solution.py:242
  15.0 0.3 multiply_cosine_fusion
  15.3 0.1 pad_maximum_fusion.1.table_ref
  15.5 1.3 %pad_maximum_fusion.w_ref = bf16[3072,256]{1,0:T(8,128)(2,1)S(1)} fusion(bf16[3072,128]{1,0:T(8,128)(2,1)S(1)} %copy-done.2, bf16[3072,128]{1,0:T(8,128)(2,1)} %param.13), kind=kLoop, calls=%fused_computation | loop fusion | flops 3145728 | bytes 3145728 | tf_op jit(solution)/shard_map/concatenate | solution.py:247
  16.8 5.1 %all-to-all-done = bf16[8,8,3200]{2,1,0:T(8,128)(2,1)S(1)} async-done(((bf16[8,8,3200]{2,1,0:T(8,128)(2,1)}), bf16[8,8,3200]{2,1,0:T(8,128)(2,1)S(1)}, u32[]{:S(2)}, u32[]{:S(2)}) %all-to-all-start) | async-done | bytes 409632 | tf_op jit(solution)/shard_map/all_to_all | solution.py:242
  21.9 3.5 %kv.1 = (bf16[128,3072]{1,0:T(8,128)(2,1)S(1)}, bf16[8,128,256]{2,1,0:T(8,128)(2,1)}, f32[16,3072]{1,0:T(8,128)S(1)}) custom-call(bf16[64,3200]{1,0:T(8,128)(2,1)S(1)} %bitcast.14, bf16[128,3072]{1,0:T(8,128)(2,1)} %bitcast.17, f32[1,3072]{1,0:T(1,128)S(1)} %bitcast.15, f32[128,256]{1,0:T(8,128)S(1)} %pad_maximum_fusion.1.table_ref, ...), custom_call_target="tpu_custom_call" | custom-call | tf_op jit(solution)/shard_map/kv/pallas_call | solution.py:250
  25.4 7.9 %all-to-all-start.1 = ((bf16[8,128,256]{2,1,0:T(8,128)(2,1)}), bf16[8,128,256]{2,1,0:T(8,128)(2,1)S(1)}, u32[]{:S(2)}, u32[]{:S(2)}) async-start(bf16[8,128,256]{2,1,0:T(8,128)(2,1)} %get-tuple-element.17), calls=%async_computation.1 | async-start | bytes 1048576 | tf_op jit(solution)/shard_map/all_to_all | solution.py:279
  33.2 0.0 all-gather.7.cloned.1.call-start
  33.3 1.7 %copy-done = bf16[3072,384]{1,0:T(8,128)(2,1)S(1)} copy-done((bf16[3072,384]{1,0:T(8,128)(2,1)S(1)}, bf16[3072,384]{1,0:T(8,128)(2,1)}, u32[]{:S(2)}) %copy-start) | copy-done | bytes 2359320
  34.9 1.6 %q.1 = bf16[4,128,384]{2,1,0:T(8,128)(2,1)} custom-call(bf16[128,3072]{1,0:T(8,128)(2,1)S(1)} %get-tuple-element.19.normed_ref, f32[128,256]{1,0:T(8,128)S(1)} %pad_maximum_fusion.1.table_ref, bf16[3072,384]{1,0:T(8,128)(2,1)S(1)} %copy-done), custom_call_target="tpu_custom_call" | custom-call | flops 301989888 | bytes 2359296 | tf_op jit(solution)/shard_map/q/pallas_call | solution.py:267
  36.5 12.6 %all-gather.5.cloned.1.call-done = bf16[32,48,384]{2,1,0:T(8,128)(2,1)} async-done(((bf16[4,48,384]{2,1,0:T(8,128)(2,1)}), bf16[32,48,384]{2,1,0:T(8,128)(2,1)}) %all-gather.5.cloned.1.call-update) | async-done | bytes 1179664 | tf_op jit(solution)/shard_map/all_gather | solution.py:238
  49.1 1.6 %dynamic-slice_bitcast_fusion = bf16[4,48,384]{2,1,0:T(8,128)(2,1)} fusion(bf16[4,2,4,48,384]{4,3,2,1,0:T(8,128)(2,1)} %bitcast.20, s32[]{:T(128)S(6)} %select_n.3), kind=kLoop, calls=%fused_computation.3 | loop fusion | bytes 294916 | tf_op jit(solution)/shard_map/reshape | solution.py:239
  50.7 7.2 %all-to-all-start.2 = ((bf16[4,128,384]{2,1,0:T(8,128)(2,1)}), bf16[4,128,384]{2,1,0:T(8,128)(2,1)S(1)}, u32[]{:S(2)}, u32[]{:S(2)}) async-start(bf16[4,128,384]{2,1,0:T(8,128)(2,1)} %q.1), calls=%async_computation.2 | async-start | bytes 786432 | tf_op jit(solution)/shard_map/all_to_all | solution.py:283
  57.9 5.1 %collective-permute-start = (bf16[8,128,256]{2,1,0:T(8,128)(2,1)S(1)}, bf16[8,128,256]{2,1,0:T(8,128)(2,1)S(1)}, u32[]{:S(2)}, u32[]{:S(2)}) collective-permute-start(bf16[8,128,256]{2,1,0:T(8,128)(2,1)S(1)} %all-to-all-done.1.near_ref), channel_id=1, source_target_pairs={{1,0},{0,1},{3,2},{2,3},{5,4},{4,5},{7,6},{6,7},{9,8},{8,9},{11,10... | collective-permute-start | bytes 1572872 | tf_op jit(solution)/shard_map/ppermute | solution.py:284
  63.0 1.5 %collective-permute-done.far_ref = bf16[8,128,256]{2,1,0:T(8,128)(2,1)S(1)} collective-permute-done((bf16[8,128,256]{2,1,0:T(8,128)(2,1)S(1)}, bf16[8,128,256]{2,1,0:T(8,128)(2,1)S(1)}, u32[]{:S(2)}, u32[]{:S(2)}) %collective-permute-start) | collective-permute-done | bytes 524320 | tf_op jit(solution)/shard_map/ppermute | solution.py:284
  64.5 2.4 %all-to-all-done.2.q_ref = bf16[4,128,384]{2,1,0:T(8,128)(2,1)S(1)} async-done(((bf16[4,128,384]{2,1,0:T(8,128)(2,1)}), bf16[4,128,384]{2,1,0:T(8,128)(2,1)S(1)}, u32[]{:S(2)}, u32[]{:S(2)}) %all-to-all-start.2) | async-done | bytes 393248 | tf_op jit(solution)/shard_map/all_to_all | solution.py:283
  66.9 5.5 %attend.1 = (bf16[4,400,128]{2,1,0:T(8,128)(2,1)S(1)}, f32[384,128]{1,0:T(8,128)S(1)}) custom-call(bf16[4,128,384]{2,1,0:T(8,128)(2,1)S(1)} %all-to-all-done.2.q_ref, bf16[8,128,256]{2,1,0:T(8,128)(2,1)S(1)} %all-to-all-done.1.near_ref, bf16[8,128,256]{2,1,0:T(8,128)(2,1)S(1)} %collective-permute-done.far_ref), custom_call_target="tpu_custom_call" | custom-call | tf_op jit(solution)/shard_map/attend/pallas_call | solution.py:286
  72.4 14.3 %all_to_all.25.o_ref = bf16[4,400,128]{2,1,0:T(8,128)(2,1)S(1)} all-to-all(bf16[4,400,128]{2,1,0:T(8,128)(2,1)S(1)} %get-tuple-element.22), channel_id=1, replica_groups=mesh['uly'=8,'blk_y'=8,'blk_z'=4,'blk_c'=2] {'blk_z'}, dimensions={0} | all-to-all | bytes 819200 | tf_op jit(solution)/shard_map/all_to_all | solution.py:299
  86.6 5.6 %all-gather.7.cloned.1.call-done = bf16[64,48,384]{2,1,0:T(8,128)(2,1)} async-done(((bf16[4,48,384]{2,1,0:T(8,128)(2,1)}), bf16[64,48,384]{2,1,0:T(8,128)(2,1)}) %all-gather.7.cloned.1.call-update) | async-done | bytes 2359312 | tf_op jit(solution)/shard_map/all_gather | solution.py:281
  92.2 2.7 %project.1 = bf16[128,3072]{1,0:T(8,128)(2,1)S(1)} custom-call(bf16[4,400,128]{2,1,0:T(8,128)(2,1)S(1)} %all_to_all.25.o_ref, f32[384,128]{1,0:T(8,128)S(1)} %get-tuple-element.23.mine_ref, bf16[8,2,4,48,384]{4,3,2,1,0:T(8,128)(2,1)} %bitcast.16), custom_call_target="tpu_custom_call" | custom-call | tf_op jit(solution)/shard_map/project/pallas_call | solution.py:300
  94.9 17.2 %all_to_all.26 = bf16[8,16,3072]{2,1,0:T(8,128)(2,1)S(1)} all-to-all(bf16[8,16,3072]{2,1,0:T(8,128)(2,1)S(1)} %bitcast.13), channel_id=1, replica_groups=mesh['uly'=8,'blk_y'=8,'blk_z'=4,'blk_c'=2] {'uly'}, dimensions={0} | all-to-all | bytes 1572864 | tf_op jit(solution)/shard_map/all_to_all | solution.py:314
  112.1 0.1 convert_reduce_fusion
  112.2 0.7 fusion
  (11 shorter events, 0.1 us)
Async XLA Ops:
  6.5 8.9 %copy-start.2 = (bf16[3072,128]{1,0:T(8,128)(2,1)S(1)}, bf16[3072,128]{1,0:T(8,128)(2,1)}, u32[]{:S(2)}) copy-start(bf16[3072,128]{1,0:T(8,128)(2,1)} %param.14) | copy-start | bytes 2359300
  6.5 42.5 %all-gather.5.cloned.1.call-start = ((), (), s32[]{:S(2)}) async-start(), calls=%async_computation.5 | async-start | bytes 1327104 | tf_op jit(solution)/shard_map/all_gather | solution.py:238
  8.3 13.6 %all-to-all-start = ((bf16[8,8,3200]{2,1,0:T(8,128)(2,1)}), bf16[8,8,3200]{2,1,0:T(8,128)(2,1)S(1)}, u32[]{:S(2)}, u32[]{:S(2)}) async-start(bf16[8,8,3200]{2,1,0:T(8,128)(2,1)} %get-tuple-element.15), calls=%async_computation | async-start | bytes 819200 | tf_op jit(solution)/shard_map/all_to_all | solution.py:242
  15.4 6.5 %copy-start.1 = (f32[3072]{0:T(1024)S(1)}, f32[3072]{0:T(1024)}, u32[]{:S(2)}) copy-start(f32[3072]{0:T(1024)} %param.11) | copy-start | bytes 36868
  25.4 25.3 %all-to-all-start.1 = ((bf16[8,128,256]{2,1,0:T(8,128)(2,1)}), bf16[8,128,256]{2,1,0:T(8,128)(2,1)S(1)}, u32[]{:S(2)}, u32[]{:S(2)}) async-start(bf16[8,128,256]{2,1,0:T(8,128)(2,1)} %get-tuple-element.17), calls=%async_computation.1 | async-start | bytes 1048576 | tf_op jit(solution)/shard_map/all_to_all | solution.py:279
  33.2 59.0 %all-gather.7.cloned.1.call-start = ((), (), s32[]{:S(2)}) async-start(), calls=%async_computation.6 | async-start | bytes 2506752 | tf_op jit(solution)/shard_map/all_gather | solution.py:281
  33.3 1.7 %copy-start = (bf16[3072,384]{1,0:T(8,128)(2,1)S(1)}, bf16[3072,384]{1,0:T(8,128)(2,1)}, u32[]{:S(2)}) copy-start(bf16[3072,384]{1,0:T(8,128)(2,1)} %w_ref.1) | copy-start | bytes 7077892
  50.7 16.2 %all-to-all-start.2 = ((bf16[4,128,384]{2,1,0:T(8,128)(2,1)}), bf16[4,128,384]{2,1,0:T(8,128)(2,1)S(1)}, u32[]{:S(2)}, u32[]{:S(2)}) async-start(bf16[4,128,384]{2,1,0:T(8,128)(2,1)} %q.1), calls=%async_computation.2 | async-start | bytes 786432 | tf_op jit(solution)/shard_map/all_to_all | solution.py:283
  57.9 6.6 %collective-permute-start = (bf16[8,128,256]{2,1,0:T(8,128)(2,1)S(1)}, bf16[8,128,256]{2,1,0:T(8,128)(2,1)S(1)}, u32[]{:S(2)}, u32[]{:S(2)}) collective-permute-start(bf16[8,128,256]{2,1,0:T(8,128)(2,1)S(1)} %all-to-all-done.1.near_ref), channel_id=1, source_target_pairs={{1,0},{0,1},{3,2},{2,3},{5,4},{4,5},{7,6},{6,7},{9,8},{8,9},{11,10... | collective-permute-start | bytes 1572872 | tf_op jit(solution)/shard_map/ppermute | solution.py:284
Sparse Core Ops, SparseCore 0:
  9.5 39.5 all-gather.4
  51.2 40.9 all-gather.6

commit v10 on v9

--- a/solution.py
+++ b/solution.py
@@ -15,7 +15,7 @@
 CHUNK = 2
 STEPS = 4
 HIDE = 3.0e38
-W_REPEATS = 4
+REPEATED_ROWS = 176
 EXP2_SCALE = math.log2(math.e) / math.sqrt(HEAD)
 STAT_ROWS = 16
 F32 = jnp.float32
@@ -39,8 +39,10 @@
 
 
 def tag_kernel(img_ref, slot_ref, w_ref, out_ref, again_ref):
-    for i in range(again_ref.shape[0]):
-        again_ref[i] = w_ref[...]
+    piece = w_ref.shape[0]
+    for i in range(0, again_ref.shape[0], piece):
+        count_here = min(piece, again_ref.shape[0] - i)
+        again_ref[i : i + count_here, :] = w_ref[:count_here, :]
     count, width = img_ref.shape
     row = lax.broadcasted_iota(jnp.int32, (count, count), 0)
     own = row == lax.broadcasted_iota(jnp.int32, (count, count), 1)
@@ -228,16 +230,16 @@
         tag_kernel,
         out_shape=(
             jax.ShapeDtypeStruct((n_uly, image_rows.shape[2], width + HEAD), BF16),
-            jax.ShapeDtypeStruct((W_REPEATS, *w_turned.shape), BF16),
+            jax.ShapeDtypeStruct((REPEATED_ROWS, q_width), BF16),
         ),
         in_specs=[vmem] * 3,
         out_specs=[vmem] * 2,
         compiler_params=pltpu.CompilerParams(vmem_limit_bytes=60 << 20),
         name="tag",
     )(image_rows[0, 0], image_slots[0], w_turned)
-    w_near = lax.all_gather(repeated, BLK[1:], axis=0, tiled=False).reshape(n_z, n_c, W_REPEATS, *w_turned.shape)
+    w_near = lax.all_gather(repeated, BLK[1:], axis=0, tiled=False).reshape(n_z, n_c, REPEATED_ROWS, q_width)
     w_near = lax.dynamic_slice(
-        w_near, (0, c, 0, 0, 0), (n_z, 1, 1, *w_turned.shape)
+        w_near, (0, c, 0, 0), (n_z, 1, *w_turned.shape)
     ).reshape(n_z, *w_turned.shape)
     images = lax.all_to_all(tagged, "uly", 0, 0, tiled=True).reshape(-1, width + HEAD)
 

time: 120 us -> 120 us (level)
  no operation moved by 1% of the time
where the time goes in v10:
time: 120 us; the launch traced here: 119 us
  blocking collectives  31.3 us (26%)
  starting transfers between devices  27 us (22%)
  waiting for transfers between devices  26.3 us (22%)
  Pallas kernels  15 us (12%)
  between operations  13.5 us (11%)
  local copies, waits for them, and re-layouts  3.26 us (3%)
  other arithmetic  2.53 us (2%)
    all_to_all x1, blocking collectives, body(): lax.all_to_all(projected.reshape(n_uly, own_len, width), 'uly', 0, 0, til...  16.8 us
    all_to_all x1, blocking collectives, body(): parts = lax.all_to_all(partial, BLK[1], 0, 0, tiled=True)  14.4 us
    all_gather x1, waiting for transfers between devices, body(): lax.all_gather(repeated, BLK[1:], axis=0, tiled=False)  12.4 us
    all_to_all x1, starting transfers between devices, body(): near = lax.all_to_all(key_value, BLK[0], 0, 0, tiled=True)  7.85 us
    all_to_all x1, starting transfers between devices, body(): asked = lax.all_to_all(queries, BLK[1], 0, 0, tiled=True)  7.42 us
    all_to_all x1, starting transfers between devices, body(): lax.all_to_all(tagged, 'uly', 0, 0, tiled=True).reshape(-1, width + HEAD)  6.67 us
    pallas_call x1, Pallas kernels, body(): pl.pallas_call(attend_kernel, out_shape=(jax.ShapeDtypeStruct((n_z, rows...  5.46 us
    all_to_all x1, waiting for transfers between devices, body(): lax.all_to_all(tagged, 'uly', 0, 0, tiled=True).reshape(-1, width + HEAD)  5.13 us
  transfers between devices with their start and end apart: 6, of which 5 were waited for; matrix products, arithmetic and copies ran while one was open for 3% of the time, Pallas kernels for 9%

profile of v10, /device:TPU:1, one launch (start us, length us, event | category | flops | bytes accessed | tf_op | source)
XLA Modules:
  0.0 118.9 jit_solution(8662742106036736520)
XLA Ops:
  6.5 1.8 %tag.1 = (bf16[8,8,3200]{2,1,0:T(8,128)(2,1)}, bf16[176,384]{1,0:T(8,128)(2,1)}) custom-call(bf16[8,3072]{1,0:T(8,128)(2,1)} %bitcast.18, s32[1,8]{1,0:T(1,128)} %bitcast.21, bf16[48,384]{1,0:T(8,128)(2,1)} %bitcast.19), custom_call_target="tpu_custom_call" | custom-call | tf_op jit(solution)/shard_map/tag/pallas_call | solution.py:229
  8.3 6.7 %all-to-all-start = ((bf16[8,8,3200]{2,1,0:T(8,128)(2,1)}), bf16[8,8,3200]{2,1,0:T(8,128)(2,1)S(1)}, u32[]{:S(2)}, u32[]{:S(2)}) async-start(bf16[8,8,3200]{2,1,0:T(8,128)(2,1)} %get-tuple-element.15), calls=%async_computation | async-start | bytes 819200 | tf_op jit(solution)/shard_map/all_to_all | solution.py:244
  15.0 0.3 multiply_cosine_fusion
  15.3 0.1 pad_maximum_fusion.1.table_ref
  15.5 1.3 %pad_maximum_fusion.w_ref = bf16[3072,256]{1,0:T(8,128)(2,1)S(1)} fusion(bf16[3072,128]{1,0:T(8,128)(2,1)S(1)} %copy-done.2, bf16[3072,128]{1,0:T(8,128)(2,1)} %param.13), kind=kLoop, calls=%fused_computation | loop fusion | flops 3145728 | bytes 3145728 | tf_op jit(solution)/shard_map/concatenate | solution.py:249
  16.8 5.1 %all-to-all-done = bf16[8,8,3200]{2,1,0:T(8,128)(2,1)S(1)} async-done(((bf16[8,8,3200]{2,1,0:T(8,128)(2,1)}), bf16[8,8,3200]{2,1,0:T(8,128)(2,1)S(1)}, u32[]{:S(2)}, u32[]{:S(2)}) %all-to-all-start) | async-done | bytes 409632 | tf_op jit(solution)/shard_map/all_to_all | solution.py:244
  21.9 3.5 %kv.1 = (bf16[128,3072]{1,0:T(8,128)(2,1)S(1)}, bf16[8,128,256]{2,1,0:T(8,128)(2,1)}, f32[16,3072]{1,0:T(8,128)S(1)}) custom-call(bf16[64,3200]{1,0:T(8,128)(2,1)S(1)} %bitcast.14, bf16[128,3072]{1,0:T(8,128)(2,1)} %bitcast.17, f32[1,3072]{1,0:T(1,128)S(1)} %bitcast.15, f32[128,256]{1,0:T(8,128)S(1)} %pad_maximum_fusion.1.table_ref, ...), custom_call_target="tpu_custom_call" | custom-call | tf_op jit(solution)/shard_map/kv/pallas_call | solution.py:252
  25.4 7.9 %all-to-all-start.1 = ((bf16[8,128,256]{2,1,0:T(8,128)(2,1)}), bf16[8,128,256]{2,1,0:T(8,128)(2,1)S(1)}, u32[]{:S(2)}, u32[]{:S(2)}) async-start(bf16[8,128,256]{2,1,0:T(8,128)(2,1)} %get-tuple-element.17), calls=%async_computation.1 | async-start | bytes 1048576 | tf_op jit(solution)/shard_map/all_to_all | solution.py:281
  33.3 0.0 all-gather.7.cloned.1.call-start
  33.3 1.7 %copy-done = bf16[3072,384]{1,0:T(8,128)(2,1)S(1)} copy-done((bf16[3072,384]{1,0:T(8,128)(2,1)S(1)}, bf16[3072,384]{1,0:T(8,128)(2,1)}, u32[]{:S(2)}) %copy-start) | copy-done | bytes 2359320
  35.0 1.6 %q.1 = bf16[4,128,384]{2,1,0:T(8,128)(2,1)} custom-call(bf16[128,3072]{1,0:T(8,128)(2,1)S(1)} %get-tuple-element.19.normed_ref, f32[128,256]{1,0:T(8,128)S(1)} %pad_maximum_fusion.1.table_ref, bf16[3072,384]{1,0:T(8,128)(2,1)S(1)} %copy-done), custom_call_target="tpu_custom_call" | custom-call | flops 301989888 | bytes 2359296 | tf_op jit(solution)/shard_map/q/pallas_call | solution.py:269
  36.6 12.4 %all-gather.5.cloned.1.call-done = bf16[1408,384]{1,0:T(8,128)(2,1)} async-done(((bf16[176,384]{1,0:T(8,128)(2,1)}), bf16[1408,384]{1,0:T(8,128)(2,1)}) %all-gather.5.cloned.1.call-update) | async-done | bytes 1081360 | tf_op jit(solution)/shard_map/all_gather | solution.py:240
  48.9 1.6 %dynamic-slice_bitcast_fusion = bf16[4,48,384]{2,1,0:T(8,128)(2,1)} fusion(bf16[4,2,176,384]{3,2,1,0:T(8,128)(2,1)} %bitcast.20, s32[]{:T(128)S(6)} %select_n.3), kind=kLoop, calls=%fused_computation.3 | loop fusion | bytes 294916 | tf_op jit(solution)/shard_map/reshape | solution.py:241
  50.6 7.4 %all-to-all-start.2 = ((bf16[4,128,384]{2,1,0:T(8,128)(2,1)}), bf16[4,128,384]{2,1,0:T(8,128)(2,1)S(1)}, u32[]{:S(2)}, u32[]{:S(2)}) async-start(bf16[4,128,384]{2,1,0:T(8,128)(2,1)} %q.1), calls=%async_computation.2 | async-start | bytes 786432 | tf_op jit(solution)/shard_map/all_to_all | solution.py:285
  58.0 5.1 %collective-permute-start = (bf16[8,128,256]{2,1,0:T(8,128)(2,1)S(1)}, bf16[8,128,256]{2,1,0:T(8,128)(2,1)S(1)}, u32[]{:S(2)}, u32[]{:S(2)}) collective-permute-start(bf16[8,128,256]{2,1,0:T(8,128)(2,1)S(1)} %all-to-all-done.1.near_ref), channel_id=1, source_target_pairs={{1,0},{0,1},{3,2},{2,3},{5,4},{4,5},{7,6},{6,7},{9,8},{8,9},{11,10... | collective-permute-start | bytes 1572872 | tf_op jit(solution)/shard_map/ppermute | solution.py:286
  63.1 1.5 %collective-permute-done.far_ref = bf16[8,128,256]{2,1,0:T(8,128)(2,1)S(1)} collective-permute-done((bf16[8,128,256]{2,1,0:T(8,128)(2,1)S(1)}, bf16[8,128,256]{2,1,0:T(8,128)(2,1)S(1)}, u32[]{:S(2)}, u32[]{:S(2)}) %collective-permute-start) | collective-permute-done | bytes 524320 | tf_op jit(solution)/shard_map/ppermute | solution.py:286
  64.6 2.4 %all-to-all-done.2.q_ref = bf16[4,128,384]{2,1,0:T(8,128)(2,1)S(1)} async-done(((bf16[4,128,384]{2,1,0:T(8,128)(2,1)}), bf16[4,128,384]{2,1,0:T(8,128)(2,1)S(1)}, u32[]{:S(2)}, u32[]{:S(2)}) %all-to-all-start.2) | async-done | bytes 393248 | tf_op jit(solution)/shard_map/all_to_all | solution.py:285
  67.0 5.5 %attend.1 = (bf16[4,400,128]{2,1,0:T(8,128)(2,1)S(1)}, f32[384,128]{1,0:T(8,128)S(1)}) custom-call(bf16[4,128,384]{2,1,0:T(8,128)(2,1)S(1)} %all-to-all-done.2.q_ref, bf16[8,128,256]{2,1,0:T(8,128)(2,1)S(1)} %all-to-all-done.1.near_ref, bf16[8,128,256]{2,1,0:T(8,128)(2,1)S(1)} %collective-permute-done.far_ref), custom_call_target="tpu_custom_call" | custom-call | tf_op jit(solution)/shard_map/attend/pallas_call | solution.py:288
  72.4 14.4 %all_to_all.25.o_ref = bf16[4,400,128]{2,1,0:T(8,128)(2,1)S(1)} all-to-all(bf16[4,400,128]{2,1,0:T(8,128)(2,1)S(1)} %get-tuple-element.22), channel_id=1, replica_groups=mesh['uly'=8,'blk_y'=8,'blk_z'=4,'blk_c'=2] {'blk_z'}, dimensions={0} | all-to-all | bytes 819200 | tf_op jit(solution)/shard_map/all_to_all | solution.py:301
  86.9 4.9 %all-gather.7.cloned.1.call-done = bf16[64,48,384]{2,1,0:T(8,128)(2,1)} async-done(((bf16[4,48,384]{2,1,0:T(8,128)(2,1)}), bf16[64,48,384]{2,1,0:T(8,128)(2,1)}) %all-gather.7.cloned.1.call-update) | async-done | bytes 2359312 | tf_op jit(solution)/shard_map/all_gather | solution.py:283
  91.7 2.7 %project.1 = bf16[128,3072]{1,0:T(8,128)(2,1)S(1)} custom-call(bf16[4,400,128]{2,1,0:T(8,128)(2,1)S(1)} %all_to_all.25.o_ref, f32[384,128]{1,0:T(8,128)S(1)} %get-tuple-element.23.mine_ref, bf16[8,2,4,48,384]{4,3,2,1,0:T(8,128)(2,1)} %bitcast.16), custom_call_target="tpu_custom_call" | custom-call | tf_op jit(solution)/shard_map/project/pallas_call | solution.py:302
  94.4 16.8 %all_to_all.26 = bf16[8,16,3072]{2,1,0:T(8,128)(2,1)S(1)} all-to-all(bf16[8,16,3072]{2,1,0:T(8,128)(2,1)S(1)} %bitcast.13), channel_id=1, replica_groups=mesh['uly'=8,'blk_y'=8,'blk_z'=4,'blk_c'=2] {'uly'}, dimensions={0} | all-to-all | bytes 1572864 | tf_op jit(solution)/shard_map/all_to_all | solution.py:316
  111.2 0.1 convert_reduce_fusion
  111.4 0.7 fusion
  (11 shorter events, 0.1 us)
Async XLA Ops:
  6.5 8.9 %copy-start.2 = (bf16[3072,128]{1,0:T(8,128)(2,1)S(1)}, bf16[3072,128]{1,0:T(8,128)(2,1)}, u32[]{:S(2)}) copy-start(bf16[3072,128]{1,0:T(8,128)(2,1)} %param.14) | copy-start | bytes 2359300
  6.5 42.4 %all-gather.5.cloned.1.call-start = ((), (), s32[]{:S(2)}) async-start(), calls=%async_computation.5 | async-start | bytes 1216512 | tf_op jit(solution)/shard_map/all_gather | solution.py:240
  8.3 13.6 %all-to-all-start = ((bf16[8,8,3200]{2,1,0:T(8,128)(2,1)}), bf16[8,8,3200]{2,1,0:T(8,128)(2,1)S(1)}, u32[]{:S(2)}, u32[]{:S(2)}) async-start(bf16[8,8,3200]{2,1,0:T(8,128)(2,1)} %get-tuple-element.15), calls=%async_computation | async-start | bytes 819200 | tf_op jit(solution)/shard_map/all_to_all | solution.py:244
  15.5 6.5 %copy-start.1 = (f32[3072]{0:T(1024)S(1)}, f32[3072]{0:T(1024)}, u32[]{:S(2)}) copy-start(f32[3072]{0:T(1024)} %param.11) | copy-start | bytes 36868
  25.4 25.1 %all-to-all-start.1 = ((bf16[8,128,256]{2,1,0:T(8,128)(2,1)}), bf16[8,128,256]{2,1,0:T(8,128)(2,1)S(1)}, u32[]{:S(2)}, u32[]{:S(2)}) async-start(bf16[8,128,256]{2,1,0:T(8,128)(2,1)} %get-tuple-element.17), calls=%async_computation.1 | async-start | bytes 1048576 | tf_op jit(solution)/shard_map/all_to_all | solution.py:281
  33.3 58.5 %all-gather.7.cloned.1.call-start = ((), (), s32[]{:S(2)}) async-start(), calls=%async_computation.6 | async-start | bytes 2506752 | tf_op jit(solution)/shard_map/all_gather | solution.py:283
  33.3 1.7 %copy-start = (bf16[3072,384]{1,0:T(8,128)(2,1)S(1)}, bf16[3072,384]{1,0:T(8,128)(2,1)}, u32[]{:S(2)}) copy-start(bf16[3072,384]{1,0:T(8,128)(2,1)} %w_ref.1) | copy-start | bytes 7077892
  50.6 16.4 %all-to-all-start.2 = ((bf16[4,128,384]{2,1,0:T(8,128)(2,1)}), bf16[4,128,384]{2,1,0:T(8,128)(2,1)S(1)}, u32[]{:S(2)}, u32[]{:S(2)}) async-start(bf16[4,128,384]{2,1,0:T(8,128)(2,1)} %q.1), calls=%async_computation.2 | async-start | bytes 786432 | tf_op jit(solution)/shard_map/all_to_all | solution.py:285
  58.0 6.6 %collective-permute-start = (bf16[8,128,256]{2,1,0:T(8,128)(2,1)S(1)}, bf16[8,128,256]{2,1,0:T(8,128)(2,1)S(1)}, u32[]{:S(2)}, u32[]{:S(2)}) collective-permute-start(bf16[8,128,256]{2,1,0:T(8,128)(2,1)S(1)} %all-to-all-done.1.near_ref), channel_id=1, source_target_pairs={{1,0},{0,1},{3,2},{2,3},{5,4},{4,5},{7,6},{6,7},{9,8},{8,9},{11,10... | collective-permute-start | bytes 1572872 | tf_op jit(solution)/shard_map/ppermute | solution.py:286
Sparse Core Ops, SparseCore 0:
  9.5 39.4 all-gather.4
  51.1 40.6 all-gather.6
